TPU v7x, 32 devices: a whole 2x2x4 slice. The times are simulated.
32 devices in a mesh: lat: 4 (over y, x), lon: 8 (over z, core).
Axes of the slice: x: 2, y: 2, z: 4, core: 2. Of those that a mesh axis runs over, the one named last changes fastest.
Arguments:
- analysis_vector: float32 [69, 64, 1024], P(None, 'lat', 'lon'), may hold values from -6 to 6
- prior_estimate: float32 [69, 64, 1024], P(None, 'lat', 'lon'), may hold values from -6 to 6
- prior_precision: float32 [69], replicated, may hold values from 0.5 to 2
- encoder_weight: bfloat16 [69, 256], replicated, may hold values from -0.75 to 0.75
- conv_weights: bfloat16 [2, 3, 3, 256, 256], replicated, may hold values from -0.125 to 0.125
- readout_matrix: bfloat16 [256, 69], replicated, may hold values from -0.375 to 0.375
- obs_in_weight: bfloat16 [4, 69, 1024], replicated, may hold values from -0.375 to 0.375
- obs_out_weight: bfloat16 [1024, 128], replicated, may hold values from -0.1875 to 0.1875
- obs_values: float32 [65536, 128], P(('lat', 'lon')), may hold values from -6 to 6
- obs_precision: float32 [128], replicated, may hold values from 0.5 to 2
- foot_cells: int32 [65536, 4], P(('lat', 'lon')), may hold values from 0 to 65535, as said below
- obs_count: int32 [32], P(('lat', 'lon')), may hold values from 512 to 2048, as said below
Outputs:
- departures: float32 [65536, 128], P(('lat', 'lon'))
- cost_derivative: float32 [69, 64, 1024], P(None, 'lat', 'lon')
Inputs may be any that keep to these rules, and one draw needn't show every extreme that they name: `foot_cells`: each observation's 4 columns form a 2x2 block of neighbouring cells inside one device's tile. Each device has its own order of all 32 tiles, drawn from the seed, and its observation slot o (counted within the device) lies on the tile at place o mod 32 of that order, so that every device puts exactly 256 footprint columns of its slots on every tile. `obs_count`: the devices of at least one latitude row of the mesh (a swath), sometimes more rows, have 2048 valid observations; every other device has between 512 and 682.
All inputs are finite; a program needn't handle non-finite values.
Results may differ from a plain program's by a relative error of at most 0.008.
Values may be sent and summed in bfloat16 or wider, within the bound.
No kernel may reach another device: no remote copies, remote signals or barrier semaphores. Data moves between devices by JAX's collectives and lax.ppermute only.
A program may use at most 128 MiB of HBM per device.

v0:
```python
import functools
import itertools

import jax
import jax.numpy as jnp
from jax import lax
from jax.experimental import pallas as pl
from jax.experimental.pallas import tpu as pltpu
from jax.sharding import PartitionSpec as P

F32 = jnp.float32
BF16 = jnp.bfloat16
LANES = 128
EDGE = 8
HALO = 4
BACK = 2
META = 8
VMEM = pltpu.VMEM
SMEM = pltpu.SMEM


def call(body, outs, n_in, scratch=(), smem=(), flops=0, moved=0, name=None):
    specs = [pl.BlockSpec(memory_space=SMEM if i in smem else VMEM) for i in range(n_in)]
    return pl.pallas_call(
        body,
        out_shape=tuple(jax.ShapeDtypeStruct(s, d) for s, d in outs),
        in_specs=specs,
        out_specs=tuple(pl.BlockSpec(memory_space=VMEM) for _ in outs),
        scratch_shapes=list(scratch),
        cost_estimate=pl.CostEstimate(flops=flops, bytes_accessed=moved, transcendentals=0),
        name=name,
    )


def sigma(v):
    return 0.5 * jnp.tanh(0.5 * v) + 0.5


def dot(a, b):
    return jnp.dot(a, b, preferred_element_type=F32)


def state_body(a_ref, at_ref, s_ref, first_ref, last_ref):
    v, rows, cols = a_ref.shape
    pad = jnp.zeros((LANES - v, cols), F32)
    for r in range(rows):
        x = jnp.concatenate([a_ref[:, r, :], pad], axis=0).T
        at_ref[r] = x
        half = x.astype(BF16)
        s_ref[r] = half
        first_ref[r] = half[:EDGE]
        last_ref[r] = half[cols - EDGE :]


def pack_body(order_ref, obs_ref, meta_ref, out_ref):
    tiles = out_ref.shape[0]
    per = out_ref.shape[1] - META

    def one(p, c):
        h = order_ref[p]
        out_ref[h, 0:per, :] = obs_ref[pl.ds(p, per, stride=tiles), :].astype(BF16)
        return c

    lax.fori_loop(0, tiles, one, 0)
    for h in range(tiles):
        out_ref[h, per : per + META, :] = meta_ref[h]


def unpack_body(order_ref, count_ref, got_ref, obs_ref, prec_ref, out_ref):
    tiles, per, _ = got_ref.shape
    prec = prec_ref[...]
    slot = lax.broadcasted_iota(jnp.int32, (per, LANES), 0) * tiles

    def one(p, c):
        h = order_ref[p]
        obs = obs_ref[pl.ds(p, per, stride=tiles), :]
        dep = (got_ref[h].astype(F32) - obs) * prec
        out_ref[pl.ds(p, per, stride=tiles), :] = jnp.where(slot + p < count_ref[0], dep, 0.0)
        return c

    lax.fori_loop(0, tiles, one, 0)


def shift_pairs(size, wrap):
    up = [(i, (i + 1) % size) for i in range(size if wrap else size - 1)]
    return up, [(j, i) for i, j in up]


def halo(mid, first, last, width):
    up, down = shift_pairs(lax.axis_size("lat"), False)
    rows = mid.shape[0]
    top = lax.ppermute(mid[rows - width :], "lat", up)
    bottom = lax.ppermute(mid[:width], "lat", down)
    up, down = shift_pairs(lax.axis_size("lon"), True)
    cols = mid.shape[1]
    near = jnp.concatenate([top[:, :EDGE], first, bottom[:, :EDGE]], axis=0)
    far = jnp.concatenate([top[:, cols - EDGE :], last, bottom[:, cols - EDGE :]], axis=0)
    left = lax.ppermute(far, "lon", up)
    right = lax.ppermute(near, "lon", down)
    side = jnp.concatenate([right, left], axis=1)
    return top, bottom, side


def row_parts(mid_ref, top_ref, bottom_ref, width):
    rows = mid_ref.shape[0]
    return (
        (width, 0, top_ref),
        (rows, width, mid_ref),
        (width, width + rows, bottom_ref),
    )


def put_shifted(ref, e, value):
    w, ch = value.shape
    ref[e, :, 0:ch] = pltpu.roll(value, 1, 0).astype(BF16)
    ref[e, :, ch : 2 * ch] = value.astype(BF16)
    ref[e, :, 2 * ch : 3 * ch] = pltpu.roll(value, w - 1, 0).astype(BF16)


def conv_rows(ref, e, count, width, weight):
    parts = [
        ref[pl.ds(e + i, count), 0:width, :].reshape(count * width, ref.shape[2]) for i in range(3)
    ]
    return dot(jnp.concatenate(parts, axis=1), weight)


def inside(row0_ref, a):
    g = row0_ref[0] + a
    return jnp.logical_and(g >= 0, g < row0_ref[1])


STEP = 2


def forward_body(
    row0_ref, mid_ref, top_ref, bottom_ref, side_ref, at_ref, enc_ref, w_ref, ro_ref,
    cols_ref, slope0_ref, slope1_ref, a0, a1,
):
    rows, cols, _ = mid_ref.shape
    width, ch = a0.shape[1], enc_ref.shape[1]
    for count, base, src in row_parts(mid_ref, top_ref, bottom_ref, HALO):

        def embed(i, c, base=base, src=src):
            x = jnp.concatenate([src[i], side_ref[base + i]], axis=0)
            h = dot(x, enc_ref[...]).astype(BF16).astype(F32)
            put_shifted(a0, base + i, h)
            return c

        lax.fori_loop(0, count, embed, 0)

    def first(k, c):
        e = k * STEP
        pre = conv_rows(a0, e, STEP, width, w_ref[0]).reshape(STEP, width, ch)
        s = sigma(pre)
        act = pre * s
        slope0_ref[pl.ds(e, STEP)] = (s + act * (1.0 - s)).astype(BF16)
        for q in range(STEP):
            h = a0[e + q + 1, :, ch : 2 * ch].astype(F32) + act[q]
            h = jnp.where(inside(row0_ref, e + q - HALO + 1), h, 0.0)
            put_shifted(a1, e + q, h.astype(BF16).astype(F32))
        return c

    lax.fori_loop(0, (rows + 2 * HALO - 2) // STEP, first, 0)

    def second(k, c):
        e = k * STEP
        pre = conv_rows(a1, e, STEP, width, w_ref[1]).reshape(STEP, width, ch)
        s = sigma(pre)
        act = pre * s
        slope1_ref[pl.ds(e, STEP)] = (s + act * (1.0 - s)).astype(BF16)
        a = e - (HALO - 2)

        @pl.when(jnp.logical_and(a >= 0, a < rows))
        def _():
            for q in range(STEP):
                h = a1[e + q + 1, 0:cols, ch : 2 * ch].astype(F32) + act[q, 0:cols]
                grow = dot(h.astype(BF16), ro_ref[...])
                cols_ref[a + q] = (at_ref[a + q] + grow).astype(BF16)

        return c

    lax.fori_loop(0, (rows + 2 * HALO - 4) // STEP, second, 0)


BLOCK = 512


def observe_body(
    table_ref, cols_ref, got_ref, win_ref, wout_ref, woutt_ref, wint_ref, prec_ref,
    adj_ref, half_ref, pred_ref,
    xs, slope, grid, hot, weights, fa, meta,
):
    rows, cols, _ = cols_ref.shape
    cells = rows * cols
    half = cells // 2
    tiles, per, nch = pred_ref.shape
    obs_n = tiles * per
    group = LANES // per
    prec2 = prec_ref[...] * prec_ref[...]
    c0 = cols_ref[...].reshape(cells, LANES)
    c1 = pltpu.roll(c0.astype(F32), cells - 1, 0).astype(BF16)
    xs[0] = c0
    xs[1] = c1
    xs[2] = jnp.concatenate([c0[cols:], c0[:cols]], axis=0)
    xs[3] = jnp.concatenate([c1[cols:], c1[:cols]], axis=0)
    rest = jnp.zeros((1, LANES), F32)
    for m in range(obs_n // LANES):
        total = got_ref[m * group, per : per + META, :].astype(F32)
        for g in range(1, group):
            total += got_ref[m * group + g, per : per + META, :].astype(F32)
        meta[m] = total
        rest += jnp.where(total[2:3] == table_ref[0, 4].astype(F32), 0.0, 1.0)
    trips = jnp.where(jnp.sum(rest) > 0.0, table_ref.shape[0], 1)
    fa[...] = jnp.zeros_like(fa)

    def arrangement(cls, carry):
        place = [table_ref[cls, f] for f in range(4)]
        code = table_ref[cls, 4].astype(F32)

        def forward(k, c):
            at = pl.ds(k * BLOCK, BLOCK)
            x = jnp.concatenate([xs[place[f], at, :] for f in range(4)], axis=1)
            inner = dot(x, win_ref[...])
            s = sigma(inner)
            act = inner * s
            slope[at, :] = (s + act * (1.0 - s)).astype(BF16)
            grid[at, :] = dot(act.astype(BF16), wout_ref[...]).astype(BF16)
            return c

        lax.fori_loop(0, cells // BLOCK, forward, 0)
        both = jnp.concatenate([grid[0:half, :], grid[half:, :]], axis=1)
        lane = lax.broadcasted_iota(jnp.int32, (LANES, LANES), 1).astype(F32)
        sub = lax.broadcasted_iota(jnp.int32, (LANES, LANES), 0).astype(F32)
        top = float(rows // 2)

        def gather(m, c):
            mine = meta[m, 2:3, :] == code
            row = jnp.broadcast_to(jnp.where(mine, meta[m, 0:1, :], float(rows)), (LANES, LANES))
            col = jnp.broadcast_to(meta[m, 1:2, :], (LANES, LANES))
            row_t, col_t = row.T, col.T
            local = jnp.where(row_t < top, row_t, row_t - top)
            value = jnp.where(col_t == lane, local, -1.0)
            sel = jnp.concatenate(
                [jnp.where(value == float(t), 1.0, 0.0).astype(BF16) for t in range(rows // 2)],
                axis=1,
            )
            out = dot(sel, both)
            upper = row_t >= top
            pred = jnp.where(upper, out[:, nch:], out[:, :nch])
            pred = jnp.where(row_t < float(rows), pred, 0.0)
            obs = got_ref[pl.ds(m * group, group), 0:per, :].astype(F32).reshape(LANES, nch)
            w = (pred - obs) * prec2
            at = pl.ds(m * LANES, LANES)
            weights[at, 0:nch] = jnp.where(upper, 0.0, w).astype(BF16)
            weights[at, nch:] = jnp.where(upper, w, 0.0).astype(BF16)
            pred = pred.reshape(group, per, nch)
            where = pl.ds(m * group, group)

            @pl.when(cls == 0)
            def _():
                pred_ref[where] = pred.astype(BF16)

            @pl.when(cls > 0)
            def _():
                pred_ref[where] = (pred_ref[where].astype(F32) + pred).astype(BF16)

            local = jnp.where(row < top, row, row - top)
            value = jnp.where(col == sub, local, -1.0)
            for t in range(rows // 2):
                hot[t * LANES : (t + 1) * LANES, pl.ds(pl.multiple_of(m * LANES, LANES), LANES)] = (
                    jnp.where(value == float(t), 1.0, 0.0).astype(BF16)
                )
            return c

        lax.fori_loop(0, obs_n // LANES, gather, 0)

        def scatter(k, c):
            at = pl.ds(k * BLOCK, BLOCK)
            total = dot(hot[at, :], weights[...])
            grid[at, :] = total[:, :nch].astype(BF16)
            grid[pl.ds(half + k * BLOCK, BLOCK), :] = total[:, nch:].astype(BF16)
            return c

        lax.fori_loop(0, half // BLOCK, scatter, 0)

        def backward(k, c):
            at = pl.ds(k * BLOCK, BLOCK)
            act = dot(grid[at, :], woutt_ref[...])
            inner = (act * slope[at, :].astype(F32)).astype(BF16)
            x = dot(inner, wint_ref[...])
            for f in range(4):
                fa[place[f], at, :] += x[:, f * LANES : (f + 1) * LANES]
            return c

        lax.fori_loop(0, cells // BLOCK, backward, 0)
        return carry

    lax.fori_loop(0, trips, arrangement, 0)
    high = fa[3]
    one = fa[1] + jnp.concatenate([high[cells - cols :], high[: cells - cols]], axis=0)
    low = fa[2]
    total = fa[0] + jnp.concatenate([low[cells - cols :], low[: cells - cols]], axis=0)
    total += pltpu.roll(one, 1, 0)
    total = total.reshape(rows, cols, LANES)
    adj_ref[...] = total
    half_ref[...] = total.astype(BF16)


def adjoint_body(
    row0_ref, mid_ref, top_ref, bottom_ref, side_ref, adj_ref, slope0_ref, slope1_ref,
    rot_ref, w_ref, enct_ref, state_ref, prior_ref, prec_ref,
    out_ref, b1, b0, adj2, adj1,
):
    rows, cols, _ = mid_ref.shape
    width, ch = b1.shape[1], rot_ref.shape[1]
    v = out_ref.shape[0]
    for count, base, src in row_parts(mid_ref, top_ref, bottom_ref, BACK):

        def lift(i, c, base=base, src=src):
            x = jnp.concatenate([src[i], side_ref[base + i]], axis=0)
            g = dot(x, rot_ref[...])
            adj2[base + i] = g
            g = (g * slope1_ref[base + i].astype(F32)).astype(BF16)
            put_shifted(b1, base + i, g.astype(F32))
            return c

        lax.fori_loop(0, count, lift, 0)

    def first(k, c):
        e = k * STEP
        g = conv_rows(b1, e, STEP, width, w_ref[1]).reshape(STEP, width, ch)
        for q in range(STEP):
            total = adj2[e + q + 1] + g[q]
            adj1[e + q] = total
            h = total * slope0_ref[e + q + 2].astype(F32)
            h = jnp.where(inside(row0_ref, e + q - 1), h, 0.0)
            put_shifted(b0, e + q, h.astype(BF16).astype(F32))
        return c

    lax.fori_loop(0, (rows + 2) // STEP, first, 0)

    def second(k, c):
        a = k * STEP
        g = conv_rows(b0, a, STEP, cols, w_ref[0]).reshape(STEP, cols, ch)
        for q in range(STEP):
            total = adj1[a + q + 1, 0:cols, :] + g[q]
            grow = dot(total.astype(BF16), enct_ref[...]) + adj_ref[a + q]
            diff = state_ref[:, a + q, :] - prior_ref[:, a + q, :]
            out_ref[:, a + q, :] = prec_ref[...] * diff + grow.T[0:v, :]
        return c

    lax.fori_loop(0, rows // STEP, second, 0)


def arrangement_table():
    orders = list(itertools.permutations(range(4)))
    first = (0, 2, 1, 3)
    orders.remove(first)
    return [
        list(o) + [sum(q * 4**f for f, q in enumerate(o))] for o in [first] + orders
    ]


def on_device(
    analysis_vector,
    prior_estimate,
    prior_precision,
    encoder_weight,
    conv_weights,
    readout_matrix,
    obs_in_weight,
    obs_out_weight,
    obs_values,
    obs_precision,
    foot_cells,
    obs_count,
):
    v, rows, cols = analysis_vector.shape
    n_lat, n_lon = lax.axis_size("lat"), lax.axis_size("lon")
    tiles = n_lat * n_lon
    obs_n, foot = foot_cells.shape
    per = obs_n // tiles
    ch = encoder_weight.shape[1]
    hid, nch = obs_out_weight.shape
    width = cols + 2 * EDGE
    cells = rows * cols
    lat, lon = lax.axis_index("lat"), lax.axis_index("lon")
    row0 = jnp.stack([lat * rows, jnp.int32(n_lat * rows)])

    at, s16, first, last = call(
        state_body,
        [((rows, cols, LANES), F32), ((rows, cols, LANES), BF16)] + [((rows, EDGE, LANES), BF16)] * 2,
        1, moved=cells * v * 8, name="state",
    )(analysis_vector)
    top, bottom, side = halo(s16, first, last, HALO)

    lon_total = cols * n_lon
    lat_g, lon_g = foot_cells // lon_total, foot_cells % lon_total
    order = lat_g[:tiles, 0] // rows * n_lon + lon_g[:tiles, 0] // cols
    base_lat, base_lon = jnp.min(lat_g, axis=1), jnp.min(lon_g, axis=1)
    place = (lat_g - base_lat[:, None]) * 2 + (lon_g - base_lon[:, None])
    code = jnp.sum(place * (4 ** jnp.arange(foot)), axis=1)
    valid = jnp.arange(obs_n) < obs_count[0]
    local = jnp.where(valid, base_lat % rows, rows)
    fields = jnp.stack([local, base_lon % cols, code]).astype(BF16).reshape(3, per, tiles)
    pick = (order[None, :] == jnp.arange(tiles)[:, None]).astype(BF16)
    meta = jnp.einsum("fkp,hp->hfk", fields, pick, preferred_element_type=F32).astype(BF16)
    group = LANES // per
    mine = jnp.arange(group) == (lat * n_lon + lon) % group
    meta = jnp.where(mine[:, None], meta[:, :, None, :], jnp.zeros((), BF16)).reshape(tiles, 3, LANES)
    meta = jnp.pad(meta, ((0, 0), (0, META - 3), (0, 0)))
    (send,) = call(
        pack_body, [((tiles, per + META, nch), BF16)], 3, smem=(0,), moved=obs_n * nch * 6, name="pack"
    )(order, obs_values, meta)
    got = lax.all_to_all(send, ("lat", "lon"), split_axis=0, concat_axis=0, tiled=True)

    pad_v = ((0, LANES - v), (0, 0))
    enc = jnp.pad(encoder_weight, pad_v)
    rot = jnp.pad(readout_matrix.T, pad_v)
    win = jnp.pad(obs_in_weight, ((0, 0),) + pad_v).reshape(foot * LANES, hid)
    w_fwd = conv_weights.reshape(conv_weights.shape[0], 9 * ch, ch)
    w_back = jnp.transpose(conv_weights[:, ::-1, ::-1], (0, 1, 2, 4, 3)).reshape(w_fwd.shape)

    conv_flops = 2 * cells * 9 * ch * ch
    cols16, slope0, slope1 = call(
        forward_body,
        [
            ((rows, cols, LANES), BF16),
            ((rows + 2 * HALO - 2, width, ch), BF16),
            ((rows + 2 * HALO - 4, width, ch), BF16),
        ],
        9,
        [VMEM((rows + 2 * HALO, width, 3 * ch), BF16), VMEM((rows + 2 * HALO - 2, width, 3 * ch), BF16)],
        (0,), 3 * conv_flops, cells * ch * 8, "forward",
    )(row0, s16, top, bottom, side, at, enc, w_fwd, rot.T)

    adj, adj16, pred = call(
        observe_body,
        [((rows, cols, LANES), F32), ((rows, cols, LANES), BF16), ((tiles, per, nch), BF16)],
        8,
        [
            VMEM((4, cells, LANES), BF16),
            VMEM((cells, hid), BF16),
            VMEM((cells, nch), BF16),
            VMEM((cells // 2, obs_n), BF16),
            VMEM((obs_n, 2 * nch), BF16),
            VMEM((4, cells, LANES), F32),
            VMEM((obs_n // LANES, META, LANES), F32),
        ],
        (0,), 4 * cells * hid * (foot * LANES + nch), cells * hid * 4, "observe",
    )(
        jnp.array(arrangement_table(), jnp.int32), cols16, got, win, obs_out_weight,
        obs_out_weight.T, win.T, obs_precision[None, :],
    )
    back = lax.all_to_all(pred, ("lat", "lon"), split_axis=0, concat_axis=0, tiled=True)

    top, bottom, side = halo(adj16, adj16[:, :EDGE], adj16[:, cols - EDGE :], BACK)
    (derivative,) = call(
        adjoint_body,
        [((v, rows, cols), F32)],
        14,
        [
            VMEM((rows + 2 * BACK, width, 3 * ch), BF16),
            VMEM((rows + 2, width, 3 * ch), BF16),
            VMEM((rows + 2 * BACK, width, ch), F32),
            VMEM((rows + 2, width, ch), F32),
        ],
        (0,), 3 * conv_flops, cells * ch * 8, "adjoint",
    )(
        row0, adj16, top, bottom, side, adj, slope0, slope1, rot, w_back, enc.T,
        analysis_vector, prior_estimate, jnp.broadcast_to(prior_precision[:, None], (v, cols)),
    )
    (departures,) = call(
        unpack_body, [((obs_n, nch), F32)], 5, smem=(0, 1), moved=obs_n * nch * 10, name="unpack"
    )(order, obs_count, back, obs_values, obs_precision[None, :])
    return departures, derivative


def solution(mesh):
    return jax.shard_map(
        on_device,
        mesh=mesh,
        in_specs=(
            P(None, "lat", "lon"),
            P(None, "lat", "lon"),
            P(),
            P(),
            P(),
            P(),
            P(),
            P(),
            P(("lat", "lon"), None),
            P(),
            P(("lat", "lon"), None),
            P(("lat", "lon")),
        ),
        out_specs=(P(("lat", "lon"), None), P(None, "lat", "lon")),
        check_vma=False,
    )
```

profile of v0, /device:TPU:0, one launch (start us, length us, event | category | flops | bytes accessed | tf_op | source)
XLA Modules:
  0.0 137.1 jit_solution(9972946843173100493)
XLA Ops:
  0.7 0.1 broadcast_in_dim.49
  0.8 0.1 broadcast_in_dim.50
  0.8 0.9 fusion.19
  1.7 0.1 reduce_min.23
  1.8 0.1 reduce_min.25
  1.9 0.1 multiply_reduce_fusion
  2.0 0.1 stack.16
  2.1 0.1 copy.32
  2.2 0.1 copy.26
  2.2 0.1 copy.29
  3.0 0.1 convolution_convert_fusion
  3.2 0.1 broadcast_in_dim.53
  3.3 0.6 pad.17.meta_ref
  4.0 3.3 %pack.1 = bf16[32,72,128]{2,1,0:T(8,128)(2,1)} custom-call(s32[32]{0:T(128)} %copy-done.8, f32[2048,128]{1,0:T(8,128)} %obs_ref.3, bf16[32,8,128]{2,1,0:T(8,128)(2,1)} %pad.17.meta_ref), custom_call_target="tpu_custom_call" | custom-call | bytes 1572864 | tf_op jit(solution)/shard_map/pack/pallas_call | solution.py:412
  7.3 7.4 %all-to-all-start = ((bf16[32,72,128]{2,1,0:T(8,128)(2,1)}), bf16[32,72,128]{2,1,0:T(8,128)(2,1)}, u32[]{:S(2)}, u32[]{:S(2)}) async-start(bf16[32,72,128]{2,1,0:T(8,128)(2,1)} %pack.1), calls=%async_computation | async-start | bytes 1179648 | tf_op jit(solution)/shard_map/all_to_all | solution.py:415
  14.7 2.6 %state.1 = (f32[16,128,128]{2,1,0:T(8,128)}, bf16[16,128,128]{2,1,0:T(8,128)(2,1)}, bf16[16,8,128]{2,1,0:T(8,128)(2,1)}, bf16[16,8,128]{2,1,0:T(8,128)(2,1)}) custom-call(f32[69,16,128]{2,1,0:T(8,128)} %state_ref.1), custom_call_target="tpu_custom_call" | custom-call | bytes 1130496 | tf_op jit(solution)/shard_map/state/pallas_call | solution.py:390
  17.3 1.0 fusion.23
  18.3 3.6 %collective-permute-start = (bf16[4,128,128]{2,1,0:T(8,128)(2,1)S(1)}, bf16[4,128,128]{2,1,0:T(8,128)(2,1)S(1)}, u32[]{:S(2)}, u32[]{:S(2)}) collective-permute-start(bf16[4,128,128]{2,1,0:T(8,128)(2,1)S(1)} %get-tuple-element.33), channel_id=1, source_target_pairs={{0,8},{8,16},{16,24},{1,9},{9,17},{17,25},{2,10},{10,18},{18,26},{... | collective-permute-start | bytes 393224 | tf_op jit(solution)/shard_map/ppermute | solution.py:92
  21.9 0.0 copy-start.3
  21.9 0.0 copy-start.2
  22.0 1.4 %collective-permute-start.1 = (bf16[4,128,128]{2,1,0:T(8,128)(2,1)S(1)}, bf16[4,128,128]{2,1,0:T(8,128)(2,1)S(1)}, u32[]{:S(2)}, u32[]{:S(2)}) collective-permute-start(bf16[4,128,128]{2,1,0:T(8,128)(2,1)S(1)} %get-tuple-element.32), channel_id=1, source_target_pairs={{8,0},{16,8},{24,16},{9,1},{17,9},{25,17},{10,2},{18,10},{26,18},{... | collective-permute-start | bytes 393224 | tf_op jit(solution)/shard_map/ppermute | solution.py:93
  23.4 1.8 %reverse_bitcast_fusion = bf16[2,3,3,256,256]{3,4,2,1,0:T(8,128)(2,1)S(1)} fusion(bf16[2,3,3,256,256]{4,3,2,1,0:T(8,128)(2,1)} %param.17), kind=kLoop, calls=%fused_computation | loop fusion | bytes 4718592 | tf_op jit(solution)/shard_map/transpose | solution.py:422
  25.2 0.6 fusion.28
  25.9 0.0 collective-permute-done.top_ref
  25.9 6.1 %collective-permute-done.1.bottom_ref = bf16[4,128,128]{2,1,0:T(8,128)(2,1)S(1)} collective-permute-done((bf16[4,128,128]{2,1,0:T(8,128)(2,1)S(1)}, bf16[4,128,128]{2,1,0:T(8,128)(2,1)S(1)}, u32[]{:S(2)}, u32[]{:S(2)}) %collective-permute-start.1) | collective-permute-done | bytes 131104 | tf_op jit(solution)/shard_map/ppermute | solution.py:93
  32.0 1.7 %collective-permute-start.2 = (bf16[24,8,128]{2,1,0:T(8,128)(2,1)S(1)}, bf16[24,8,128]{2,1,0:T(8,128)(2,1)}, u32[]{:S(2)}, u32[]{:S(2)}) collective-permute-start(bf16[24,8,128]{2,1,0:T(8,128)(2,1)S(1)} %pad_maximum_fusion.2), channel_id=1, source_target_pairs={{1,0},{2,1},{3,2},{4,3},{5,4},{6,5},{7,6},{0,7},{9,8},{10,9},{11,1... | collective-permute-start | bytes 147464 | tf_op jit(solution)/shard_map/ppermute | solution.py:99
  33.7 0.0 copy-done.4
  33.7 0.6 pad_maximum_fusion.3
  34.3 0.0 collective-permute-start.3
  34.3 0.6 pad_add_fusion.row0_ref
  34.9 0.7 copy.25.ro_ref
  35.6 0.1 copy.23
  35.7 0.1 copy.44
  35.8 0.6 pad.15.clone.enc_ref
  36.5 2.7 %copy.38 = bf16[4,69,1024]{1,0,2:T(4,128)(2,1)S(1)} copy(bf16[4,69,1024]{2,0,1:T(4,128)(2,1)} %param.19) | data formatting | bytes 1130496
  39.2 0.5 pad.18.clone
  39.7 0.2 copy.45
  39.9 1.3 copy.36.win_ref
  41.2 1.8 %copy.35 = bf16[1024,128]{0,1:T(8,128)(2,1)} copy(bf16[1024,128]{1,0:T(8,128)(2,1)} %wout_ref.1) | data formatting | bytes 524288 | tf_op args[7]
  43.0 0.0 collective-permute-done.2
  43.0 0.0 collective-permute-done.3
  43.0 1.5 %pad_maximum_fusion.side_ref = bf16[24,16,128]{2,1,0:T(8,128)(2,1)} fusion(bf16[24,8,128]{2,1,0:T(8,128)(2,1)} %collective-permute-done.3, bf16[24,8,128]{2,1,0:T(8,128)(2,1)} %collective-permute-done.2), kind=kLoop, calls=%fused_computation.3 | loop fusion | flops 196608 | bytes 196608 | tf_op jit(solution)/shard_map/concatenate | solution.py:100
  44.5 21.9 %forward.1 = (bf16[16,128,128]{2,1,0:T(8,128)(2,1)}, bf16[22,144,256]{2,1,0:T(8,128)(2,1)}, bf16[20,144,256]{2,1,0:T(8,128)(2,1)}) custom-call(s32[2]{0:T(128)} %pad_add_fusion.row0_ref, bf16[16,128,128]{2,1,0:T(8,128)(2,1)} %get-tuple-element.12.mid_ref, bf16[4,128,128]{2,1,0:T(8,128)(2,1)} %copy-done.6, bf16[4,128,128]{2,1,0:T(8,128)(2,1)} %copy-done.7, ...), custom_call_target="tpu_custom_call" | custom-call | flops 7247757312 | bytes 4194304 | tf_op jit(solution)/shard_map/forward/pallas_call | solution.py:425
  66.4 0.0 all-to-all-done.got_ref
  66.4 21.0 %observe.1 = (f32[16,128,128]{2,1,0:T(8,128)}, bf16[16,128,128]{2,1,0:T(8,128)(2,1)}, bf16[32,64,128]{2,1,0:T(8,128)(2,1)}) custom-call(s32[24,5]{1,0:T(8,128)} %constant.125.clone.table_ref, bf16[16,128,128]{2,1,0:T(8,128)(2,1)} %get-tuple-element.16.cols_ref, bf16[32,72,128]{2,1,0:T(8,128)(2,1)} %all-to-all-done.got_ref, bf16[512,1024]{1,0:T(8,128)(2,1)} %copy.36.win_ref, ...), custom_call_target="tpu_custom_call" | custom-call | flops 5368709120 | bytes 8388608 | tf_op jit(solution)/shard_map/observe/pallas_call | solution.py:437
  87.4 0.9 fusion.22
  88.3 3.5 %collective-permute-start.4 = (bf16[2,128,128]{2,1,0:T(8,128)(2,1)S(1)}, bf16[2,128,128]{2,1,0:T(8,128)(2,1)S(1)}, u32[]{:S(2)}, u32[]{:S(2)}) collective-permute-start(bf16[2,128,128]{2,1,0:T(8,128)(2,1)S(1)} %get-tuple-element.31), channel_id=1, source_target_pairs={{0,8},{8,16},{16,24},{1,9},{9,17},{17,25},{2,10},{10,18},{18,26},{... | collective-permute-start | bytes 196616 | tf_op jit(solution)/shard_map/ppermute | solution.py:92
  91.8 0.8 fusion.21
  92.5 1.3 collective-permute-start.5
  93.8 5.4 %all-to-all-start.1 = ((bf16[32,64,128]{2,1,0:T(8,128)(2,1)}), bf16[32,64,128]{2,1,0:T(8,128)(2,1)S(1)}, u32[]{:S(2)}, u32[]{:S(2)}) async-start(bf16[32,64,128]{2,1,0:T(8,128)(2,1)} %get-tuple-element.17), calls=%async_computation.1 | async-start | bytes 1048576 | tf_op jit(solution)/shard_map/all_to_all | solution.py:455
  99.3 0.0 collective-permute-done.4.top_ref
  99.3 0.0 collective-permute-done.5.bottom_ref
  99.4 3.4 %collective-permute-start.6 = (bf16[20,8,128]{2,1,0:T(8,128)(2,1)S(1)}, bf16[20,8,128]{2,1,0:T(8,128)(2,1)S(1)}, u32[]{:S(2)}, u32[]{:S(2)}) collective-permute-start(bf16[20,8,128]{2,1,0:T(8,128)(2,1)S(1)} %pad_maximum_fusion.4), channel_id=1, source_target_pairs={{1,0},{2,1},{3,2},{4,3},{5,4},{6,5},{7,6},{0,7},{9,8},{10,9},{11,1... | collective-permute-start | bytes 122888 | tf_op jit(solution)/shard_map/ppermute | solution.py:99
  102.8 0.1 collective-permute-start.7
  102.8 0.6 pad_bitcast_fusion.1.enct_ref
  103.5 2.5 %copy.37 = bf16[2,3,3,256,256]{4,3,2,1,0:T(8,128)(2,1)} copy(bf16[2,3,3,256,256]{3,4,2,1,0:T(8,128)(2,1)S(1)} %reverse_bitcast_fusion) | data formatting | bytes 4718592 | tf_op jit(solution)/shard_map/transpose | solution.py:422
  105.9 3.4 %collective-permute-done.6 = bf16[20,8,128]{2,1,0:T(8,128)(2,1)S(1)} collective-permute-done((bf16[20,8,128]{2,1,0:T(8,128)(2,1)S(1)}, bf16[20,8,128]{2,1,0:T(8,128)(2,1)S(1)}, u32[]{:S(2)}, u32[]{:S(2)}) %collective-permute-start.6) | collective-permute-done | bytes 40992 | tf_op jit(solution)/shard_map/ppermute | solution.py:99
  109.3 3.4 %collective-permute-done.7 = bf16[20,8,128]{2,1,0:T(8,128)(2,1)S(1)} collective-permute-done((bf16[20,8,128]{2,1,0:T(8,128)(2,1)S(1)}, bf16[20,8,128]{2,1,0:T(8,128)(2,1)S(1)}, u32[]{:S(2)}, u32[]{:S(2)}) %collective-permute-start.7) | collective-permute-done | bytes 40992 | tf_op jit(solution)/shard_map/ppermute | solution.py:98
  112.7 0.6 pad_maximum_fusion.1.side_ref
  113.3 0.7 broadcast_in_dim.56.prec_ref
  114.0 18.4 %adjoint.1 = f32[69,16,128]{2,1,0:T(8,128)} custom-call(s32[2]{0:T(128)} %pad_add_fusion.row0_ref, bf16[16,128,128]{2,1,0:T(8,128)(2,1)} %get-tuple-element.18.mid_ref, bf16[2,128,128]{2,1,0:T(8,128)(2,1)} %copy-done.9, bf16[2,128,128]{2,1,0:T(8,128)(2,1)} %copy-done.10, bf16[20,16,128]{2,1,0:T(8,128)(2,1)} %pad_maximum_fusion.1.side_ref, ...), custom_call_target="tpu_custom_call" | custom-call | flops 7247757312 | bytes 4194304 | tf_op jit(solution)/shard_map/adjoint/pallas_call | solution.py:458
  132.4 0.0 all-to-all-done.1.got_ref
  132.5 0.8 copy-done.1
  133.3 3.9 %unpack.1 = f32[2048,128]{1,0:T(8,128)} custom-call(s32[32]{0:T(128)} %copy-done.8, s32[1]{0:T(128)} %copy.46.count_ref, bf16[32,64,128]{2,1,0:T(8,128)(2,1)} %copy-done.1, f32[2048,128]{1,0:T(8,128)} %obs_ref.3, f32[1,128]{1,0:T(1,128)} %bitcast.46), custom_call_target="tpu_custom_call" | custom-call | bytes 2621440 | tf_op jit(solution)/shard_map/unpack/pallas_call | solution.py:473
  (34 shorter events, 0.2 us)
Async XLA Ops:
  1.9 2.1 %copy-start.8 = (s32[32]{0:T(128)}, s32[32]{0:T(128)S(1)}, u32[]{:S(2)}) copy-start(s32[32]{0:T(128)S(1)} %fusion.16.order_ref) | copy-start | bytes 388
  7.3 59.2 %all-to-all-start = ((bf16[32,72,128]{2,1,0:T(8,128)(2,1)}), bf16[32,72,128]{2,1,0:T(8,128)(2,1)}, u32[]{:S(2)}, u32[]{:S(2)}) async-start(bf16[32,72,128]{2,1,0:T(8,128)(2,1)} %pack.1), calls=%async_computation | async-start | bytes 1179648 | tf_op jit(solution)/shard_map/all_to_all | solution.py:415
  18.3 7.6 %collective-permute-start = (bf16[4,128,128]{2,1,0:T(8,128)(2,1)S(1)}, bf16[4,128,128]{2,1,0:T(8,128)(2,1)S(1)}, u32[]{:S(2)}, u32[]{:S(2)}) collective-permute-start(bf16[4,128,128]{2,1,0:T(8,128)(2,1)S(1)} %get-tuple-element.33), channel_id=1, source_target_pairs={{0,8},{8,16},{16,24},{1,9},{9,17},{17,25},{2,10},{10,18},{18,26},{... | collective-permute-start | bytes 393224 | tf_op jit(solution)/shard_map/ppermute | solution.py:92
  21.9 3.3 %copy-start.3 = (bf16[256,69]{0,1:T(8,128)(2,1)S(1)}, bf16[256,69]{0,1:T(8,128)(2,1)}, u32[]{:S(2)}) copy-start(bf16[256,69]{0,1:T(8,128)(2,1)} %param.18) | copy-start | bytes 105988
  21.9 10.1 %copy-start.5 = (bf16[16,8,128]{2,1,0:T(8,128)(2,1)S(1)}, bf16[16,8,128]{2,1,0:T(8,128)(2,1)}, u32[]{:S(2)}) copy-start(bf16[16,8,128]{2,1,0:T(8,128)(2,1)} %get-tuple-element.13) | copy-start | bytes 98308
  21.9 11.7 %copy-start.4 = (bf16[16,8,128]{2,1,0:T(8,128)(2,1)S(1)}, bf16[16,8,128]{2,1,0:T(8,128)(2,1)}, u32[]{:S(2)}) copy-start(bf16[16,8,128]{2,1,0:T(8,128)(2,1)} %get-tuple-element.14) | copy-start | bytes 98308
  21.9 13.6 %copy-start.2 = (bf16[69,256]{1,0:T(8,128)(2,1)S(1)}, bf16[69,256]{1,0:T(8,128)(2,1)}, u32[]{:S(2)}) copy-start(bf16[69,256]{1,0:T(8,128)(2,1)} %param.16) | copy-start | bytes 105988
  22.0 10.0 %collective-permute-start.1 = (bf16[4,128,128]{2,1,0:T(8,128)(2,1)S(1)}, bf16[4,128,128]{2,1,0:T(8,128)(2,1)S(1)}, u32[]{:S(2)}, u32[]{:S(2)}) collective-permute-start(bf16[4,128,128]{2,1,0:T(8,128)(2,1)S(1)} %get-tuple-element.32), channel_id=1, source_target_pairs={{8,0},{16,8},{24,16},{9,1},{17,9},{25,17},{10,2},{18,10},{26,18},{... | collective-permute-start | bytes 393224 | tf_op jit(solution)/shard_map/ppermute | solution.py:93
  25.9 10.0 %copy-start.6 = (bf16[4,128,128]{2,1,0:T(8,128)(2,1)}, bf16[4,128,128]{2,1,0:T(8,128)(2,1)S(1)}, u32[]{:S(2)}) copy-start(bf16[4,128,128]{2,1,0:T(8,128)(2,1)S(1)} %collective-permute-done.top_ref) | copy-start | bytes 393220
  32.0 3.9 %copy-start.7 = (bf16[4,128,128]{2,1,0:T(8,128)(2,1)}, bf16[4,128,128]{2,1,0:T(8,128)(2,1)S(1)}, u32[]{:S(2)}) copy-start(bf16[4,128,128]{2,1,0:T(8,128)(2,1)S(1)} %collective-permute-done.1.bottom_ref) | copy-start | bytes 393220
  32.0 11.0 %collective-permute-start.2 = (bf16[24,8,128]{2,1,0:T(8,128)(2,1)S(1)}, bf16[24,8,128]{2,1,0:T(8,128)(2,1)}, u32[]{:S(2)}, u32[]{:S(2)}) collective-permute-start(bf16[24,8,128]{2,1,0:T(8,128)(2,1)S(1)} %pad_maximum_fusion.2), channel_id=1, source_target_pairs={{1,0},{2,1},{3,2},{4,3},{5,4},{6,5},{7,6},{0,7},{9,8},{10,9},{11,1... | collective-permute-start | bytes 147464 | tf_op jit(solution)/shard_map/ppermute | solution.py:99
  34.3 8.8 %collective-permute-start.3 = (bf16[24,8,128]{2,1,0:T(8,128)(2,1)}, bf16[24,8,128]{2,1,0:T(8,128)(2,1)}, u32[]{:S(2)}, u32[]{:S(2)}) collective-permute-start(bf16[24,8,128]{2,1,0:T(8,128)(2,1)} %pad_maximum_fusion.3), channel_id=1, source_target_pairs={{0,1},{1,2},{2,3},{3,4},{4,5},{5,6},{6,7},{7,0},{8,9},{9,10},{10,1... | collective-permute-start | bytes 147464 | tf_op jit(solution)/shard_map/ppermute | solution.py:98
  39.9 26.5 %copy-start = (bf16[128,8,4,128]{3,1,2,0:T(8,128)(2,1)}, bf16[128,8,4,128]{3,1,2,0:T(8,128)(2,1)S(1)}, u32[]{:S(2)}) copy-start(bf16[128,8,4,128]{3,1,2,0:T(8,128)(2,1)S(1)} %copy.45) | copy-start | bytes 3145732
  88.3 11.0 %collective-permute-start.4 = (bf16[2,128,128]{2,1,0:T(8,128)(2,1)S(1)}, bf16[2,128,128]{2,1,0:T(8,128)(2,1)S(1)}, u32[]{:S(2)}, u32[]{:S(2)}) collective-permute-start(bf16[2,128,128]{2,1,0:T(8,128)(2,1)S(1)} %get-tuple-element.31), channel_id=1, source_target_pairs={{0,8},{8,16},{16,24},{1,9},{9,17},{17,25},{2,10},{10,18},{18,26},{... | collective-permute-start | bytes 196616 | tf_op jit(solution)/shard_map/ppermute | solution.py:92
  92.5 6.8 %collective-permute-start.5 = (bf16[2,128,128]{2,1,0:T(8,128)(2,1)S(1)}, bf16[2,128,128]{2,1,0:T(8,128)(2,1)S(1)}, u32[]{:S(2)}, u32[]{:S(2)}) collective-permute-start(bf16[2,128,128]{2,1,0:T(8,128)(2,1)S(1)} %get-tuple-element.30), channel_id=1, source_target_pairs={{8,0},{16,8},{24,16},{9,1},{17,9},{25,17},{10,2},{18,10},{26,18},{... | collective-permute-start | bytes 196616 | tf_op jit(solution)/shard_map/ppermute | solution.py:93
  93.8 38.6 %all-to-all-start.1 = ((bf16[32,64,128]{2,1,0:T(8,128)(2,1)}), bf16[32,64,128]{2,1,0:T(8,128)(2,1)S(1)}, u32[]{:S(2)}, u32[]{:S(2)}) async-start(bf16[32,64,128]{2,1,0:T(8,128)(2,1)} %get-tuple-element.17), calls=%async_computation.1 | async-start | bytes 1048576 | tf_op jit(solution)/shard_map/all_to_all | solution.py:455
  99.3 6.6 %copy-start.9 = (bf16[2,128,128]{2,1,0:T(8,128)(2,1)}, bf16[2,128,128]{2,1,0:T(8,128)(2,1)S(1)}, u32[]{:S(2)}) copy-start(bf16[2,128,128]{2,1,0:T(8,128)(2,1)S(1)} %collective-permute-done.4.top_ref) | copy-start | bytes 196612
  99.3 6.6 %copy-start.10 = (bf16[2,128,128]{2,1,0:T(8,128)(2,1)}, bf16[2,128,128]{2,1,0:T(8,128)(2,1)S(1)}, u32[]{:S(2)}) copy-start(bf16[2,128,128]{2,1,0:T(8,128)(2,1)S(1)} %collective-permute-done.5.bottom_ref) | copy-start | bytes 196612
  99.4 10.0 %collective-permute-start.6 = (bf16[20,8,128]{2,1,0:T(8,128)(2,1)S(1)}, bf16[20,8,128]{2,1,0:T(8,128)(2,1)S(1)}, u32[]{:S(2)}, u32[]{:S(2)}) collective-permute-start(bf16[20,8,128]{2,1,0:T(8,128)(2,1)S(1)} %pad_maximum_fusion.4), channel_id=1, source_target_pairs={{1,0},{2,1},{3,2},{4,3},{5,4},{6,5},{7,6},{0,7},{9,8},{10,9},{11,1... | collective-permute-start | bytes 122888 | tf_op jit(solution)/shard_map/ppermute | solution.py:99
  102.8 9.9 %collective-permute-start.7 = (bf16[20,8,128]{2,1,0:T(8,128)(2,1)S(1)}, bf16[20,8,128]{2,1,0:T(8,128)(2,1)S(1)}, u32[]{:S(2)}, u32[]{:S(2)}) collective-permute-start(bf16[20,8,128]{2,1,0:T(8,128)(2,1)S(1)} %pad_maximum_fusion.5), channel_id=1, source_target_pairs={{0,1},{1,2},{2,3},{3,4},{4,5},{5,6},{6,7},{7,0},{8,9},{9,10},{10,1... | collective-permute-start | bytes 122888 | tf_op jit(solution)/shard_map/ppermute | solution.py:98
  103.5 9.9 %copy-start.11 = (f32[69]{0:T(128)S(1)}, f32[69]{0:T(128)}, u32[]{:S(2)}) copy-start(f32[69]{0:T(128)} %param.15) | copy-start | bytes 832
  132.4 0.8 copy-start.1
where the time goes:
time: 138 us; the launch traced here: 137 us
  Pallas kernels  71 us (51%)
  starting transfers between devices  27.8 us (20%)
  local copies, waits for them, and re-layouts  19.2 us (14%)
  waiting for transfers between devices  12.9 us (9%)
  other arithmetic  4.41 us (3%)
  between operations  1.63 us (1%)
    pallas_call x1, Pallas kernels, on_device(): call(forward_body, [((rows, cols, LANES), BF16), ((rows + 2 * HALO - 2, w...  21.9 us
    pallas_call x1, Pallas kernels, on_device(): call(observe_body, [((rows, cols, LANES), F32), ((rows, cols, LANES), BF1...  21 us
    pallas_call x1, Pallas kernels, on_device(): call(adjoint_body, [((v, rows, cols), F32)], 14, [VMEM((rows + 2 * BACK,...  18.4 us
    all_to_all x1, starting transfers between devices, on_device(): lax.all_to_all(send, ('lat', 'lon'), split_axis=0, concat_axis=0, tiled=T...  7.44 us
    ppermute x2, starting transfers between devices, halo(): top = lax.ppermute(mid[rows - width:], 'lat', up)  7.1 us
    ppermute x2, waiting for transfers between devices, halo(): bottom = lax.ppermute(mid[:width], 'lat', down)  6.11 us
    unnamed x29, local copies, waits for them, and re-layouts  5.75 us
    all_to_all x1, starting transfers between devices, on_device(): lax.all_to_all(pred, ('lat', 'lon'), split_axis=0, concat_axis=0, tiled=T...  5.43 us
  transfers between devices with their start and end apart: 10, of which 3 were waited for; matrix products, arithmetic and copies ran while one was open for 14% of the time, Pallas kernels for 31%

commit v1 on v0

--- a/solution.py
+++ b/solution.py
@@ -19,7 +19,7 @@
 SMEM = pltpu.SMEM
 
 
-def call(body, outs, n_in, scratch=(), smem=(), flops=0, moved=0, name=None):
+def call(body, outs, n_in, scratch=(), smem=(), flops=0, moved=0, name=None, limit=16):
     specs = [pl.BlockSpec(memory_space=SMEM if i in smem else VMEM) for i in range(n_in)]
     return pl.pallas_call(
         body,
@@ -28,6 +28,7 @@
         out_specs=tuple(pl.BlockSpec(memory_space=VMEM) for _ in outs),
         scratch_shapes=list(scratch),
         cost_estimate=pl.CostEstimate(flops=flops, bytes_accessed=moved, transcendentals=0),
+        compiler_params=pltpu.CompilerParams(vmem_limit_bytes=limit * 2**20),
         name=name,
     )
 
@@ -40,7 +41,25 @@
     return jnp.dot(a, b, preferred_element_type=F32)
 
 
-def state_body(a_ref, at_ref, s_ref, first_ref, last_ref):
+def dot_t(a, b):
+    return lax.dot_general(a, b, (((1,), (1,)), ((), ())), preferred_element_type=F32)
+
+
+def padded(ref, src_ref):
+    ref[...] = jnp.zeros_like(ref)
+    ref[0 : src_ref.shape[0], :] = src_ref[...]
+
+
+def edges(half, r, rows, width, first_ref, last_ref, head_ref, tail_ref):
+    first_ref[r] = half[:EDGE]
+    last_ref[r] = half[half.shape[0] - EDGE :]
+    if r < width:
+        head_ref[r] = half
+    if r >= rows - width:
+        tail_ref[r - rows + width] = half
+
+
+def state_body(a_ref, at_ref, s_ref, first_ref, last_ref, head_ref, tail_ref):
     v, rows, cols = a_ref.shape
     pad = jnp.zeros((LANES - v, cols), F32)
     for r in range(rows):
@@ -48,8 +67,18 @@
         at_ref[r] = x
         half = x.astype(BF16)
         s_ref[r] = half
-        first_ref[r] = half[:EDGE]
-        last_ref[r] = half[cols - EDGE :]
+        edges(half, r, rows, HALO, first_ref, last_ref, head_ref, tail_ref)
+
+
+def sides_body(top_ref, bottom_ref, first_ref, last_ref, near_ref, far_ref):
+    width, cols, _ = top_ref.shape
+    rows = first_ref.shape[0]
+    near_ref[0:width] = top_ref[:, :EDGE]
+    near_ref[width : width + rows] = first_ref[...]
+    near_ref[width + rows :] = bottom_ref[:, :EDGE]
+    far_ref[0:width] = top_ref[:, cols - EDGE :]
+    far_ref[width : width + rows] = last_ref[...]
+    far_ref[width + rows :] = bottom_ref[:, cols - EDGE :]
 
 
 def pack_body(order_ref, obs_ref, meta_ref, out_ref):
@@ -86,108 +115,170 @@
     return up, [(j, i) for i, j in up]
 
 
-def halo(mid, first, last, width):
+def halo(first, last, head, tail, after=None):
     up, down = shift_pairs(lax.axis_size("lat"), False)
-    rows = mid.shape[0]
-    top = lax.ppermute(mid[rows - width :], "lat", up)
-    bottom = lax.ppermute(mid[:width], "lat", down)
+    top = lax.ppermute(tail, "lat", up)
+    bottom = lax.ppermute(head, "lat", down)
     up, down = shift_pairs(lax.axis_size("lon"), True)
-    cols = mid.shape[1]
-    near = jnp.concatenate([top[:, :EDGE], first, bottom[:, :EDGE]], axis=0)
-    far = jnp.concatenate([top[:, cols - EDGE :], last, bottom[:, cols - EDGE :]], axis=0)
+    shape = (first.shape[0] + 2 * head.shape[0],) + first.shape[1:]
+    near, far = call(sides_body, [(shape, BF16)] * 2, 4, name="sides", limit=4)(
+        top, bottom, first, last
+    )
     left = lax.ppermute(far, "lon", up)
     right = lax.ppermute(near, "lon", down)
-    side = jnp.concatenate([right, left], axis=1)
-    return top, bottom, side
-
-
-def row_parts(mid_ref, top_ref, bottom_ref, width):
+    return top, bottom, right, left
+
+
+def bands(mid_ref, top_ref, bottom_ref, width):
     rows = mid_ref.shape[0]
     return (
-        (width, 0, top_ref),
-        (rows, width, mid_ref),
-        (width, width + rows, bottom_ref),
+        [(top_ref, r) for r in range(width)]
+        + [(mid_ref, r) for r in range(rows)]
+        + [(bottom_ref, r) for r in range(width)]
     )
 
 
-def put_shifted(ref, e, value):
-    w, ch = value.shape
-    ref[e, :, 0:ch] = pltpu.roll(value, 1, 0).astype(BF16)
-    ref[e, :, ch : 2 * ch] = value.astype(BF16)
-    ref[e, :, 2 * ch : 3 * ch] = pltpu.roll(value, w - 1, 0).astype(BF16)
-
-
-def conv_rows(ref, e, count, width, weight):
+def fold_row(nat_ref, e, q_n):
+    slabs = [nat_ref[e, pl.ds(q, SUB, stride=q_n), :] for q in range(q_n)]
+    return jnp.concatenate(slabs, axis=0)
+
+
+def unfold_row(nat_ref, e, value, q_n):
+    for q in range(q_n):
+        nat_ref[e, pl.ds(q, SUB, stride=q_n), :] = value[q * SUB : (q + 1) * SUB]
+
+
+def put_row(ref, e, value):
+    n, ch = value.shape
+    q_n = n // SUB
+    ref[e, 1 : q_n + 1] = value.astype(BF16).reshape(q_n, SUB, ch)
+    ref[e, 0] = pltpu.roll(value[n - SUB :], 1, 0).astype(BF16)
+    ref[e, q_n + 1] = pltpu.roll(value[:SUB], SUB - 1, 0).astype(BF16)
+
+
+def center(ref, e):
+    q_n, ch = ref.shape[1] - 2, ref.shape[3]
+    return ref[e, 1 : q_n + 1].reshape(q_n * SUB, ch)
+
+
+def conv_rows(ref, e, count, weight):
+    q_n, ch = ref.shape[1] - 2, ref.shape[3]
     parts = [
-        ref[pl.ds(e + i, count), 0:width, :].reshape(count * width, ref.shape[2]) for i in range(3)
+        ref[e + i : e + i + count, j : j + q_n].reshape(count * q_n * SUB, ch)
+        for i in range(3)
+        for j in range(3)
     ]
     return dot(jnp.concatenate(parts, axis=1), weight)
 
 
-def inside(row0_ref, a):
-    g = row0_ref[0] + a
-    return jnp.logical_and(g >= 0, g < row0_ref[1])
+def inside(lat_ref, a, rows, n_lat):
+    g = lat_ref[0] * rows + a
+    return jnp.logical_and(g >= 0, g < n_lat * rows)
 
 
 STEP = 2
+SUB = 16
 
 
 def forward_body(
-    row0_ref, mid_ref, top_ref, bottom_ref, side_ref, at_ref, enc_ref, w_ref, ro_ref,
-    cols_ref, slope0_ref, slope1_ref, a0, a1,
+    n_lat, lat_ref, mid_ref, top_ref, bottom_ref, right_ref, left_ref, at_ref, enc_in, w_ref, ro_in,
+    cols_ref, slope0_ref, slope1_ref, a0, a1, nat, back, enc_ref, ro_ref,
 ):
+    padded(enc_ref, enc_in)
+    padded(ro_ref, ro_in)
     rows, cols, _ = mid_ref.shape
-    width, ch = a0.shape[1], enc_ref.shape[1]
-    for count, base, src in row_parts(mid_ref, top_ref, bottom_ref, HALO):
-
-        def embed(i, c, base=base, src=src):
-            x = jnp.concatenate([src[i], side_ref[base + i]], axis=0)
-            h = dot(x, enc_ref[...]).astype(BF16).astype(F32)
-            put_shifted(a0, base + i, h)
-            return c
-
-        lax.fori_loop(0, count, embed, 0)
-
-    def first(k, c):
-        e = k * STEP
-        pre = conv_rows(a0, e, STEP, width, w_ref[0]).reshape(STEP, width, ch)
+    q_n = a0.shape[1] - 2
+    n = q_n * SUB
+    for e, (src, r) in enumerate(bands(mid_ref, top_ref, bottom_ref, HALO)):
+        nat[e, 0:cols, :] = src[r].astype(F32)
+        nat[e, cols : cols + EDGE, :] = right_ref[e].astype(F32)
+        nat[e, cols + EDGE :, :] = left_ref[e].astype(F32)
+        x = fold_row(nat, e, q_n).astype(BF16)
+        put_row(a0, e, dot(x, enc_ref[...]))
+
+    def first(e):
+        pre = conv_rows(a0, e, STEP, w_ref[0])
         s = sigma(pre)
         act = pre * s
-        slope0_ref[pl.ds(e, STEP)] = (s + act * (1.0 - s)).astype(BF16)
+        slope = (s + act * (1.0 - s)).astype(BF16)
         for q in range(STEP):
-            h = a0[e + q + 1, :, ch : 2 * ch].astype(F32) + act[q]
-            h = jnp.where(inside(row0_ref, e + q - HALO + 1), h, 0.0)
-            put_shifted(a1, e + q, h.astype(BF16).astype(F32))
-        return c
-
-    lax.fori_loop(0, (rows + 2 * HALO - 2) // STEP, first, 0)
-
-    def second(k, c):
-        e = k * STEP
-        pre = conv_rows(a1, e, STEP, width, w_ref[1]).reshape(STEP, width, ch)
+            at = slice(q * n, (q + 1) * n)
+            slope0_ref[e + q] = slope[at]
+            h = center(a0, e + q + 1).astype(F32) + act[at]
+            a = e + q - HALO + 1
+            if a < 0 or a >= rows:
+                h = jnp.where(inside(lat_ref, a, rows, n_lat), h, 0.0)
+            put_row(a1, e + q, h)
+
+    def second(e):
+        pre = conv_rows(a1, e, STEP, w_ref[1])
         s = sigma(pre)
         act = pre * s
-        slope1_ref[pl.ds(e, STEP)] = (s + act * (1.0 - s)).astype(BF16)
-        a = e - (HALO - 2)
-
-        @pl.when(jnp.logical_and(a >= 0, a < rows))
-        def _():
-            for q in range(STEP):
-                h = a1[e + q + 1, 0:cols, ch : 2 * ch].astype(F32) + act[q, 0:cols]
-                grow = dot(h.astype(BF16), ro_ref[...])
-                cols_ref[a + q] = (at_ref[a + q] + grow).astype(BF16)
-
-        return c
-
-    lax.fori_loop(0, (rows + 2 * HALO - 4) // STEP, second, 0)
+        slope = (s + act * (1.0 - s)).astype(BF16)
+        for q in range(STEP):
+            at = slice(q * n, (q + 1) * n)
+            slope1_ref[e + q] = slope[at]
+            a = e + q - HALO + 2
+            if 0 <= a < rows:
+                h = center(a1, e + q + 1).astype(F32) + act[at]
+                unfold_row(back, a, dot_t(h.astype(BF16), ro_ref[...]), q_n)
+                cols_ref[a] = (at_ref[a] + back[a, 0:cols, :]).astype(BF16)
+
+    for e in range(0, rows + 2 * HALO - 2, STEP):
+        first(e)
+    for e in range(0, rows + 2 * HALO - 4, STEP):
+        second(e)
+
+
+def adjoint_body(
+    n_lat, lat_ref, mid_ref, top_ref, bottom_ref, right_ref, left_ref, adj_ref, slope0_ref, slope1_ref,
+    rot_in, w_ref, enc_in, state_ref, prior_ref, prec_in,
+    out_ref, b1, b0, adj2, adj1, nat, back, rot_ref, enc_ref, prec_pad,
+):
+    padded(rot_ref, rot_in)
+    padded(enc_ref, enc_in)
+    prec_pad[...] = jnp.zeros_like(prec_pad)
+    prec_pad[0:1, 0 : prec_in.shape[1]] = prec_in[...]
+    rows, cols, _ = mid_ref.shape
+    q_n = b1.shape[1] - 2
+    n = q_n * SUB
+    v = out_ref.shape[0]
+    prec = jnp.broadcast_to(prec_pad[0:1, :], (LANES, LANES)).T[0:v, :]
+    for e, (src, r) in enumerate(bands(mid_ref, top_ref, bottom_ref, BACK)):
+        nat[e, 0:cols, :] = src[r].astype(F32)
+        nat[e, cols : cols + EDGE, :] = right_ref[e].astype(F32)
+        nat[e, cols + EDGE :, :] = left_ref[e].astype(F32)
+        g = dot(fold_row(nat, e, q_n).astype(BF16), rot_ref[...])
+        adj2[e] = g
+        put_row(b1, e, g * slope1_ref[e].astype(F32))
+
+    for e in range(0, rows + 2, STEP):
+        g = conv_rows(b1, e, STEP, w_ref[1])
+        for q in range(STEP):
+            total = adj2[e + q + 1] + g[q * n : (q + 1) * n]
+            adj1[e + q] = total
+            h = total * slope0_ref[e + q + 2].astype(F32)
+            a = e + q - 1
+            if a < 0 or a >= rows:
+                h = jnp.where(inside(lat_ref, a, rows, n_lat), h, 0.0)
+            put_row(b0, e + q, h)
+
+    for a in range(0, rows, STEP):
+        g = conv_rows(b0, a, STEP, w_ref[0])
+        for q in range(STEP):
+            total = adj1[a + q + 1] + g[q * n : (q + 1) * n]
+            unfold_row(back, a + q, dot_t(total.astype(BF16), enc_ref[...]), q_n)
+            grow = back[a + q, 0:cols, :] + adj_ref[a + q]
+            diff = state_ref[:, a + q, :] - prior_ref[:, a + q, :]
+            out_ref[:, a + q, :] = prec * diff + grow.T[0:v, :]
 
 
 BLOCK = 512
 
 
 def observe_body(
-    table_ref, cols_ref, got_ref, win_ref, wout_ref, woutt_ref, wint_ref, prec_ref,
-    adj_ref, half_ref, pred_ref,
+    table_ref, cols_ref, got_ref, win_ref, wout_ref, prec_ref,
+    adj_ref, half_ref, first_ref, last_ref, head_ref, tail_ref, pred_ref,
     xs, slope, grid, hot, weights, fa, meta,
 ):
     rows, cols, _ = cols_ref.shape
@@ -285,9 +376,9 @@
 
         def backward(k, c):
             at = pl.ds(k * BLOCK, BLOCK)
-            act = dot(grid[at, :], woutt_ref[...])
+            act = dot_t(grid[at, :], wout_ref[...])
             inner = (act * slope[at, :].astype(F32)).astype(BF16)
-            x = dot(inner, wint_ref[...])
+            x = dot_t(inner, win_ref[...])
             for f in range(4):
                 fa[place[f], at, :] += x[:, f * LANES : (f + 1) * LANES]
             return c
@@ -303,53 +394,10 @@
     total += pltpu.roll(one, 1, 0)
     total = total.reshape(rows, cols, LANES)
     adj_ref[...] = total
-    half_ref[...] = total.astype(BF16)
-
-
-def adjoint_body(
-    row0_ref, mid_ref, top_ref, bottom_ref, side_ref, adj_ref, slope0_ref, slope1_ref,
-    rot_ref, w_ref, enct_ref, state_ref, prior_ref, prec_ref,
-    out_ref, b1, b0, adj2, adj1,
-):
-    rows, cols, _ = mid_ref.shape
-    width, ch = b1.shape[1], rot_ref.shape[1]
-    v = out_ref.shape[0]
-    for count, base, src in row_parts(mid_ref, top_ref, bottom_ref, BACK):
-
-        def lift(i, c, base=base, src=src):
-            x = jnp.concatenate([src[i], side_ref[base + i]], axis=0)
-            g = dot(x, rot_ref[...])
-            adj2[base + i] = g
-            g = (g * slope1_ref[base + i].astype(F32)).astype(BF16)
-            put_shifted(b1, base + i, g.astype(F32))
-            return c
-
-        lax.fori_loop(0, count, lift, 0)
-
-    def first(k, c):
-        e = k * STEP
-        g = conv_rows(b1, e, STEP, width, w_ref[1]).reshape(STEP, width, ch)
-        for q in range(STEP):
-            total = adj2[e + q + 1] + g[q]
-            adj1[e + q] = total
-            h = total * slope0_ref[e + q + 2].astype(F32)
-            h = jnp.where(inside(row0_ref, e + q - 1), h, 0.0)
-            put_shifted(b0, e + q, h.astype(BF16).astype(F32))
-        return c
-
-    lax.fori_loop(0, (rows + 2) // STEP, first, 0)
-
-    def second(k, c):
-        a = k * STEP
-        g = conv_rows(b0, a, STEP, cols, w_ref[0]).reshape(STEP, cols, ch)
-        for q in range(STEP):
-            total = adj1[a + q + 1, 0:cols, :] + g[q]
-            grow = dot(total.astype(BF16), enct_ref[...]) + adj_ref[a + q]
-            diff = state_ref[:, a + q, :] - prior_ref[:, a + q, :]
-            out_ref[:, a + q, :] = prec_ref[...] * diff + grow.T[0:v, :]
-        return c
-
-    lax.fori_loop(0, rows // STEP, second, 0)
+    total = total.astype(BF16)
+    half_ref[...] = total
+    for r in range(rows):
+        edges(total[r], r, rows, BACK, first_ref, last_ref, head_ref, tail_ref)
 
 
 def arrangement_table():
@@ -385,14 +433,16 @@
     width = cols + 2 * EDGE
     cells = rows * cols
     lat, lon = lax.axis_index("lat"), lax.axis_index("lon")
-    row0 = jnp.stack([lat * rows, jnp.int32(n_lat * rows)])
-
-    at, s16, first, last = call(
+    lat_id = lat.reshape(1)
+
+    strip = (rows, EDGE, LANES)
+    at, s16, *rim = call(
         state_body,
-        [((rows, cols, LANES), F32), ((rows, cols, LANES), BF16)] + [((rows, EDGE, LANES), BF16)] * 2,
+        [((rows, cols, LANES), F32), ((rows, cols, LANES), BF16)]
+        + [(strip, BF16)] * 2 + [((HALO, cols, LANES), BF16)] * 2,
         1, moved=cells * v * 8, name="state",
     )(analysis_vector)
-    top, bottom, side = halo(s16, first, last, HALO)
+    top, bottom, right, left = halo(*rim)
 
     lon_total = cols * n_lon
     lat_g, lon_g = foot_cells // lon_total, foot_cells % lon_total
@@ -414,30 +464,36 @@
     )(order, obs_values, meta)
     got = lax.all_to_all(send, ("lat", "lon"), split_axis=0, concat_axis=0, tiled=True)
 
-    pad_v = ((0, LANES - v), (0, 0))
-    enc = jnp.pad(encoder_weight, pad_v)
-    rot = jnp.pad(readout_matrix.T, pad_v)
-    win = jnp.pad(obs_in_weight, ((0, 0),) + pad_v).reshape(foot * LANES, hid)
+    rot = readout_matrix.T
+    win = jnp.pad(obs_in_weight, ((0, 0), (0, LANES - v), (0, 0))).reshape(foot * LANES, hid)
     w_fwd = conv_weights.reshape(conv_weights.shape[0], 9 * ch, ch)
     w_back = jnp.transpose(conv_weights[:, ::-1, ::-1], (0, 1, 2, 4, 3)).reshape(w_fwd.shape)
 
     conv_flops = 2 * cells * 9 * ch * ch
     cols16, slope0, slope1 = call(
-        forward_body,
+        functools.partial(forward_body, n_lat),
         [
             ((rows, cols, LANES), BF16),
             ((rows + 2 * HALO - 2, width, ch), BF16),
             ((rows + 2 * HALO - 4, width, ch), BF16),
         ],
-        9,
-        [VMEM((rows + 2 * HALO, width, 3 * ch), BF16), VMEM((rows + 2 * HALO - 2, width, 3 * ch), BF16)],
-        (0,), 3 * conv_flops, cells * ch * 8, "forward",
-    )(row0, s16, top, bottom, side, at, enc, w_fwd, rot.T)
-
-    adj, adj16, pred = call(
+        10,
+        [
+            VMEM((rows + 2 * HALO, width // SUB + 2, SUB, ch), BF16),
+            VMEM((rows + 2 * HALO - 2, width // SUB + 2, SUB, ch), BF16),
+            VMEM((rows + 2 * HALO, width, LANES), F32),
+            VMEM((rows, width, LANES), F32),
+            VMEM((LANES, ch), BF16),
+            VMEM((LANES, ch), BF16),
+        ],
+        (0,), 3 * conv_flops, cells * ch * 8, "forward", 30,
+    )(lat_id, s16, top, bottom, right, left, at, encoder_weight, w_fwd, rot)
+
+    adj, adj16, *rim, pred = call(
         observe_body,
-        [((rows, cols, LANES), F32), ((rows, cols, LANES), BF16), ((tiles, per, nch), BF16)],
-        8,
+        [((rows, cols, LANES), F32), ((rows, cols, LANES), BF16)]
+        + [(strip, BF16)] * 2 + [((BACK, cols, LANES), BF16)] * 2 + [((tiles, per, nch), BF16)],
+        6,
         [
             VMEM((4, cells, LANES), BF16),
             VMEM((cells, hid), BF16),
@@ -447,28 +503,33 @@
             VMEM((4, cells, LANES), F32),
             VMEM((obs_n // LANES, META, LANES), F32),
         ],
-        (0,), 4 * cells * hid * (foot * LANES + nch), cells * hid * 4, "observe",
+        (0,), 4 * cells * hid * (foot * LANES + nch), cells * hid * 4, "observe", 32,
     )(
         jnp.array(arrangement_table(), jnp.int32), cols16, got, win, obs_out_weight,
-        obs_out_weight.T, win.T, obs_precision[None, :],
+        obs_precision[None, :],
     )
     back = lax.all_to_all(pred, ("lat", "lon"), split_axis=0, concat_axis=0, tiled=True)
 
-    top, bottom, side = halo(adj16, adj16[:, :EDGE], adj16[:, cols - EDGE :], BACK)
+    top, bottom, right, left = halo(*rim)
     (derivative,) = call(
-        adjoint_body,
+        functools.partial(adjoint_body, n_lat),
         [((v, rows, cols), F32)],
-        14,
+        15,
         [
-            VMEM((rows + 2 * BACK, width, 3 * ch), BF16),
-            VMEM((rows + 2, width, 3 * ch), BF16),
+            VMEM((rows + 2 * BACK, width // SUB + 2, SUB, ch), BF16),
+            VMEM((rows + 2, width // SUB + 2, SUB, ch), BF16),
             VMEM((rows + 2 * BACK, width, ch), F32),
             VMEM((rows + 2, width, ch), F32),
+            VMEM((rows + 2 * BACK, width, LANES), F32),
+            VMEM((rows, width, LANES), F32),
+            VMEM((LANES, ch), BF16),
+            VMEM((LANES, ch), BF16),
+            VMEM((8, LANES), F32),
         ],
-        (0,), 3 * conv_flops, cells * ch * 8, "adjoint",
+        (0,), 3 * conv_flops, cells * ch * 8, "adjoint", 34,
     )(
-        row0, adj16, top, bottom, side, adj, slope0, slope1, rot, w_back, enc.T,
-        analysis_vector, prior_estimate, jnp.broadcast_to(prior_precision[:, None], (v, cols)),
+        lat_id, adj16, top, bottom, right, left, adj, slope0, slope1, rot, w_back, encoder_weight,
+        analysis_vector, prior_estimate, prior_precision[None, :],
     )
     (departures,) = call(
         unpack_body, [((obs_n, nch), F32)], 5, smem=(0, 1), moved=obs_n * nch * 10, name="unpack"

time: 138 us -> 129 us (0.935)
  Pallas kernels: 71 us -> 51.1 us
  local copies, waits for them, and re-layouts: 19.2 us -> 27.5 us
  waiting for transfers between devices: 12.9 us -> 19.5 us
  other arithmetic: 4.41 us -> 1.05 us
    unnamed x29 -> x61, local copies, waits for them, and re-layouts: 5.75 us -> 22.2 us
    pallas_call x2 -> x4, Pallas kernels: 40.3 us -> 25.1 us  [the longest x1 12.3 us: on_device(): call(functools.partial(adjoint_body, n_lat), [((v, rows, cols), F32)], 15...]
    ppermute x4, waiting for transfers between devices: 6.11 us -> 14.5 us  [the longest x2 9.59 us: halo(): bottom = lax.ppermute(head, 'lat', down)]
    ppermute x2, waiting for transfers between devices: 3.4 us -> 0.39 us  [halo(): right = lax.ppermute(near, 'lon', down)]
    concatenate x6 -> x0, other arithmetic: 2.78 us -> none  [the longest x2 2.13 us: halo(): side = jnp.concatenate([right, left], axis=1)]
    slice x7 -> x0, local copies, waits for them, and re-layouts: 2.67 us -> none  [the longest x2 1.87 us: halo(): bottom = lax.ppermute(mid[:width], 'lat', down)]
    pallas_call x1, Pallas kernels: 2.61 us -> 0.41 us  [on_device(): call(state_body, [((rows, cols, LANES), F32), ((rows, cols, LANES), BF16)...]
    all_to_all x1, starting transfers between devices: 5.43 us -> 3.34 us  [on_device(): lax.all_to_all(pred, ('lat', 'lon'), split_axis=0, concat_axis=0, tiled=T...]
  transfers between devices with their start and end apart: 10 -> 10, of which waited for: 3 -> 7; matrix products, arithmetic and copies ran while one was open for 14% -> 5% of each run, Pallas kernels for 31% -> 20%
where the time goes in v1:
time: 129 us; the launch traced here: 128 us
  Pallas kernels  51.1 us (40%)
  local copies, waits for them, and re-layouts  27.5 us (21%)
  starting transfers between devices  26.9 us (21%)
  waiting for transfers between devices  19.5 us (15%)
  between operations  1.58 us (1%)
    unnamed x61, local copies, waits for them, and re-layouts  22.2 us
    pallas_call x1, Pallas kernels, on_device(): call(observe_body, [((rows, cols, LANES), F32), ((rows, cols, LANES), BF1...  19.4 us
    pallas_call x1, Pallas kernels, on_device(): call(functools.partial(adjoint_body, n_lat), [((v, rows, cols), F32)], 15...  12.3 us
    pallas_call x1, Pallas kernels, on_device(): call(functools.partial(forward_body, n_lat), [((rows, cols, LANES), BF16)...  12.1 us
    ppermute x2, waiting for transfers between devices, halo(): bottom = lax.ppermute(head, 'lat', down)  9.59 us
    all_to_all x1, starting transfers between devices, on_device(): lax.all_to_all(send, ('lat', 'lon'), split_axis=0, concat_axis=0, tiled=T...  7.44 us
    ppermute x2, starting transfers between devices, halo(): top = lax.ppermute(tail, 'lat', up)  7.08 us
    ppermute x2, starting transfers between devices, halo(): right = lax.ppermute(near, 'lon', down)  6.46 us
  transfers between devices with their start and end apart: 10, of which 7 were waited for; matrix products, arithmetic and copies ran while one was open for 5% of the time, Pallas kernels for 20%

profile of v1, /device:TPU:0, one launch (start us, length us, event | category | flops | bytes accessed | tf_op | source)
XLA Modules:
  0.0 127.8 jit_solution(8030204670581669037)
XLA Ops:
  0.6 0.0 copy-start.3
  0.7 0.1 broadcast_in_dim.46
  0.8 0.1 broadcast_in_dim.47
  0.9 0.9 fusion.18
  1.7 0.1 reduce_min.23
  1.8 0.1 reduce_min.25
  1.9 0.1 multiply_reduce_fusion
  2.0 0.1 stack.8
  2.1 0.1 copy.24
  2.2 0.1 copy.18
  2.2 0.1 copy.21
  3.0 0.1 convolution_convert_fusion
  3.2 0.1 broadcast_in_dim.50
  3.3 0.0 copy-start
  3.3 1.2 copy-done
  4.6 2.6 %pack.1 = bf16[32,72,128]{2,1,0:T(8,128)(2,1)} custom-call(s32[32]{0:T(128)S(1)} %fusion.16.order_ref, f32[2048,128]{1,0:T(8,128)S(1)} %copy-done, bf16[32,8,128]{2,1,0:T(8,128)(2,1)S(1)} %pad.8.meta_ref), custom_call_target="tpu_custom_call" | custom-call | bytes 1572864 | tf_op jit(solution)/shard_map/pack/pallas_call | solution.py:462
  7.2 7.4 %all-to-all-start = ((bf16[32,72,128]{2,1,0:T(8,128)(2,1)}), bf16[32,72,128]{2,1,0:T(8,128)(2,1)}, u32[]{:S(2)}, u32[]{:S(2)}) async-start(bf16[32,72,128]{2,1,0:T(8,128)(2,1)} %pack.1), calls=%async_computation | async-start | bytes 1179648 | tf_op jit(solution)/shard_map/all_to_all | solution.py:465
  14.6 0.4 state.1
  15.0 3.6 %collective-permute-start = (bf16[4,128,128]{2,1,0:T(8,128)(2,1)S(1)}, bf16[4,128,128]{2,1,0:T(8,128)(2,1)S(1)}, u32[]{:S(2)}, u32[]{:S(2)}) collective-permute-start(bf16[4,128,128]{2,1,0:T(8,128)(2,1)S(1)} %get-tuple-element.23), channel_id=1, source_target_pairs={{0,8},{8,16},{16,24},{1,9},{9,17},{17,25},{2,10},{10,18},{18,26},{... | collective-permute-start | bytes 393224 | tf_op jit(solution)/shard_map/ppermute | solution.py:120
  18.7 1.3 %collective-permute-start.1 = (bf16[4,128,128]{2,1,0:T(8,128)(2,1)S(1)}, bf16[4,128,128]{2,1,0:T(8,128)(2,1)S(1)}, u32[]{:S(2)}, u32[]{:S(2)}) collective-permute-start(bf16[4,128,128]{2,1,0:T(8,128)(2,1)S(1)} %get-tuple-element.24), channel_id=1, source_target_pairs={{8,0},{16,8},{24,16},{9,1},{17,9},{25,17},{10,2},{18,10},{26,18},{... | collective-permute-start | bytes 393224 | tf_op jit(solution)/shard_map/ppermute | solution.py:121
  20.0 3.3 %collective-permute-done.top_ref = bf16[4,128,128]{2,1,0:T(8,128)(2,1)S(1)} collective-permute-done((bf16[4,128,128]{2,1,0:T(8,128)(2,1)S(1)}, bf16[4,128,128]{2,1,0:T(8,128)(2,1)S(1)}, u32[]{:S(2)}, u32[]{:S(2)}) %collective-permute-start) | collective-permute-done | bytes 131104 | tf_op jit(solution)/shard_map/ppermute | solution.py:120
  23.2 5.9 %collective-permute-done.1.bottom_ref = bf16[4,128,128]{2,1,0:T(8,128)(2,1)S(1)} collective-permute-done((bf16[4,128,128]{2,1,0:T(8,128)(2,1)S(1)}, bf16[4,128,128]{2,1,0:T(8,128)(2,1)S(1)}, u32[]{:S(2)}, u32[]{:S(2)}) %collective-permute-start.1) | collective-permute-done | bytes 131104 | tf_op jit(solution)/shard_map/ppermute | solution.py:121
  29.2 3.2 %collective-permute-start.2 = (bf16[24,8,128]{2,1,0:T(8,128)(2,1)S(1)}, bf16[24,8,128]{2,1,0:T(8,128)(2,1)S(1)}, u32[]{:S(2)}, u32[]{:S(2)}) collective-permute-start(bf16[24,8,128]{2,1,0:T(8,128)(2,1)S(1)} %get-tuple-element.27), channel_id=1, source_target_pairs={{1,0},{2,1},{3,2},{4,3},{5,4},{6,5},{7,6},{0,7},{9,8},{10,9},{11,1... | collective-permute-start | bytes 147464 | tf_op jit(solution)/shard_map/ppermute | solution.py:128
  32.4 1.2 copy.28
  33.6 0.1 pad.9.clone
  33.7 0.4 collective-permute-done.2.right_ref
  34.1 3.6 %collective-permute-done.3.left_ref = bf16[24,8,128]{2,1,0:T(8,128)(2,1)S(1)} collective-permute-done((bf16[24,8,128]{2,1,0:T(8,128)(2,1)S(1)}, bf16[24,8,128]{2,1,0:T(8,128)(2,1)S(1)}, u32[]{:S(2)}, u32[]{:S(2)}) %collective-permute-start.3) | collective-permute-done | bytes 49184 | tf_op jit(solution)/shard_map/ppermute | solution.py:127
  37.7 0.0 copy-start.19
  37.7 12.1 %forward.1 = (bf16[16,128,128]{2,1,0:T(8,128)(2,1)S(1)}, bf16[22,144,256]{2,1,0:T(8,128)(2,1)S(1)}, bf16[20,144,256]{2,1,0:T(8,128)(2,1)S(1)}) custom-call(s32[1]{0:T(128)} %bitcast.2.lat_ref, bf16[16,128,128]{2,1,0:T(8,128)(2,1)S(1)} %get-tuple-element.22.mid_ref, bf16[4,128,128]{2,1,0:T(8,128)(2,1)S(1)} %collective-permute-done.top_ref, ...), custom_call_target="tpu_custom_call" | custom-call | flops 7247757312 | bytes 4194304 | tf_op jit(solution)/shard_map/forward/pallas_call | solution.py:473
  49.9 1.1 copy-done.20
  51.0 1.2 copy-done.22
  52.2 0.8 copy-done.28
  53.0 0.0 copy-start.12
  53.0 0.9 copy-done.12
  54.0 1.0 copy-done.29
  55.0 19.4 %observe.1 = (f32[16,128,128]{2,1,0:T(8,128)S(1)}, bf16[16,128,128]{2,1,0:T(8,128)(2,1)S(1)}, bf16[16,8,128]{2,1,0:T(8,128)(2,1)S(1)}, bf16[16,8,128]{2,1,0:T(8,...) custom-call(s32[24,5]{1,0:T(8,128)S(1)} %copy-done.19, ...), custom_call_target="tpu_custom_call" | custom-call | flops 5368709120 | bytes 8388608 | tf_op jit(solution)/shard_map/observe/pallas_call | solution.py:492
  74.4 0.8 copy-done.5
  75.3 0.6 copy-done.6
  75.9 0.6 copy-done.8
  76.5 0.6 copy-done.13
  77.1 1.0 copy-done.24
  78.1 0.8 copy-done.26
  78.9 3.3 %all-to-all-start.1 = ((bf16[32,64,128]{2,1,0:T(8,128)(2,1)}), bf16[32,64,128]{2,1,0:T(8,128)(2,1)}, u32[]{:S(2)}, u32[]{:S(2)}) async-start(bf16[32,64,128]{2,1,0:T(8,128)(2,1)} %copy-done.5), calls=%async_computation.1 | async-start | bytes 1048576 | tf_op jit(solution)/shard_map/all_to_all | solution.py:511
  82.2 3.5 %collective-permute-start.4 = (bf16[2,128,128]{2,1,0:T(8,128)(2,1)}, bf16[2,128,128]{2,1,0:T(8,128)(2,1)S(1)}, u32[]{:S(2)}, u32[]{:S(2)}) collective-permute-start(bf16[2,128,128]{2,1,0:T(8,128)(2,1)} %get-tuple-element.33), channel_id=1, source_target_pairs={{0,8},{8,16},{16,24},{1,9},{9,17},{17,25},{2,10},{10,18},{18,26},{... | collective-permute-start | bytes 196616 | tf_op jit(solution)/shard_map/ppermute | solution.py:120
  85.7 1.3 %collective-permute-start.5 = (bf16[2,128,128]{2,1,0:T(8,128)(2,1)}, bf16[2,128,128]{2,1,0:T(8,128)(2,1)S(1)}, u32[]{:S(2)}, u32[]{:S(2)}) collective-permute-start(bf16[2,128,128]{2,1,0:T(8,128)(2,1)} %copy-done.13), channel_id=1, source_target_pairs={{8,0},{16,8},{24,16},{9,1},{17,9},{25,17},{10,2},{18,10},{26,18},{... | collective-permute-start | bytes 196616 | tf_op jit(solution)/shard_map/ppermute | solution.py:121
  87.0 1.6 %collective-permute-done.4.top_ref = bf16[2,128,128]{2,1,0:T(8,128)(2,1)S(1)} collective-permute-done((bf16[2,128,128]{2,1,0:T(8,128)(2,1)}, bf16[2,128,128]{2,1,0:T(8,128)(2,1)S(1)}, u32[]{:S(2)}, u32[]{:S(2)}) %collective-permute-start.4) | collective-permute-done | bytes 65568 | tf_op jit(solution)/shard_map/ppermute | solution.py:120
  88.6 3.7 %collective-permute-done.5.bottom_ref = bf16[2,128,128]{2,1,0:T(8,128)(2,1)S(1)} collective-permute-done((bf16[2,128,128]{2,1,0:T(8,128)(2,1)}, bf16[2,128,128]{2,1,0:T(8,128)(2,1)S(1)}, u32[]{:S(2)}, u32[]{:S(2)}) %collective-permute-start.5) | collective-permute-done | bytes 65568 | tf_op jit(solution)/shard_map/ppermute | solution.py:121
  92.3 0.8 copy-done.7
  93.0 0.8 copy-done.9
  93.8 0.6 sides.3
  94.4 3.2 %collective-permute-start.6 = (bf16[20,8,128]{2,1,0:T(8,128)(2,1)}, bf16[20,8,128]{2,1,0:T(8,128)(2,1)}, u32[]{:S(2)}, u32[]{:S(2)}) collective-permute-start(bf16[20,8,128]{2,1,0:T(8,128)(2,1)} %get-tuple-element.37), channel_id=1, source_target_pairs={{1,0},{2,1},{3,2},{4,3},{5,4},{6,5},{7,6},{0,7},{9,8},{10,9},{11,1... | collective-permute-start | bytes 122888 | tf_op jit(solution)/shard_map/ppermute | solution.py:128
  97.7 1.6 %reverse_bitcast_fusion = bf16[2,3,3,256,256]{3,4,2,1,0:T(8,128)(2,1)} fusion(bf16[2,3,3,256,256]{4,3,2,1,0:T(8,128)(2,1)S(1)} %copy-done.2), kind=kLoop, calls=%fused_computation | loop fusion | bytes 4718592 | tf_op jit(solution)/shard_map/transpose | solution.py:470
  99.3 2.8 %copy.27 = bf16[2,3,3,256,256]{4,3,2,1,0:T(8,128)(2,1)S(1)} copy(bf16[2,3,3,256,256]{3,4,2,1,0:T(8,128)(2,1)} %reverse_bitcast_fusion) | data formatting | bytes 4718592 | tf_op jit(solution)/shard_map/transpose | solution.py:470
  102.1 1.1 collective-permute-done.7.left_ref
  103.2 1.1 copy-done.4
  104.3 1.1 copy-done.11
  105.3 0.8 copy-done.15
  106.1 0.8 copy-done.17
  106.9 1.4 %copy-done.21 = bf16[22,144,256]{2,1,0:T(8,128)(2,1)S(1)} copy-done((bf16[22,144,256]{2,1,0:T(8,128)(2,1)S(1)}, bf16[22,144,256]{2,1,0:T(8,128)(2,1)}, u32[]{:S(2)}) %copy-start.21) | copy-done | bytes 1622040
  108.3 1.4 %copy-done.23 = bf16[20,144,256]{2,1,0:T(8,128)(2,1)S(1)} copy-done((bf16[20,144,256]{2,1,0:T(8,128)(2,1)S(1)}, bf16[20,144,256]{2,1,0:T(8,128)(2,1)}, u32[]{:S(2)}) %copy-start.23) | copy-done | bytes 1474584
  109.7 1.2 copy-done.25
  110.9 1.0 copy-done.27
  111.9 12.3 %adjoint.1 = f32[69,16,128]{2,1,0:T(8,128)} custom-call(s32[1]{0:T(128)} %bitcast.2.lat_ref, bf16[16,128,128]{2,1,0:T(8,128)(2,1)S(1)} %copy-done.27, bf16[2,128,128]{2,1,0:T(8,128)(2,1)S(1)} %collective-permute-done.4.top_ref, bf16[2,128,128]{2,1,0:T(8,128)(2,1)S(1)} %collective-permute-done.5.bottom_ref, ...), custom_call_target="tpu_custom_call" | custom-call | flops 7247757312 | bytes 4194304 | tf_op jit(solution)/shard_map/adjoint/pallas_call | solution.py:514
  124.2 3.6 %unpack.1 = f32[2048,128]{1,0:T(8,128)} custom-call(s32[32]{0:T(128)S(1)} %fusion.16.order_ref, s32[1]{0:T(128)} %copy.30.count_ref, bf16[32,64,128]{2,1,0:T(8,128)(2,1)} %all-to-all-done.1.got_ref, f32[2048,128]{1,0:T(8,128)S(1)} %copy-done.1, f32[1,128]{1,0:T(1,128)S(1)} %bitcast.28), custom_call_target="tpu_custom_call" | custom-call | bytes 2621440 | tf_op jit(solution)/shard_map/unpack/pallas_call | solution.py:534
  (48 shorter events, 0.2 us)
Async XLA Ops:
  0.6 14.0 %copy-start.3 = (f32[69,16,128]{2,1,0:T(8,128)S(1)}, f32[69,16,128]{2,1,0:T(8,128)}, u32[]{:S(2)}) copy-start(f32[69,16,128]{2,1,0:T(8,128)} %state_ref.1) | copy-start | bytes 1695748
  3.3 1.2 copy-start
  7.2 30.6 %copy-start.2 = (bf16[2,3,3,256,256]{4,3,2,1,0:T(8,128)(2,1)S(1)}, bf16[2,3,3,256,256]{4,3,2,1,0:T(8,128)(2,1)}, u32[]{:S(2)}) copy-start(bf16[2,3,3,256,256]{4,3,2,1,0:T(8,128)(2,1)} %param.17) | copy-start | bytes 7077892
  7.2 30.6 %copy-start.14 = (bf16[69,256]{1,0:T(8,128)(2,1)S(1)}, bf16[69,256]{1,0:T(8,128)(2,1)}, u32[]{:S(2)}) copy-start(bf16[69,256]{1,0:T(8,128)(2,1)} %enc_in.3) | copy-start | bytes 105988
  7.2 30.6 %copy-start.16 = (bf16[256,69]{0,1:T(8,128)(2,1)S(1)}, bf16[256,69]{0,1:T(8,128)(2,1)}, u32[]{:S(2)}) copy-start(bf16[256,69]{0,1:T(8,128)(2,1)} %param.18) | copy-start | bytes 105988
  7.2 45.8 %all-to-all-start = ((bf16[32,72,128]{2,1,0:T(8,128)(2,1)}), bf16[32,72,128]{2,1,0:T(8,128)(2,1)}, u32[]{:S(2)}, u32[]{:S(2)}) async-start(bf16[32,72,128]{2,1,0:T(8,128)(2,1)} %pack.1), calls=%async_computation | async-start | bytes 1179648 | tf_op jit(solution)/shard_map/all_to_all | solution.py:465
  15.0 8.2 %collective-permute-start = (bf16[4,128,128]{2,1,0:T(8,128)(2,1)S(1)}, bf16[4,128,128]{2,1,0:T(8,128)(2,1)S(1)}, u32[]{:S(2)}, u32[]{:S(2)}) collective-permute-start(bf16[4,128,128]{2,1,0:T(8,128)(2,1)S(1)} %get-tuple-element.23), channel_id=1, source_target_pairs={{0,8},{8,16},{16,24},{1,9},{9,17},{17,25},{2,10},{10,18},{18,26},{... | collective-permute-start | bytes 393224 | tf_op jit(solution)/shard_map/ppermute | solution.py:120
  18.7 10.5 %collective-permute-start.1 = (bf16[4,128,128]{2,1,0:T(8,128)(2,1)S(1)}, bf16[4,128,128]{2,1,0:T(8,128)(2,1)S(1)}, u32[]{:S(2)}, u32[]{:S(2)}) collective-permute-start(bf16[4,128,128]{2,1,0:T(8,128)(2,1)S(1)} %get-tuple-element.24), channel_id=1, source_target_pairs={{8,0},{16,8},{24,16},{9,1},{17,9},{25,17},{10,2},{18,10},{26,18},{... | collective-permute-start | bytes 393224 | tf_op jit(solution)/shard_map/ppermute | solution.py:121
  29.2 5.0 %collective-permute-start.2 = (bf16[24,8,128]{2,1,0:T(8,128)(2,1)S(1)}, bf16[24,8,128]{2,1,0:T(8,128)(2,1)S(1)}, u32[]{:S(2)}, u32[]{:S(2)}) collective-permute-start(bf16[24,8,128]{2,1,0:T(8,128)(2,1)S(1)} %get-tuple-element.27), channel_id=1, source_target_pairs={{1,0},{2,1},{3,2},{4,3},{5,4},{6,5},{7,6},{0,7},{9,8},{10,9},{11,1... | collective-permute-start | bytes 147464 | tf_op jit(solution)/shard_map/ppermute | solution.py:128
  32.4 5.3 %collective-permute-start.3 = (bf16[24,8,128]{2,1,0:T(8,128)(2,1)S(1)}, bf16[24,8,128]{2,1,0:T(8,128)(2,1)S(1)}, u32[]{:S(2)}, u32[]{:S(2)}) collective-permute-start(bf16[24,8,128]{2,1,0:T(8,128)(2,1)S(1)} %get-tuple-element.28), channel_id=1, source_target_pairs={{0,1},{1,2},{2,3},{3,4},{4,5},{5,6},{6,7},{7,0},{8,9},{9,10},{10,1... | collective-permute-start | bytes 147464 | tf_op jit(solution)/shard_map/ppermute | solution.py:127
  37.7 15.3 %copy-start.10 = (f32[128]{0:T(128)S(1)}, f32[128]{0:T(128)}, u32[]{:S(2)}) copy-start(f32[128]{0:T(128)} %param.22) | copy-start | bytes 1540
  37.7 15.3 %copy-start.19 = (s32[24,5]{1,0:T(8,128)S(1)}, s32[24,5]{1,0:T(8,128)}, u32[]{:S(2)}) copy-start(s32[24,5]{1,0:T(8,128)} %constant.123.clone.table_ref) | copy-start | bytes 1444
  49.9 1.2 copy-start.20
  51.0 1.2 copy-start.22
  52.2 0.8 copy-start.28
  53.0 1.0 copy-start.12
  54.0 1.0 copy-start.29
  74.4 0.8 copy-start.5
  75.3 0.6 copy-start.6
  75.9 0.6 copy-start.8
  76.5 0.6 copy-start.13
  77.1 1.0 copy-start.24
  78.1 0.8 copy-start.26
  78.9 45.3 %all-to-all-start.1 = ((bf16[32,64,128]{2,1,0:T(8,128)(2,1)}), bf16[32,64,128]{2,1,0:T(8,128)(2,1)}, u32[]{:S(2)}, u32[]{:S(2)}) async-start(bf16[32,64,128]{2,1,0:T(8,128)(2,1)} %copy-done.5), calls=%async_computation.1 | async-start | bytes 1048576 | tf_op jit(solution)/shard_map/all_to_all | solution.py:511
  82.2 6.4 %collective-permute-start.4 = (bf16[2,128,128]{2,1,0:T(8,128)(2,1)}, bf16[2,128,128]{2,1,0:T(8,128)(2,1)S(1)}, u32[]{:S(2)}, u32[]{:S(2)}) collective-permute-start(bf16[2,128,128]{2,1,0:T(8,128)(2,1)} %get-tuple-element.33), channel_id=1, source_target_pairs={{0,8},{8,16},{16,24},{1,9},{9,17},{17,25},{2,10},{10,18},{18,26},{... | collective-permute-start | bytes 196616 | tf_op jit(solution)/shard_map/ppermute | solution.py:120
  85.7 6.6 %collective-permute-start.5 = (bf16[2,128,128]{2,1,0:T(8,128)(2,1)}, bf16[2,128,128]{2,1,0:T(8,128)(2,1)S(1)}, u32[]{:S(2)}, u32[]{:S(2)}) collective-permute-start(bf16[2,128,128]{2,1,0:T(8,128)(2,1)} %copy-done.13), channel_id=1, source_target_pairs={{8,0},{16,8},{24,16},{9,1},{17,9},{25,17},{10,2},{18,10},{26,18},{... | collective-permute-start | bytes 196616 | tf_op jit(solution)/shard_map/ppermute | solution.py:121
  92.2 0.8 copy-start.7
  93.0 0.8 copy-start.9
  94.4 7.7 %collective-permute-start.6 = (bf16[20,8,128]{2,1,0:T(8,128)(2,1)}, bf16[20,8,128]{2,1,0:T(8,128)(2,1)}, u32[]{:S(2)}, u32[]{:S(2)}) collective-permute-start(bf16[20,8,128]{2,1,0:T(8,128)(2,1)} %get-tuple-element.37), channel_id=1, source_target_pairs={{1,0},{2,1},{3,2},{4,3},{5,4},{6,5},{7,6},{0,7},{9,8},{10,9},{11,1... | collective-permute-start | bytes 122888 | tf_op jit(solution)/shard_map/ppermute | solution.py:128
  97.7 5.5 %collective-permute-start.7 = (bf16[20,8,128]{2,1,0:T(8,128)(2,1)}, bf16[20,8,128]{2,1,0:T(8,128)(2,1)}, u32[]{:S(2)}, u32[]{:S(2)}) collective-permute-start(bf16[20,8,128]{2,1,0:T(8,128)(2,1)} %get-tuple-element.38), channel_id=1, source_target_pairs={{0,1},{1,2},{2,3},{3,4},{4,5},{5,6},{6,7},{7,0},{8,9},{9,10},{10,1... | collective-permute-start | bytes 122888 | tf_op jit(solution)/shard_map/ppermute | solution.py:127
  99.3 4.0 %copy-start.18 = (f32[69]{0:T(128)S(1)}, f32[69]{0:T(128)}, u32[]{:S(2)}) copy-start(f32[69]{0:T(128)} %param.15) | copy-start | bytes 832
  103.2 1.1 copy-start.4
  104.3 1.1 copy-start.11
  105.3 0.8 copy-start.15
  106.1 0.8 copy-start.17
  106.9 1.4 %copy-start.21 = (bf16[22,144,256]{2,1,0:T(8,128)(2,1)S(1)}, bf16[22,144,256]{2,1,0:T(8,128)(2,1)}, u32[]{:S(2)}) copy-start(bf16[22,144,256]{2,1,0:T(8,128)(2,1)} %copy-done.20) | copy-start | bytes 4866052
  108.3 1.4 %copy-start.23 = (bf16[20,144,256]{2,1,0:T(8,128)(2,1)S(1)}, bf16[20,144,256]{2,1,0:T(8,128)(2,1)}, u32[]{:S(2)}) copy-start(bf16[20,144,256]{2,1,0:T(8,128)(2,1)} %copy-done.22) | copy-start | bytes 4423684
  109.7 1.2 copy-start.25
  110.9 1.0 copy-start.27
  111.9 12.3 %copy-start.1 = (f32[2048,128]{1,0:T(8,128)S(1)}, f32[2048,128]{1,0:T(8,128)}, u32[]{:S(2)}) copy-start(f32[2048,128]{1,0:T(8,128)} %obs_ref.3) | copy-start | bytes 3145732

commit v2 on v1

--- a/solution.py
+++ b/solution.py
@@ -19,13 +19,17 @@
 SMEM = pltpu.SMEM
 
 
-def call(body, outs, n_in, scratch=(), smem=(), flops=0, moved=0, name=None, limit=16):
-    specs = [pl.BlockSpec(memory_space=SMEM if i in smem else VMEM) for i in range(n_in)]
+def call(body, outs, n_in, scratch=(), smem=(), flops=0, moved=0, name=None, limit=53, far=(), far_out=()):
+    def spec(i, far=far, smem=smem):
+        space = SMEM if i in smem else pltpu.HBM if i in far else VMEM
+        return pl.BlockSpec(memory_space=space)
+
+    specs = [spec(i) for i in range(n_in)]
     return pl.pallas_call(
         body,
         out_shape=tuple(jax.ShapeDtypeStruct(s, d) for s, d in outs),
         in_specs=specs,
-        out_specs=tuple(pl.BlockSpec(memory_space=VMEM) for _ in outs),
+        out_specs=tuple(spec(i, far_out, ()) for i in range(len(outs))),
         scratch_shapes=list(scratch),
         cost_estimate=pl.CostEstimate(flops=flops, bytes_accessed=moved, transcendentals=0),
         compiler_params=pltpu.CompilerParams(vmem_limit_bytes=limit * 2**20),
@@ -43,6 +47,12 @@
 
 def dot_t(a, b):
     return lax.dot_general(a, b, (((1,), (1,)), ((), ())), preferred_element_type=F32)
+
+
+def fetch(src, dst, sem):
+    copy = pltpu.make_async_copy(src, dst, sem)
+    copy.start()
+    return copy
 
 
 def padded(ref, src_ref):
@@ -115,18 +125,22 @@
     return up, [(j, i) for i, j in up]
 
 
-def halo(first, last, head, tail, after=None):
+def halo_rows(first, last, head, tail):
     up, down = shift_pairs(lax.axis_size("lat"), False)
     top = lax.ppermute(tail, "lat", up)
     bottom = lax.ppermute(head, "lat", down)
-    up, down = shift_pairs(lax.axis_size("lon"), True)
     shape = (first.shape[0] + 2 * head.shape[0],) + first.shape[1:]
-    near, far = call(sides_body, [(shape, BF16)] * 2, 4, name="sides", limit=4)(
+    near, far = call(sides_body, [(shape, BF16)] * 2, 4, name="sides")(
         top, bottom, first, last
     )
+    return top, bottom, near, far
+
+
+def halo_columns(near, far):
+    up, down = shift_pairs(lax.axis_size("lon"), True)
     left = lax.ppermute(far, "lon", up)
     right = lax.ppermute(near, "lon", down)
-    return top, bottom, right, left
+    return right, left
 
 
 def bands(mid_ref, top_ref, bottom_ref, width):
@@ -171,6 +185,17 @@
     return dot(jnp.concatenate(parts, axis=1), weight)
 
 
+def conv_back(ref, e, count, weight_ref):
+    q_n, ch = ref.shape[1] - 2, ref.shape[3]
+    parts = [
+        ref[e + i : e + i + count, j : j + q_n].reshape(count * q_n * SUB, ch)
+        for i in range(3)
+        for j in range(3)
+    ]
+    taps = [weight_ref[(8 - t) * ch : (9 - t) * ch, :] for t in range(9)]
+    return dot_t(jnp.concatenate(parts, axis=1), jnp.concatenate(taps, axis=1))
+
+
 def inside(lat_ref, a, rows, n_lat):
     g = lat_ref[0] * rows + a
     return jnp.logical_and(g >= 0, g < n_lat * rows)
@@ -182,8 +207,12 @@
 
 def forward_body(
     n_lat, lat_ref, mid_ref, top_ref, bottom_ref, right_ref, left_ref, at_ref, enc_in, w_ref, ro_in,
-    cols_ref, slope0_ref, slope1_ref, a0, a1, nat, back, enc_ref, ro_ref,
+    cols_ref, slope0_out, slope1_out,
+    a0, a1, nat, back, enc_ref, ro_ref, w_v, at_v, slope0_ref, slope1_ref, sem,
 ):
+    w0 = fetch(w_ref.at[0], w_v.at[0], sem.at[0])
+    w1 = fetch(w_ref.at[1], w_v.at[1], sem.at[1])
+    at_in = fetch(at_ref, at_v, sem.at[2])
     padded(enc_ref, enc_in)
     padded(ro_ref, ro_in)
     rows, cols, _ = mid_ref.shape
@@ -197,7 +226,7 @@
         put_row(a0, e, dot(x, enc_ref[...]))
 
     def first(e):
-        pre = conv_rows(a0, e, STEP, w_ref[0])
+        pre = conv_rows(a0, e, STEP, w_v[0])
         s = sigma(pre)
         act = pre * s
         slope = (s + act * (1.0 - s)).astype(BF16)
@@ -211,7 +240,7 @@
             put_row(a1, e + q, h)
 
     def second(e):
-        pre = conv_rows(a1, e, STEP, w_ref[1])
+        pre = conv_rows(a1, e, STEP, w_v[1])
         s = sigma(pre)
         act = pre * s
         slope = (s + act * (1.0 - s)).astype(BF16)
@@ -222,19 +251,37 @@
             if 0 <= a < rows:
                 h = center(a1, e + q + 1).astype(F32) + act[at]
                 unfold_row(back, a, dot_t(h.astype(BF16), ro_ref[...]), q_n)
-                cols_ref[a] = (at_ref[a] + back[a, 0:cols, :]).astype(BF16)
-
+                cols_ref[a] = (at_v[a] + back[a, 0:cols, :]).astype(BF16)
+
+    w0.wait()
     for e in range(0, rows + 2 * HALO - 2, STEP):
         first(e)
+    out0 = fetch(slope0_ref, slope0_out, sem.at[3])
+    w1.wait()
+    at_in.wait()
     for e in range(0, rows + 2 * HALO - 4, STEP):
         second(e)
+    out1 = fetch(slope1_ref, slope1_out, sem.at[4])
+    out0.wait()
+    out1.wait()
 
 
 def adjoint_body(
-    n_lat, lat_ref, mid_ref, top_ref, bottom_ref, right_ref, left_ref, adj_ref, slope0_ref, slope1_ref,
-    rot_in, w_ref, enc_in, state_ref, prior_ref, prec_in,
+    n_lat, lat_ref, mid_ref, top_ref, bottom_ref, right_ref, left_ref, adj_in, slope0_in, slope1_in,
+    rot_in, w_in, enc_in, state_in, prior_in, prec_in,
     out_ref, b1, b0, adj2, adj1, nat, back, rot_ref, enc_ref, prec_pad,
+    adj_ref, slope0_ref, slope1_ref, w_ref, state_ref, prior_ref, sem,
 ):
+    slope1_got = fetch(slope1_in, slope1_ref, sem.at[0])
+    w1 = fetch(w_in.at[1], w_ref.at[1], sem.at[1])
+    slope0_got = fetch(slope0_in, slope0_ref, sem.at[2])
+    w0 = fetch(w_in.at[0], w_ref.at[0], sem.at[3])
+    late = [
+        fetch(src, dst, sem.at[4 + i])
+        for i, (src, dst) in enumerate(
+            ((adj_in, adj_ref), (state_in, state_ref), (prior_in, prior_ref))
+        )
+    ]
     padded(rot_ref, rot_in)
     padded(enc_ref, enc_in)
     prec_pad[...] = jnp.zeros_like(prec_pad)
@@ -244,6 +291,7 @@
     n = q_n * SUB
     v = out_ref.shape[0]
     prec = jnp.broadcast_to(prec_pad[0:1, :], (LANES, LANES)).T[0:v, :]
+    slope1_got.wait()
     for e, (src, r) in enumerate(bands(mid_ref, top_ref, bottom_ref, BACK)):
         nat[e, 0:cols, :] = src[r].astype(F32)
         nat[e, cols : cols + EDGE, :] = right_ref[e].astype(F32)
@@ -252,8 +300,10 @@
         adj2[e] = g
         put_row(b1, e, g * slope1_ref[e].astype(F32))
 
+    slope0_got.wait()
+    w1.wait()
     for e in range(0, rows + 2, STEP):
-        g = conv_rows(b1, e, STEP, w_ref[1])
+        g = conv_back(b1, e, STEP, w_ref.at[1])
         for q in range(STEP):
             total = adj2[e + q + 1] + g[q * n : (q + 1) * n]
             adj1[e + q] = total
@@ -263,8 +313,11 @@
                 h = jnp.where(inside(lat_ref, a, rows, n_lat), h, 0.0)
             put_row(b0, e + q, h)
 
+    w0.wait()
+    for copy in late:
+        copy.wait()
     for a in range(0, rows, STEP):
-        g = conv_rows(b0, a, STEP, w_ref[0])
+        g = conv_back(b0, a, STEP, w_ref.at[0])
         for q in range(STEP):
             total = adj1[a + q + 1] + g[q * n : (q + 1) * n]
             unfold_row(back, a + q, dot_t(total.astype(BF16), enc_ref[...]), q_n)
@@ -273,14 +326,15 @@
             out_ref[:, a + q, :] = prec * diff + grow.T[0:v, :]
 
 
-BLOCK = 512
+BLOCK = 1024
 
 
 def observe_body(
-    table_ref, cols_ref, got_ref, win_ref, wout_ref, prec_ref,
+    table_ref, cols_ref, got_in, win_ref, wout_ref, prec_ref,
     adj_ref, half_ref, first_ref, last_ref, head_ref, tail_ref, pred_ref,
-    xs, slope, grid, hot, weights, fa, meta,
+    xs, slope, grid, hot, weights, fa, meta, got_ref, sem,
 ):
+    got = fetch(got_in, got_ref, sem.at[0])
     rows, cols, _ = cols_ref.shape
     cells = rows * cols
     half = cells // 2
@@ -295,6 +349,7 @@
     xs[2] = jnp.concatenate([c0[cols:], c0[:cols]], axis=0)
     xs[3] = jnp.concatenate([c1[cols:], c1[:cols]], axis=0)
     rest = jnp.zeros((1, LANES), F32)
+    got.wait()
     for m in range(obs_n // LANES):
         total = got_ref[m * group, per : per + META, :].astype(F32)
         for g in range(1, group):
@@ -442,7 +497,8 @@
         + [(strip, BF16)] * 2 + [((HALO, cols, LANES), BF16)] * 2,
         1, moved=cells * v * 8, name="state",
     )(analysis_vector)
-    top, bottom, right, left = halo(*rim)
+    foot_cells, obs_sent, *rim = lax.optimization_barrier((foot_cells, obs_values, *rim))
+    top, bottom, near, far = halo_rows(*rim)
 
     lon_total = cols * n_lon
     lat_g, lon_g = foot_cells // lon_total, foot_cells % lon_total
@@ -461,13 +517,14 @@
     meta = jnp.pad(meta, ((0, 0), (0, META - 3), (0, 0)))
     (send,) = call(
         pack_body, [((tiles, per + META, nch), BF16)], 3, smem=(0,), moved=obs_n * nch * 6, name="pack"
-    )(order, obs_values, meta)
+    )(order, obs_sent, meta)
+    send, near, far = lax.optimization_barrier((send, near, far))
+    right, left = halo_columns(near, far)
     got = lax.all_to_all(send, ("lat", "lon"), split_axis=0, concat_axis=0, tiled=True)
 
     rot = readout_matrix.T
     win = jnp.pad(obs_in_weight, ((0, 0), (0, LANES - v), (0, 0))).reshape(foot * LANES, hid)
     w_fwd = conv_weights.reshape(conv_weights.shape[0], 9 * ch, ch)
-    w_back = jnp.transpose(conv_weights[:, ::-1, ::-1], (0, 1, 2, 4, 3)).reshape(w_fwd.shape)
 
     conv_flops = 2 * cells * 9 * ch * ch
     cols16, slope0, slope1 = call(
@@ -485,8 +542,13 @@
             VMEM((rows, width, LANES), F32),
             VMEM((LANES, ch), BF16),
             VMEM((LANES, ch), BF16),
+            VMEM(w_fwd.shape, BF16),
+            VMEM((rows, cols, LANES), F32),
+            VMEM((rows + 2 * HALO - 2, width, ch), BF16),
+            VMEM((rows + 2 * HALO - 4, width, ch), BF16),
+            pltpu.SemaphoreType.DMA((5,)),
         ],
-        (0,), 3 * conv_flops, cells * ch * 8, "forward", 30,
+        (0,), 3 * conv_flops, cells * ch * 8, "forward", far=(6, 8), far_out=(1, 2),
     )(lat_id, s16, top, bottom, right, left, at, encoder_weight, w_fwd, rot)
 
     adj, adj16, *rim, pred = call(
@@ -502,15 +564,18 @@
             VMEM((obs_n, 2 * nch), BF16),
             VMEM((4, cells, LANES), F32),
             VMEM((obs_n // LANES, META, LANES), F32),
+            VMEM(got.shape, BF16),
+            pltpu.SemaphoreType.DMA((1,)),
         ],
-        (0,), 4 * cells * hid * (foot * LANES + nch), cells * hid * 4, "observe", 32,
+        (0,), 4 * cells * hid * (foot * LANES + nch), cells * hid * 4, "observe", far=(2,),
     )(
         jnp.array(arrangement_table(), jnp.int32), cols16, got, win, obs_out_weight,
         obs_precision[None, :],
     )
     back = lax.all_to_all(pred, ("lat", "lon"), split_axis=0, concat_axis=0, tiled=True)
 
-    top, bottom, right, left = halo(*rim)
+    top, bottom, near, far = halo_rows(*rim)
+    right, left = halo_columns(near, far)
     (derivative,) = call(
         functools.partial(adjoint_body, n_lat),
         [((v, rows, cols), F32)],
@@ -525,10 +590,17 @@
             VMEM((LANES, ch), BF16),
             VMEM((LANES, ch), BF16),
             VMEM((8, LANES), F32),
+            VMEM((rows, cols, LANES), F32),
+            VMEM(slope0.shape, BF16),
+            VMEM(slope1.shape, BF16),
+            VMEM(w_fwd.shape, BF16),
+            VMEM((v, rows, cols), F32),
+            VMEM((v, rows, cols), F32),
+            pltpu.SemaphoreType.DMA((7,)),
         ],
-        (0,), 3 * conv_flops, cells * ch * 8, "adjoint", 34,
+        (0,), 3 * conv_flops, cells * ch * 8, "adjoint", far=(6, 7, 8, 10, 12, 13),
     )(
-        lat_id, adj16, top, bottom, right, left, adj, slope0, slope1, rot, w_back, encoder_weight,
+        lat_id, adj16, top, bottom, right, left, adj, slope0, slope1, rot, w_fwd, encoder_weight,
         analysis_vector, prior_estimate, prior_precision[None, :],
     )
     (departures,) = call(

time: 129 us -> 119 us (0.922)
  local copies, waits for them, and re-layouts: 27.5 us -> 5.54 us
  Pallas kernels: 51.1 us -> 59.7 us
  starting transfers between devices: 26.9 us -> 30.1 us
    unnamed x61 -> x23, local copies, waits for them, and re-layouts: 22.2 us -> 3.66 us
    transpose x2 -> x0, local copies, waits for them, and re-layouts: 4.44 us -> none  [on_device(): jnp.transpose(conv_weights[:, ::-1, ::-1], (0, 1, 2, 4, 3))]
    pallas_call x1, Pallas kernels: 12.1 us -> 16 us  [on_device(): call(functools.partial(forward_body, n_lat), [((rows, cols, LANES), BF16)...]
    all_to_all x1, starting transfers between devices: 3.34 us -> 5.5 us  [on_device(): lax.all_to_all(pred, ('lat', 'lon'), split_axis=0, concat_axis=0, tiled=T...]
    pallas_call x1, Pallas kernels: 0.41 us -> 2.44 us  [on_device(): call(state_body, [((rows, cols, LANES), F32), ((rows, cols, LANES), BF16)...]
    pallas_call x1, Pallas kernels: 12.3 us -> 14.2 us  [on_device(): call(functools.partial(adjoint_body, n_lat), [((v, rows, cols), F32)], 15...]
    ppermute x8, starting transfers between devices: 16.1 us -> 17.7 us  [the longest x2 8.54 us: halo_rows(): top = lax.ppermute(tail, 'lat', up)]
  transfers between devices with their start and end apart: 10 -> 10, of which waited for: 7 -> 7; matrix products, arithmetic and copies ran while one was open for 5% -> 3% of each run, Pallas kernels for 20% -> 28%
where the time goes in v2:
time: 119 us; the launch traced here: 118 us
  Pallas kernels  59.7 us (50%)
  starting transfers between devices  30.1 us (25%)
  waiting for transfers between devices  20.3 us (17%)
  local copies, waits for them, and re-layouts  5.54 us (5%)
  between operations  1.52 us (1%)
    pallas_call x1, Pallas kernels, on_device(): call(observe_body, [((rows, cols, LANES), F32), ((rows, cols, LANES), BF1...  19.8 us
    pallas_call x1, Pallas kernels, on_device(): call(functools.partial(forward_body, n_lat), [((rows, cols, LANES), BF16)...  16 us
    pallas_call x1, Pallas kernels, on_device(): call(functools.partial(adjoint_body, n_lat), [((v, rows, cols), F32)], 15...  14.2 us
    ppermute x2, starting transfers between devices, halo_rows(): top = lax.ppermute(tail, 'lat', up)  8.54 us
    ppermute x2, waiting for transfers between devices, halo_columns(): right = lax.ppermute(near, 'lon', down)  8.21 us
    ppermute x2, waiting for transfers between devices, halo_columns(): left = lax.ppermute(far, 'lon', up)  6.93 us
    all_to_all x1, starting transfers between devices, on_device(): lax.all_to_all(send, ('lat', 'lon'), split_axis=0, concat_axis=0, tiled=T...  6.88 us
    ppermute x2, starting transfers between devices, halo_columns(): right = lax.ppermute(near, 'lon', down)  6.55 us
  transfers between devices with their start and end apart: 10, of which 7 were waited for; matrix products, arithmetic and copies ran while one was open for 3% of the time, Pallas kernels for 28%

profile of v2, /device:TPU:0, one launch (start us, length us, event | category | flops | bytes accessed | tf_op | source)
XLA Modules:
  0.0 118.3 jit_solution(12763835429701932548)
XLA Ops:
  0.6 2.4 %state.1 = (f32[16,128,128]{2,1,0:T(8,128)}, bf16[16,128,128]{2,1,0:T(8,128)(2,1)S(1)}, bf16[16,8,128]{2,1,0:T(8,128)(2,1)S(1)}, bf16[16,8,128]{2,1,0:T(8,128)(2...) custom-call(f32[69,16,128]{2,1,0:T(8,128)} %state_in.1), custom_call_target="tpu_custom_call" | custom-call | bytes 1130496 | tf_op jit(solution)/shard_map/state/pallas_call | solution.py:494
  3.1 0.0 copy-start.1
  3.1 0.8 copy-done.1
  3.9 4.9 %collective-permute-start = (bf16[4,128,128]{2,1,0:T(8,128)(2,1)S(1)}, bf16[4,128,128]{2,1,0:T(8,128)(2,1)S(1)}, u32[]{:S(2)}, u32[]{:S(2)}) collective-permute-start(bf16[4,128,128]{2,1,0:T(8,128)(2,1)S(1)} %get-tuple-element.37), channel_id=1, source_target_pairs={{0,8},{8,16},{16,24},{1,9},{9,17},{17,25},{2,10},{10,18},{18,26},{... | collective-permute-start | bytes 393224 | tf_op jit(solution)/shard_map/ppermute | solution.py:130
  8.7 1.3 %collective-permute-start.1 = (bf16[4,128,128]{2,1,0:T(8,128)(2,1)S(1)}, bf16[4,128,128]{2,1,0:T(8,128)(2,1)S(1)}, u32[]{:S(2)}, u32[]{:S(2)}) collective-permute-start(bf16[4,128,128]{2,1,0:T(8,128)(2,1)S(1)} %get-tuple-element.38), channel_id=1, source_target_pairs={{8,0},{16,8},{24,16},{9,1},{17,9},{25,17},{10,2},{18,10},{26,18},{... | collective-permute-start | bytes 393224 | tf_op jit(solution)/shard_map/ppermute | solution.py:131
  10.7 0.1 broadcast_in_dim.46
  10.8 0.1 broadcast_in_dim.47
  10.9 0.9 fusion.18
  11.8 0.1 reduce_min.23
  11.8 0.1 reduce_min.25
  11.9 0.1 multiply_reduce_fusion
  12.0 0.1 stack.8
  12.1 0.1 copy.23
  12.2 0.1 copy.17
  12.3 0.1 copy.20
  12.4 0.1 convolution_convert_fusion
  12.6 0.1 broadcast_in_dim.50
  12.7 0.0 copy-start.10
  12.7 3.4 %pack.1 = bf16[32,72,128]{2,1,0:T(8,128)(2,1)} custom-call(s32[32]{0:T(128)S(1)} %fusion.16.order_ref, f32[2048,128]{1,0:T(8,128)} %obs_ref.2, bf16[32,8,128]{2,1,0:T(8,128)(2,1)S(1)} %pad.8.meta_ref), custom_call_target="tpu_custom_call" | custom-call | bytes 1572864 | tf_op jit(solution)/shard_map/pack/pallas_call | solution.py:518
  16.1 0.0 collective-permute-done.top_ref
  16.1 0.1 collective-permute-done.1.bottom_ref
  16.2 6.9 %all-to-all-start = ((bf16[32,72,128]{2,1,0:T(8,128)(2,1)}), bf16[32,72,128]{2,1,0:T(8,128)(2,1)S(1)}, u32[]{:S(2)}, u32[]{:S(2)}) async-start(bf16[32,72,128]{2,1,0:T(8,128)(2,1)} %pack.1), calls=%async_computation | async-start | bytes 1179648 | tf_op jit(solution)/shard_map/all_to_all | solution.py:523
  23.1 0.0 copy-start.3
  23.1 0.0 copy-start.4
  23.1 3.4 %collective-permute-start.2 = (bf16[24,8,128]{2,1,0:T(8,128)(2,1)S(1)}, bf16[24,8,128]{2,1,0:T(8,128)(2,1)S(1)}, u32[]{:S(2)}, u32[]{:S(2)}) collective-permute-start(bf16[24,8,128]{2,1,0:T(8,128)(2,1)S(1)} %get-tuple-element.44), channel_id=1, source_target_pairs={{1,0},{2,1},{3,2},{4,3},{5,4},{6,5},{7,6},{0,7},{9,8},{10,9},{11,1... | collective-permute-start | bytes 147464 | tf_op jit(solution)/shard_map/ppermute | solution.py:142
  26.6 0.0 collective-permute-start.3
  26.6 0.0 copy-done.10
  26.6 0.2 copy.26
  26.7 1.1 pad.9.clone
  27.9 6.5 %collective-permute-done.2.right_ref = bf16[24,8,128]{2,1,0:T(8,128)(2,1)S(1)} collective-permute-done((bf16[24,8,128]{2,1,0:T(8,128)(2,1)S(1)}, bf16[24,8,128]{2,1,0:T(8,128)(2,1)S(1)}, u32[]{:S(2)}, u32[]{:S(2)}) %collective-permute-start.2) | collective-permute-done | bytes 49184 | tf_op jit(solution)/shard_map/ppermute | solution.py:142
  34.4 3.4 %collective-permute-done.3.left_ref = bf16[24,8,128]{2,1,0:T(8,128)(2,1)S(1)} collective-permute-done((bf16[24,8,128]{2,1,0:T(8,128)(2,1)S(1)}, bf16[24,8,128]{2,1,0:T(8,128)(2,1)S(1)}, u32[]{:S(2)}, u32[]{:S(2)}) %collective-permute-start.3) | collective-permute-done | bytes 49184 | tf_op jit(solution)/shard_map/ppermute | solution.py:141
  37.8 0.0 copy-done.3
  37.8 0.0 copy-done.4
  37.8 0.0 copy-start
  37.8 0.0 copy-start.2
  37.8 0.0 copy-start.6
  37.8 16.0 %forward.1 = (bf16[16,128,128]{2,1,0:T(8,128)(2,1)S(1)}, bf16[22,144,256]{2,1,0:T(8,128)(2,1)}, bf16[20,144,256]{2,1,0:T(8,128)(2,1)}) custom-call(s32[1]{0:T(128)} %bitcast.2.lat_ref, bf16[16,128,128]{2,1,0:T(8,128)(2,1)} %copy-done.1, bf16[4,128,128]{2,1,0:T(8,128)(2,1)S(1)} %collective-permute-done.top_ref, ...), custom_call_target="tpu_custom_call" | custom-call | flops 7247757312 | bytes 4194304 | tf_op jit(solution)/shard_map/forward/pallas_call | solution.py:530
  53.9 0.0 copy-start.8
  53.9 0.8 copy-done.8
  54.6 0.0 all-to-all-done.got_in
  54.7 0.0 copy-start.9
  54.7 0.8 copy-done.9
  55.5 0.0 copy-done
  55.5 0.0 copy-done.2
  55.5 0.0 copy-done.6
  55.5 0.0 copy-start.5
  55.5 19.8 %observe.1 = (f32[16,128,128]{2,1,0:T(8,128)}, bf16[16,128,128]{2,1,0:T(8,128)(2,1)}, bf16[16,8,128]{2,1,0:T(8,128)(2,1)S(1)}, bf16[16,8,128]{2,1,0:T(8,128)(2,1...) custom-call(s32[24,5]{1,0:T(8,128)S(1)} %copy-done.6, ...), custom_call_target="tpu_custom_call" | custom-call | flops 5368709120 | bytes 8388608 | tf_op jit(solution)/shard_map/observe/pallas_call | solution.py:554
  75.3 5.5 %all-to-all-start.1 = ((bf16[32,64,128]{2,1,0:T(8,128)(2,1)}), bf16[32,64,128]{2,1,0:T(8,128)(2,1)S(1)}, u32[]{:S(2)}, u32[]{:S(2)}) async-start(bf16[32,64,128]{2,1,0:T(8,128)(2,1)} %get-tuple-element.49), calls=%async_computation.1 | async-start | bytes 1048576 | tf_op jit(solution)/shard_map/all_to_all | solution.py:575
  80.8 3.7 %collective-permute-start.4 = (bf16[2,128,128]{2,1,0:T(8,128)(2,1)S(1)}, bf16[2,128,128]{2,1,0:T(8,128)(2,1)S(1)}, u32[]{:S(2)}, u32[]{:S(2)}) collective-permute-start(bf16[2,128,128]{2,1,0:T(8,128)(2,1)S(1)} %get-tuple-element.51), channel_id=1, source_target_pairs={{0,8},{8,16},{16,24},{1,9},{9,17},{17,25},{2,10},{10,18},{18,26},{... | collective-permute-start | bytes 196616 | tf_op jit(solution)/shard_map/ppermute | solution.py:130
  84.5 1.3 %collective-permute-start.5 = (bf16[2,128,128]{2,1,0:T(8,128)(2,1)S(1)}, bf16[2,128,128]{2,1,0:T(8,128)(2,1)S(1)}, u32[]{:S(2)}, u32[]{:S(2)}) collective-permute-start(bf16[2,128,128]{2,1,0:T(8,128)(2,1)S(1)} %get-tuple-element.52), channel_id=1, source_target_pairs={{8,0},{16,8},{24,16},{9,1},{17,9},{25,17},{10,2},{18,10},{26,18},{... | collective-permute-start | bytes 196616 | tf_op jit(solution)/shard_map/ppermute | solution.py:131
  85.8 1.3 %collective-permute-done.4.top_ref = bf16[2,128,128]{2,1,0:T(8,128)(2,1)S(1)} collective-permute-done((bf16[2,128,128]{2,1,0:T(8,128)(2,1)S(1)}, bf16[2,128,128]{2,1,0:T(8,128)(2,1)S(1)}, u32[]{:S(2)}, u32[]{:S(2)}) %collective-permute-start.4) | collective-permute-done | bytes 65568 | tf_op jit(solution)/shard_map/ppermute | solution.py:130
  87.1 3.8 %collective-permute-done.5.bottom_ref = bf16[2,128,128]{2,1,0:T(8,128)(2,1)S(1)} collective-permute-done((bf16[2,128,128]{2,1,0:T(8,128)(2,1)S(1)}, bf16[2,128,128]{2,1,0:T(8,128)(2,1)S(1)}, u32[]{:S(2)}, u32[]{:S(2)}) %collective-permute-start.5) | collective-permute-done | bytes 65568 | tf_op jit(solution)/shard_map/ppermute | solution.py:131
  90.9 3.1 %collective-permute-start.6 = (bf16[20,8,128]{2,1,0:T(8,128)(2,1)S(1)}, bf16[20,8,128]{2,1,0:T(8,128)(2,1)S(1)}, u32[]{:S(2)}, u32[]{:S(2)}) collective-permute-start(bf16[20,8,128]{2,1,0:T(8,128)(2,1)S(1)} %get-tuple-element.55), channel_id=1, source_target_pairs={{1,0},{2,1},{3,2},{4,3},{5,4},{6,5},{7,6},{0,7},{9,8},{10,9},{11,1... | collective-permute-start | bytes 122888 | tf_op jit(solution)/shard_map/ppermute | solution.py:142
  94.0 0.0 collective-permute-start.7
  94.0 1.7 %collective-permute-done.6.right_ref = bf16[20,8,128]{2,1,0:T(8,128)(2,1)S(1)} collective-permute-done((bf16[20,8,128]{2,1,0:T(8,128)(2,1)S(1)}, bf16[20,8,128]{2,1,0:T(8,128)(2,1)S(1)}, u32[]{:S(2)}, u32[]{:S(2)}) %collective-permute-start.6) | collective-permute-done | bytes 40992 | tf_op jit(solution)/shard_map/ppermute | solution.py:142
  95.7 3.5 %collective-permute-done.7.left_ref = bf16[20,8,128]{2,1,0:T(8,128)(2,1)S(1)} collective-permute-done((bf16[20,8,128]{2,1,0:T(8,128)(2,1)S(1)}, bf16[20,8,128]{2,1,0:T(8,128)(2,1)S(1)}, u32[]{:S(2)}, u32[]{:S(2)}) %collective-permute-start.7) | collective-permute-done | bytes 40992 | tf_op jit(solution)/shard_map/ppermute | solution.py:141
  99.3 0.0 copy-done.5
  99.3 0.0 copy-start.7
  99.3 1.0 copy-done.7
  100.3 14.2 %adjoint.1 = f32[69,16,128]{2,1,0:T(8,128)} custom-call(s32[1]{0:T(128)} %bitcast.2.lat_ref, bf16[16,128,128]{2,1,0:T(8,128)(2,1)S(1)} %copy-done.7, bf16[2,128,128]{2,1,0:T(8,128)(2,1)S(1)} %collective-permute-done.4.top_ref, bf16[2,128,128]{2,1,0:T(8,128)(2,1)S(1)} %collective-permute-done.5.bottom_ref, ...), custom_call_target="tpu_custom_call" | custom-call | flops 7247757312 | bytes 4194304 | tf_op jit(solution)/shard_map/adjoint/pallas_call | solution.py:579
  114.5 0.0 all-to-all-done.1.got_ref
  114.5 3.8 %unpack.1 = f32[2048,128]{1,0:T(8,128)} custom-call(s32[32]{0:T(128)S(1)} %fusion.16.order_ref, s32[1]{0:T(128)} %copy.28.count_ref, bf16[32,64,128]{2,1,0:T(8,128)(2,1)S(1)} %all-to-all-done.1.got_ref, f32[2048,128]{1,0:T(8,128)} %obs_ref.2, f32[1,128]{1,0:T(1,128)S(1)} %bitcast.22), custom_call_target="tpu_custom_call" | custom-call | bytes 2621440 | tf_op jit(solution)/shard_map/unpack/pallas_call | solution.py:606
  (10 shorter events, 0.2 us)
Async XLA Ops:
  3.1 0.8 copy-start.1
  3.9 12.2 %collective-permute-start = (bf16[4,128,128]{2,1,0:T(8,128)(2,1)S(1)}, bf16[4,128,128]{2,1,0:T(8,128)(2,1)S(1)}, u32[]{:S(2)}, u32[]{:S(2)}) collective-permute-start(bf16[4,128,128]{2,1,0:T(8,128)(2,1)S(1)} %get-tuple-element.37), channel_id=1, source_target_pairs={{0,8},{8,16},{16,24},{1,9},{9,17},{17,25},{2,10},{10,18},{18,26},{... | collective-permute-start | bytes 393224 | tf_op jit(solution)/shard_map/ppermute | solution.py:130
  8.7 7.5 %collective-permute-start.1 = (bf16[4,128,128]{2,1,0:T(8,128)(2,1)S(1)}, bf16[4,128,128]{2,1,0:T(8,128)(2,1)S(1)}, u32[]{:S(2)}, u32[]{:S(2)}) collective-permute-start(bf16[4,128,128]{2,1,0:T(8,128)(2,1)S(1)} %get-tuple-element.38), channel_id=1, source_target_pairs={{8,0},{16,8},{24,16},{9,1},{17,9},{25,17},{10,2},{18,10},{26,18},{... | collective-permute-start | bytes 393224 | tf_op jit(solution)/shard_map/ppermute | solution.py:131
  12.7 13.8 %copy-start.10 = (bf16[4,69,1024]{2,0,1:T(4,128)(2,1)S(1)}, bf16[4,69,1024]{2,0,1:T(4,128)(2,1)}, u32[]{:S(2)}) copy-start(bf16[4,69,1024]{2,0,1:T(4,128)(2,1)} %param.19) | copy-start | bytes 1695748
  16.2 38.4 %all-to-all-start = ((bf16[32,72,128]{2,1,0:T(8,128)(2,1)}), bf16[32,72,128]{2,1,0:T(8,128)(2,1)S(1)}, u32[]{:S(2)}, u32[]{:S(2)}) async-start(bf16[32,72,128]{2,1,0:T(8,128)(2,1)} %pack.1), calls=%async_computation | async-start | bytes 1179648 | tf_op jit(solution)/shard_map/all_to_all | solution.py:523
  23.1 14.7 %copy-start.3 = (bf16[69,256]{1,0:T(8,128)(2,1)S(1)}, bf16[69,256]{1,0:T(8,128)(2,1)}, u32[]{:S(2)}) copy-start(bf16[69,256]{1,0:T(8,128)(2,1)} %enc_in.3) | copy-start | bytes 105988
  23.1 14.6 %copy-start.4 = (bf16[256,69]{0,1:T(8,128)(2,1)S(1)}, bf16[256,69]{0,1:T(8,128)(2,1)}, u32[]{:S(2)}) copy-start(bf16[256,69]{0,1:T(8,128)(2,1)} %param.18) | copy-start | bytes 105988
  23.1 11.2 %collective-permute-start.2 = (bf16[24,8,128]{2,1,0:T(8,128)(2,1)S(1)}, bf16[24,8,128]{2,1,0:T(8,128)(2,1)S(1)}, u32[]{:S(2)}, u32[]{:S(2)}) collective-permute-start(bf16[24,8,128]{2,1,0:T(8,128)(2,1)S(1)} %get-tuple-element.44), channel_id=1, source_target_pairs={{1,0},{2,1},{3,2},{4,3},{5,4},{6,5},{7,6},{0,7},{9,8},{10,9},{11,1... | collective-permute-start | bytes 147464 | tf_op jit(solution)/shard_map/ppermute | solution.py:142
  26.6 11.2 %collective-permute-start.3 = (bf16[24,8,128]{2,1,0:T(8,128)(2,1)S(1)}, bf16[24,8,128]{2,1,0:T(8,128)(2,1)S(1)}, u32[]{:S(2)}, u32[]{:S(2)}) collective-permute-start(bf16[24,8,128]{2,1,0:T(8,128)(2,1)S(1)} %get-tuple-element.45), channel_id=1, source_target_pairs={{0,1},{1,2},{2,3},{3,4},{4,5},{5,6},{6,7},{7,0},{8,9},{9,10},{10,1... | collective-permute-start | bytes 147464 | tf_op jit(solution)/shard_map/ppermute | solution.py:141
  37.8 17.7 %copy-start = (f32[128]{0:T(128)S(1)}, f32[128]{0:T(128)}, u32[]{:S(2)}) copy-start(f32[128]{0:T(128)} %param.22) | copy-start | bytes 1540
  37.8 17.7 %copy-start.2 = (bf16[1024,128]{1,0:T(8,128)(2,1)S(1)}, bf16[1024,128]{1,0:T(8,128)(2,1)}, u32[]{:S(2)}) copy-start(bf16[1024,128]{1,0:T(8,128)(2,1)} %wout_ref.1) | copy-start | bytes 786436
  37.8 17.7 %copy-start.6 = (s32[24,5]{1,0:T(8,128)S(1)}, s32[24,5]{1,0:T(8,128)}, u32[]{:S(2)}) copy-start(s32[24,5]{1,0:T(8,128)} %constant.123.clone.table_ref) | copy-start | bytes 1444
  53.9 0.8 copy-start.8
  54.7 0.8 copy-start.9
  55.5 43.8 %copy-start.5 = (f32[69]{0:T(128)S(1)}, f32[69]{0:T(128)}, u32[]{:S(2)}) copy-start(f32[69]{0:T(128)} %param.15) | copy-start | bytes 832
  75.3 39.2 %all-to-all-start.1 = ((bf16[32,64,128]{2,1,0:T(8,128)(2,1)}), bf16[32,64,128]{2,1,0:T(8,128)(2,1)S(1)}, u32[]{:S(2)}, u32[]{:S(2)}) async-start(bf16[32,64,128]{2,1,0:T(8,128)(2,1)} %get-tuple-element.49), calls=%async_computation.1 | async-start | bytes 1048576 | tf_op jit(solution)/shard_map/all_to_all | solution.py:575
  80.8 6.2 %collective-permute-start.4 = (bf16[2,128,128]{2,1,0:T(8,128)(2,1)S(1)}, bf16[2,128,128]{2,1,0:T(8,128)(2,1)S(1)}, u32[]{:S(2)}, u32[]{:S(2)}) collective-permute-start(bf16[2,128,128]{2,1,0:T(8,128)(2,1)S(1)} %get-tuple-element.51), channel_id=1, source_target_pairs={{0,8},{8,16},{16,24},{1,9},{9,17},{17,25},{2,10},{10,18},{18,26},{... | collective-permute-start | bytes 196616 | tf_op jit(solution)/shard_map/ppermute | solution.py:130
  84.5 6.4 %collective-permute-start.5 = (bf16[2,128,128]{2,1,0:T(8,128)(2,1)S(1)}, bf16[2,128,128]{2,1,0:T(8,128)(2,1)S(1)}, u32[]{:S(2)}, u32[]{:S(2)}) collective-permute-start(bf16[2,128,128]{2,1,0:T(8,128)(2,1)S(1)} %get-tuple-element.52), channel_id=1, source_target_pairs={{8,0},{16,8},{24,16},{9,1},{17,9},{25,17},{10,2},{18,10},{26,18},{... | collective-permute-start | bytes 196616 | tf_op jit(solution)/shard_map/ppermute | solution.py:131
  90.9 4.8 %collective-permute-start.6 = (bf16[20,8,128]{2,1,0:T(8,128)(2,1)S(1)}, bf16[20,8,128]{2,1,0:T(8,128)(2,1)S(1)}, u32[]{:S(2)}, u32[]{:S(2)}) collective-permute-start(bf16[20,8,128]{2,1,0:T(8,128)(2,1)S(1)} %get-tuple-element.55), channel_id=1, source_target_pairs={{1,0},{2,1},{3,2},{4,3},{5,4},{6,5},{7,6},{0,7},{9,8},{10,9},{11,1... | collective-permute-start | bytes 122888 | tf_op jit(solution)/shard_map/ppermute | solution.py:142
  94.0 5.2 %collective-permute-start.7 = (bf16[20,8,128]{2,1,0:T(8,128)(2,1)S(1)}, bf16[20,8,128]{2,1,0:T(8,128)(2,1)S(1)}, u32[]{:S(2)}, u32[]{:S(2)}) collective-permute-start(bf16[20,8,128]{2,1,0:T(8,128)(2,1)S(1)} %get-tuple-element.56), channel_id=1, source_target_pairs={{0,1},{1,2},{2,3},{3,4},{4,5},{5,6},{6,7},{7,0},{8,9},{9,10},{10,1... | collective-permute-start | bytes 122888 | tf_op jit(solution)/shard_map/ppermute | solution.py:141
  99.3 1.0 copy-start.7

commit v3 on v2

--- a/solution.py
+++ b/solution.py
@@ -7,6 +7,7 @@
 from jax.experimental import pallas as pl
 from jax.experimental.pallas import tpu as pltpu
 from jax.sharding import PartitionSpec as P
+
 
 F32 = jnp.float32
 BF16 = jnp.bfloat16
@@ -19,7 +20,7 @@
 SMEM = pltpu.SMEM
 
 
-def call(body, outs, n_in, scratch=(), smem=(), flops=0, moved=0, name=None, limit=53, far=(), far_out=()):
+def call(body, outs, n_in, scratch=(), smem=(), flops=0, moved=0, limit=53, far=(), far_out=()):
     def spec(i, far=far, smem=smem):
         space = SMEM if i in smem else pltpu.HBM if i in far else VMEM
         return pl.BlockSpec(memory_space=space)
@@ -33,7 +34,6 @@
         scratch_shapes=list(scratch),
         cost_estimate=pl.CostEstimate(flops=flops, bytes_accessed=moved, transcendentals=0),
         compiler_params=pltpu.CompilerParams(vmem_limit_bytes=limit * 2**20),
-        name=name,
     )
 
 
@@ -100,7 +100,7 @@
         out_ref[h, 0:per, :] = obs_ref[pl.ds(p, per, stride=tiles), :].astype(BF16)
         return c
 
-    lax.fori_loop(0, tiles, one, 0)
+    lax.fori_loop(0, tiles, one, 0, unroll=8)
     for h in range(tiles):
         out_ref[h, per : per + META, :] = meta_ref[h]
 
@@ -117,7 +117,7 @@
         out_ref[pl.ds(p, per, stride=tiles), :] = jnp.where(slot + p < count_ref[0], dep, 0.0)
         return c
 
-    lax.fori_loop(0, tiles, one, 0)
+    lax.fori_loop(0, tiles, one, 0, unroll=8)
 
 
 def shift_pairs(size, wrap):
@@ -130,7 +130,7 @@
     top = lax.ppermute(tail, "lat", up)
     bottom = lax.ppermute(head, "lat", down)
     shape = (first.shape[0] + 2 * head.shape[0],) + first.shape[1:]
-    near, far = call(sides_body, [(shape, BF16)] * 2, 4, name="sides")(
+    near, far = call(sides_body, [(shape, BF16)] * 2, 4)(
         top, bottom, first, last
     )
     return top, bottom, near, far
@@ -495,7 +495,7 @@
         state_body,
         [((rows, cols, LANES), F32), ((rows, cols, LANES), BF16)]
         + [(strip, BF16)] * 2 + [((HALO, cols, LANES), BF16)] * 2,
-        1, moved=cells * v * 8, name="state",
+        1, moved=cells * v * 8,
     )(analysis_vector)
     foot_cells, obs_sent, *rim = lax.optimization_barrier((foot_cells, obs_values, *rim))
     top, bottom, near, far = halo_rows(*rim)
@@ -516,7 +516,7 @@
     meta = jnp.where(mine[:, None], meta[:, :, None, :], jnp.zeros((), BF16)).reshape(tiles, 3, LANES)
     meta = jnp.pad(meta, ((0, 0), (0, META - 3), (0, 0)))
     (send,) = call(
-        pack_body, [((tiles, per + META, nch), BF16)], 3, smem=(0,), moved=obs_n * nch * 6, name="pack"
+        pack_body, [((tiles, per + META, nch), BF16)], 3, smem=(0,), moved=obs_n * nch * 6
     )(order, obs_sent, meta)
     send, near, far = lax.optimization_barrier((send, near, far))
     right, left = halo_columns(near, far)
@@ -548,7 +548,7 @@
             VMEM((rows + 2 * HALO - 4, width, ch), BF16),
             pltpu.SemaphoreType.DMA((5,)),
         ],
-        (0,), 3 * conv_flops, cells * ch * 8, "forward", far=(6, 8), far_out=(1, 2),
+        (0,), 3 * conv_flops, cells * ch * 8, far=(6, 8), far_out=(1, 2),
     )(lat_id, s16, top, bottom, right, left, at, encoder_weight, w_fwd, rot)
 
     adj, adj16, *rim, pred = call(
@@ -567,7 +567,7 @@
             VMEM(got.shape, BF16),
             pltpu.SemaphoreType.DMA((1,)),
         ],
-        (0,), 4 * cells * hid * (foot * LANES + nch), cells * hid * 4, "observe", far=(2,),
+        (0,), 4 * cells * hid * (foot * LANES + nch), cells * hid * 4, far=(2,),
     )(
         jnp.array(arrangement_table(), jnp.int32), cols16, got, win, obs_out_weight,
         obs_precision[None, :],
@@ -598,13 +598,13 @@
             VMEM((v, rows, cols), F32),
             pltpu.SemaphoreType.DMA((7,)),
         ],
-        (0,), 3 * conv_flops, cells * ch * 8, "adjoint", far=(6, 7, 8, 10, 12, 13),
+        (0,), 3 * conv_flops, cells * ch * 8, far=(6, 7, 8, 10, 12, 13),
     )(
         lat_id, adj16, top, bottom, right, left, adj, slope0, slope1, rot, w_fwd, encoder_weight,
         analysis_vector, prior_estimate, prior_precision[None, :],
     )
     (departures,) = call(
-        unpack_body, [((obs_n, nch), F32)], 5, smem=(0, 1), moved=obs_n * nch * 10, name="unpack"
+        unpack_body, [((obs_n, nch), F32)], 5, smem=(0, 1), moved=obs_n * nch * 10
     )(order, obs_count, back, obs_values, obs_precision[None, :])
     return departures, derivative
 

time: 119 us -> 118 us (level)
  no operation moved by 1% of the time
where the time goes in v3:
time: 118 us; the launch traced here: 117 us
  Pallas kernels  58.8 us (50%)
  starting transfers between devices  29.5 us (25%)
  waiting for transfers between devices  20.9 us (18%)
  local copies, waits for them, and re-layouts  5.54 us (5%)
  between operations  1.52 us (1%)
    pallas_call x1, Pallas kernels, on_device(): call(observe_body, [((rows, cols, LANES), F32), ((rows, cols, LANES), BF1...  19.8 us
    pallas_call x1, Pallas kernels, on_device(): call(functools.partial(forward_body, n_lat), [((rows, cols, LANES), BF16)...  16 us
    pallas_call x1, Pallas kernels, on_device(): call(functools.partial(adjoint_body, n_lat), [((v, rows, cols), F32)], 15...  14.2 us
    ppermute x2, starting transfers between devices, halo_rows(): top = lax.ppermute(tail, 'lat', up)  8.54 us
    ppermute x2, waiting for transfers between devices, halo_columns(): right = lax.ppermute(near, 'lon', down)  8.21 us
    ppermute x2, waiting for transfers between devices, halo_columns(): left = lax.ppermute(far, 'lon', up)  6.93 us
    ppermute x2, starting transfers between devices, halo_columns(): right = lax.ppermute(near, 'lon', down)  6.55 us
    all_to_all x1, starting transfers between devices, on_device(): lax.all_to_all(send, ('lat', 'lon'), split_axis=0, concat_axis=0, tiled=T...  6.3 us
  transfers between devices with their start and end apart: 10, of which 7 were waited for; matrix products, arithmetic and copies ran while one was open for 3% of the time, Pallas kernels for 28%

profile of v3, /device:TPU:0, one launch (start us, length us, event | category | flops | bytes accessed | tf_op | source)
XLA Modules:
  0.0 117.5 jit_solution(14207080634008689923)
XLA Ops:
  0.6 2.4 %shard_map.140 = (f32[16,128,128]{2,1,0:T(8,128)}, bf16[16,128,128]{2,1,0:T(8,128)(2,1)S(1)}, bf16[16,8,128]{2,1,0:T(8,128)(2,1)S(1)}, bf16[16,8,128]{2,1,0:T(8,...) custom-call(f32[69,16,128]{2,1,0:T(8,128)} %state_in.1), custom_call_target="tpu_custom_call" | custom-call | bytes 1130496 | tf_op jit(solution)/shard_map/pallas_call | solution.py:494
  3.1 0.0 copy-start.1
  3.1 0.8 copy-done.1
  3.9 4.9 %collective-permute-start = (bf16[4,128,128]{2,1,0:T(8,128)(2,1)S(1)}, bf16[4,128,128]{2,1,0:T(8,128)(2,1)S(1)}, u32[]{:S(2)}, u32[]{:S(2)}) collective-permute-start(bf16[4,128,128]{2,1,0:T(8,128)(2,1)S(1)} %get-tuple-element.37), channel_id=1, source_target_pairs={{0,8},{8,16},{16,24},{1,9},{9,17},{17,25},{2,10},{10,18},{18,26},{... | collective-permute-start | bytes 393224 | tf_op jit(solution)/shard_map/ppermute | solution.py:130
  8.7 1.3 %collective-permute-start.1 = (bf16[4,128,128]{2,1,0:T(8,128)(2,1)S(1)}, bf16[4,128,128]{2,1,0:T(8,128)(2,1)S(1)}, u32[]{:S(2)}, u32[]{:S(2)}) collective-permute-start(bf16[4,128,128]{2,1,0:T(8,128)(2,1)S(1)} %get-tuple-element.38), channel_id=1, source_target_pairs={{8,0},{16,8},{24,16},{9,1},{17,9},{25,17},{10,2},{18,10},{26,18},{... | collective-permute-start | bytes 393224 | tf_op jit(solution)/shard_map/ppermute | solution.py:131
  10.7 0.1 broadcast_in_dim.46
  10.8 0.1 broadcast_in_dim.47
  10.9 0.9 fusion.18
  11.8 0.1 reduce_min.23
  11.8 0.1 reduce_min.25
  11.9 0.1 multiply_reduce_fusion
  12.0 0.1 stack.8
  12.1 0.1 copy.23
  12.2 0.1 copy.17
  12.3 0.1 copy.20
  12.4 0.1 convolution_convert_fusion
  12.6 0.1 broadcast_in_dim.50
  12.7 0.0 copy-start.10
  12.7 2.8 %shard_map.141 = bf16[32,72,128]{2,1,0:T(8,128)(2,1)} custom-call(s32[32]{0:T(128)S(1)} %fusion.16.order_ref, f32[2048,128]{1,0:T(8,128)} %obs_ref.2, bf16[32,8,128]{2,1,0:T(8,128)(2,1)S(1)} %pad.8.meta_ref), custom_call_target="tpu_custom_call" | custom-call | bytes 1572864 | tf_op jit(solution)/shard_map/pallas_call | solution.py:518
  15.5 0.0 collective-permute-done.top_ref
  15.5 0.7 collective-permute-done.1.bottom_ref
  16.2 6.3 %all-to-all-start = ((bf16[32,72,128]{2,1,0:T(8,128)(2,1)}), bf16[32,72,128]{2,1,0:T(8,128)(2,1)S(1)}, u32[]{:S(2)}, u32[]{:S(2)}) async-start(bf16[32,72,128]{2,1,0:T(8,128)(2,1)} %shard_map.141), calls=%async_computation | async-start | bytes 1179648 | tf_op jit(solution)/shard_map/all_to_all | solution.py:523
  22.5 0.0 copy-start.3
  22.6 0.0 copy-start.4
  22.6 3.4 %collective-permute-start.2 = (bf16[24,8,128]{2,1,0:T(8,128)(2,1)S(1)}, bf16[24,8,128]{2,1,0:T(8,128)(2,1)S(1)}, u32[]{:S(2)}, u32[]{:S(2)}) collective-permute-start(bf16[24,8,128]{2,1,0:T(8,128)(2,1)S(1)} %get-tuple-element.44), channel_id=1, source_target_pairs={{1,0},{2,1},{3,2},{4,3},{5,4},{6,5},{7,6},{0,7},{9,8},{10,9},{11,1... | collective-permute-start | bytes 147464 | tf_op jit(solution)/shard_map/ppermute | solution.py:142
  26.0 0.0 collective-permute-start.3
  26.0 0.0 copy-done.10
  26.0 0.2 copy.26
  26.2 1.1 pad.9.clone
  27.3 6.5 %collective-permute-done.2.right_ref = bf16[24,8,128]{2,1,0:T(8,128)(2,1)S(1)} collective-permute-done((bf16[24,8,128]{2,1,0:T(8,128)(2,1)S(1)}, bf16[24,8,128]{2,1,0:T(8,128)(2,1)S(1)}, u32[]{:S(2)}, u32[]{:S(2)}) %collective-permute-start.2) | collective-permute-done | bytes 49184 | tf_op jit(solution)/shard_map/ppermute | solution.py:142
  33.8 3.4 %collective-permute-done.3.left_ref = bf16[24,8,128]{2,1,0:T(8,128)(2,1)S(1)} collective-permute-done((bf16[24,8,128]{2,1,0:T(8,128)(2,1)S(1)}, bf16[24,8,128]{2,1,0:T(8,128)(2,1)S(1)}, u32[]{:S(2)}, u32[]{:S(2)}) %collective-permute-start.3) | collective-permute-done | bytes 49184 | tf_op jit(solution)/shard_map/ppermute | solution.py:141
  37.2 0.0 copy-done.3
  37.2 0.0 copy-done.4
  37.2 0.0 copy-start
  37.2 0.0 copy-start.2
  37.2 0.0 copy-start.6
  37.2 16.0 %shard_map.143 = (bf16[16,128,128]{2,1,0:T(8,128)(2,1)S(1)}, bf16[22,144,256]{2,1,0:T(8,128)(2,1)}, bf16[20,144,256]{2,1,0:T(8,128)(2,1)}) custom-call(s32[1]{0:T(128)} %bitcast.2.lat_ref, bf16[16,128,128]{2,1,0:T(8,128)(2,1)} %copy-done.1, bf16[4,128,128]{2,1,0:T(8,128)(2,1)S(1)} %collective-permute-done.top_ref, ...), custom_call_target="tpu_custom_call" | custom-call | flops 7247757312 | bytes 4194304 | tf_op jit(solution)/shard_map/pallas_call | solution.py:530
  53.3 0.0 copy-start.8
  53.3 0.8 copy-done.8
  54.1 0.0 all-to-all-done.got_in
  54.1 0.0 copy-start.9
  54.1 0.8 copy-done.9
  54.9 0.0 copy-done
  54.9 0.0 copy-done.2
  54.9 0.0 copy-done.6
  54.9 0.0 copy-start.5
  54.9 19.8 %shard_map.144 = (f32[16,128,128]{2,1,0:T(8,128)}, bf16[16,128,128]{2,1,0:T(8,128)(2,1)}, bf16[16,8,128]{2,1,0:T(8,128)(2,1)S(1)}, bf16[16,8,128]{2,1,0:T(8,128)...) custom-call(s32[24,5]{1,0:T(8,128)S(1)} %copy-done.6, ...), custom_call_target="tpu_custom_call" | custom-call | flops 5368709120 | bytes 8388608 | tf_op jit(solution)/shard_map/pallas_call | solution.py:554
  74.7 5.5 %all-to-all-start.1 = ((bf16[32,64,128]{2,1,0:T(8,128)(2,1)}), bf16[32,64,128]{2,1,0:T(8,128)(2,1)S(1)}, u32[]{:S(2)}, u32[]{:S(2)}) async-start(bf16[32,64,128]{2,1,0:T(8,128)(2,1)} %get-tuple-element.49), calls=%async_computation.1 | async-start | bytes 1048576 | tf_op jit(solution)/shard_map/all_to_all | solution.py:575
  80.2 3.7 %collective-permute-start.4 = (bf16[2,128,128]{2,1,0:T(8,128)(2,1)S(1)}, bf16[2,128,128]{2,1,0:T(8,128)(2,1)S(1)}, u32[]{:S(2)}, u32[]{:S(2)}) collective-permute-start(bf16[2,128,128]{2,1,0:T(8,128)(2,1)S(1)} %get-tuple-element.51), channel_id=1, source_target_pairs={{0,8},{8,16},{16,24},{1,9},{9,17},{17,25},{2,10},{10,18},{18,26},{... | collective-permute-start | bytes 196616 | tf_op jit(solution)/shard_map/ppermute | solution.py:130
  83.9 1.3 %collective-permute-start.5 = (bf16[2,128,128]{2,1,0:T(8,128)(2,1)S(1)}, bf16[2,128,128]{2,1,0:T(8,128)(2,1)S(1)}, u32[]{:S(2)}, u32[]{:S(2)}) collective-permute-start(bf16[2,128,128]{2,1,0:T(8,128)(2,1)S(1)} %get-tuple-element.52), channel_id=1, source_target_pairs={{8,0},{16,8},{24,16},{9,1},{17,9},{25,17},{10,2},{18,10},{26,18},{... | collective-permute-start | bytes 196616 | tf_op jit(solution)/shard_map/ppermute | solution.py:131
  85.2 1.3 %collective-permute-done.4.top_ref = bf16[2,128,128]{2,1,0:T(8,128)(2,1)S(1)} collective-permute-done((bf16[2,128,128]{2,1,0:T(8,128)(2,1)S(1)}, bf16[2,128,128]{2,1,0:T(8,128)(2,1)S(1)}, u32[]{:S(2)}, u32[]{:S(2)}) %collective-permute-start.4) | collective-permute-done | bytes 65568 | tf_op jit(solution)/shard_map/ppermute | solution.py:130
  86.5 3.8 %collective-permute-done.5.bottom_ref = bf16[2,128,128]{2,1,0:T(8,128)(2,1)S(1)} collective-permute-done((bf16[2,128,128]{2,1,0:T(8,128)(2,1)S(1)}, bf16[2,128,128]{2,1,0:T(8,128)(2,1)S(1)}, u32[]{:S(2)}, u32[]{:S(2)}) %collective-permute-start.5) | collective-permute-done | bytes 65568 | tf_op jit(solution)/shard_map/ppermute | solution.py:131
  90.3 3.1 %collective-permute-start.6 = (bf16[20,8,128]{2,1,0:T(8,128)(2,1)S(1)}, bf16[20,8,128]{2,1,0:T(8,128)(2,1)S(1)}, u32[]{:S(2)}, u32[]{:S(2)}) collective-permute-start(bf16[20,8,128]{2,1,0:T(8,128)(2,1)S(1)} %get-tuple-element.55), channel_id=1, source_target_pairs={{1,0},{2,1},{3,2},{4,3},{5,4},{6,5},{7,6},{0,7},{9,8},{10,9},{11,1... | collective-permute-start | bytes 122888 | tf_op jit(solution)/shard_map/ppermute | solution.py:142
  93.5 0.0 collective-permute-start.7
  93.5 1.7 %collective-permute-done.6.right_ref = bf16[20,8,128]{2,1,0:T(8,128)(2,1)S(1)} collective-permute-done((bf16[20,8,128]{2,1,0:T(8,128)(2,1)S(1)}, bf16[20,8,128]{2,1,0:T(8,128)(2,1)S(1)}, u32[]{:S(2)}, u32[]{:S(2)}) %collective-permute-start.6) | collective-permute-done | bytes 40992 | tf_op jit(solution)/shard_map/ppermute | solution.py:142
  95.1 3.5 %collective-permute-done.7.left_ref = bf16[20,8,128]{2,1,0:T(8,128)(2,1)S(1)} collective-permute-done((bf16[20,8,128]{2,1,0:T(8,128)(2,1)S(1)}, bf16[20,8,128]{2,1,0:T(8,128)(2,1)S(1)}, u32[]{:S(2)}, u32[]{:S(2)}) %collective-permute-start.7) | collective-permute-done | bytes 40992 | tf_op jit(solution)/shard_map/ppermute | solution.py:141
  98.7 0.0 copy-done.5
  98.7 0.0 copy-start.7
  98.7 1.0 copy-done.7
  99.7 14.2 %shard_map.147 = f32[69,16,128]{2,1,0:T(8,128)} custom-call(s32[1]{0:T(128)} %bitcast.2.lat_ref, bf16[16,128,128]{2,1,0:T(8,128)(2,1)S(1)} %copy-done.7, bf16[2,128,128]{2,1,0:T(8,128)(2,1)S(1)} %collective-permute-done.4.top_ref, bf16[2,128,128]{2,1,0:T(8,128)(2,1)S(1)} %collective-permute-done.5.bottom_ref, ...), custom_call_target="tpu_custom_call" | custom-call | flops 7247757312 | bytes 4194304 | tf_op jit(solution)/shard_map/pallas_call | solution.py:579
  113.9 0.0 all-to-all-done.1.got_ref
  113.9 3.5 %shard_map.145 = f32[2048,128]{1,0:T(8,128)} custom-call(s32[32]{0:T(128)S(1)} %fusion.16.order_ref, s32[1]{0:T(128)} %copy.28.count_ref, bf16[32,64,128]{2,1,0:T(8,128)(2,1)S(1)} %all-to-all-done.1.got_ref, f32[2048,128]{1,0:T(8,128)} %obs_ref.2, f32[1,128]{1,0:T(1,128)S(1)} %bitcast.22), custom_call_target="tpu_custom_call" | custom-call | bytes 2621440 | tf_op jit(solution)/shard_map/pallas_call | solution.py:606
  (10 shorter events, 0.2 us)
Async XLA Ops:
  3.1 0.8 copy-start.1
  3.9 11.6 %collective-permute-start = (bf16[4,128,128]{2,1,0:T(8,128)(2,1)S(1)}, bf16[4,128,128]{2,1,0:T(8,128)(2,1)S(1)}, u32[]{:S(2)}, u32[]{:S(2)}) collective-permute-start(bf16[4,128,128]{2,1,0:T(8,128)(2,1)S(1)} %get-tuple-element.37), channel_id=1, source_target_pairs={{0,8},{8,16},{16,24},{1,9},{9,17},{17,25},{2,10},{10,18},{18,26},{... | collective-permute-start | bytes 393224 | tf_op jit(solution)/shard_map/ppermute | solution.py:130
  8.7 7.5 %collective-permute-start.1 = (bf16[4,128,128]{2,1,0:T(8,128)(2,1)S(1)}, bf16[4,128,128]{2,1,0:T(8,128)(2,1)S(1)}, u32[]{:S(2)}, u32[]{:S(2)}) collective-permute-start(bf16[4,128,128]{2,1,0:T(8,128)(2,1)S(1)} %get-tuple-element.38), channel_id=1, source_target_pairs={{8,0},{16,8},{24,16},{9,1},{17,9},{25,17},{10,2},{18,10},{26,18},{... | collective-permute-start | bytes 393224 | tf_op jit(solution)/shard_map/ppermute | solution.py:131
  12.7 13.3 %copy-start.10 = (bf16[4,69,1024]{2,0,1:T(4,128)(2,1)S(1)}, bf16[4,69,1024]{2,0,1:T(4,128)(2,1)}, u32[]{:S(2)}) copy-start(bf16[4,69,1024]{2,0,1:T(4,128)(2,1)} %param.19) | copy-start | bytes 1695748
  16.2 37.8 %all-to-all-start = ((bf16[32,72,128]{2,1,0:T(8,128)(2,1)}), bf16[32,72,128]{2,1,0:T(8,128)(2,1)S(1)}, u32[]{:S(2)}, u32[]{:S(2)}) async-start(bf16[32,72,128]{2,1,0:T(8,128)(2,1)} %shard_map.141), calls=%async_computation | async-start | bytes 1179648 | tf_op jit(solution)/shard_map/all_to_all | solution.py:523
  22.5 14.7 %copy-start.3 = (bf16[69,256]{1,0:T(8,128)(2,1)S(1)}, bf16[69,256]{1,0:T(8,128)(2,1)}, u32[]{:S(2)}) copy-start(bf16[69,256]{1,0:T(8,128)(2,1)} %enc_in.3) | copy-start | bytes 105988
  22.6 14.6 %copy-start.4 = (bf16[256,69]{0,1:T(8,128)(2,1)S(1)}, bf16[256,69]{0,1:T(8,128)(2,1)}, u32[]{:S(2)}) copy-start(bf16[256,69]{0,1:T(8,128)(2,1)} %param.18) | copy-start | bytes 105988
  22.6 11.2 %collective-permute-start.2 = (bf16[24,8,128]{2,1,0:T(8,128)(2,1)S(1)}, bf16[24,8,128]{2,1,0:T(8,128)(2,1)S(1)}, u32[]{:S(2)}, u32[]{:S(2)}) collective-permute-start(bf16[24,8,128]{2,1,0:T(8,128)(2,1)S(1)} %get-tuple-element.44), channel_id=1, source_target_pairs={{1,0},{2,1},{3,2},{4,3},{5,4},{6,5},{7,6},{0,7},{9,8},{10,9},{11,1... | collective-permute-start | bytes 147464 | tf_op jit(solution)/shard_map/ppermute | solution.py:142
  26.0 11.2 %collective-permute-start.3 = (bf16[24,8,128]{2,1,0:T(8,128)(2,1)S(1)}, bf16[24,8,128]{2,1,0:T(8,128)(2,1)S(1)}, u32[]{:S(2)}, u32[]{:S(2)}) collective-permute-start(bf16[24,8,128]{2,1,0:T(8,128)(2,1)S(1)} %get-tuple-element.45), channel_id=1, source_target_pairs={{0,1},{1,2},{2,3},{3,4},{4,5},{5,6},{6,7},{7,0},{8,9},{9,10},{10,1... | collective-permute-start | bytes 147464 | tf_op jit(solution)/shard_map/ppermute | solution.py:141
  37.2 17.7 %copy-start = (f32[128]{0:T(128)S(1)}, f32[128]{0:T(128)}, u32[]{:S(2)}) copy-start(f32[128]{0:T(128)} %param.22) | copy-start | bytes 1540
  37.2 17.7 %copy-start.2 = (bf16[1024,128]{1,0:T(8,128)(2,1)S(1)}, bf16[1024,128]{1,0:T(8,128)(2,1)}, u32[]{:S(2)}) copy-start(bf16[1024,128]{1,0:T(8,128)(2,1)} %wout_ref.1) | copy-start | bytes 786436
  37.2 17.7 %copy-start.6 = (s32[24,5]{1,0:T(8,128)S(1)}, s32[24,5]{1,0:T(8,128)}, u32[]{:S(2)}) copy-start(s32[24,5]{1,0:T(8,128)} %constant.123.clone.table_ref) | copy-start | bytes 1444
  53.3 0.8 copy-start.8
  54.1 0.8 copy-start.9
  54.9 43.8 %copy-start.5 = (f32[69]{0:T(128)S(1)}, f32[69]{0:T(128)}, u32[]{:S(2)}) copy-start(f32[69]{0:T(128)} %param.15) | copy-start | bytes 832
  74.7 39.2 %all-to-all-start.1 = ((bf16[32,64,128]{2,1,0:T(8,128)(2,1)}), bf16[32,64,128]{2,1,0:T(8,128)(2,1)S(1)}, u32[]{:S(2)}, u32[]{:S(2)}) async-start(bf16[32,64,128]{2,1,0:T(8,128)(2,1)} %get-tuple-element.49), calls=%async_computation.1 | async-start | bytes 1048576 | tf_op jit(solution)/shard_map/all_to_all | solution.py:575
  80.2 6.2 %collective-permute-start.4 = (bf16[2,128,128]{2,1,0:T(8,128)(2,1)S(1)}, bf16[2,128,128]{2,1,0:T(8,128)(2,1)S(1)}, u32[]{:S(2)}, u32[]{:S(2)}) collective-permute-start(bf16[2,128,128]{2,1,0:T(8,128)(2,1)S(1)} %get-tuple-element.51), channel_id=1, source_target_pairs={{0,8},{8,16},{16,24},{1,9},{9,17},{17,25},{2,10},{10,18},{18,26},{... | collective-permute-start | bytes 196616 | tf_op jit(solution)/shard_map/ppermute | solution.py:130
  83.9 6.4 %collective-permute-start.5 = (bf16[2,128,128]{2,1,0:T(8,128)(2,1)S(1)}, bf16[2,128,128]{2,1,0:T(8,128)(2,1)S(1)}, u32[]{:S(2)}, u32[]{:S(2)}) collective-permute-start(bf16[2,128,128]{2,1,0:T(8,128)(2,1)S(1)} %get-tuple-element.52), channel_id=1, source_target_pairs={{8,0},{16,8},{24,16},{9,1},{17,9},{25,17},{10,2},{18,10},{26,18},{... | collective-permute-start | bytes 196616 | tf_op jit(solution)/shard_map/ppermute | solution.py:131
  90.3 4.8 %collective-permute-start.6 = (bf16[20,8,128]{2,1,0:T(8,128)(2,1)S(1)}, bf16[20,8,128]{2,1,0:T(8,128)(2,1)S(1)}, u32[]{:S(2)}, u32[]{:S(2)}) collective-permute-start(bf16[20,8,128]{2,1,0:T(8,128)(2,1)S(1)} %get-tuple-element.55), channel_id=1, source_target_pairs={{1,0},{2,1},{3,2},{4,3},{5,4},{6,5},{7,6},{0,7},{9,8},{10,9},{11,1... | collective-permute-start | bytes 122888 | tf_op jit(solution)/shard_map/ppermute | solution.py:142
  93.5 5.2 %collective-permute-start.7 = (bf16[20,8,128]{2,1,0:T(8,128)(2,1)S(1)}, bf16[20,8,128]{2,1,0:T(8,128)(2,1)S(1)}, u32[]{:S(2)}, u32[]{:S(2)}) collective-permute-start(bf16[20,8,128]{2,1,0:T(8,128)(2,1)S(1)} %get-tuple-element.56), channel_id=1, source_target_pairs={{0,1},{1,2},{2,3},{3,4},{4,5},{5,6},{6,7},{7,0},{8,9},{9,10},{10,1... | collective-permute-start | bytes 122888 | tf_op jit(solution)/shard_map/ppermute | solution.py:141
  98.7 1.0 copy-start.7

commit v4 on v3

--- a/solution.py
+++ b/solution.py
@@ -16,6 +16,7 @@
 HALO = 4
 BACK = 2
 META = 8
+CHUNK = 32
 VMEM = pltpu.VMEM
 SMEM = pltpu.SMEM
 
@@ -69,15 +70,13 @@
         tail_ref[r - rows + width] = half
 
 
-def state_body(a_ref, at_ref, s_ref, first_ref, last_ref, head_ref, tail_ref):
+def state_body(a_ref, at_ref, first_ref, last_ref, head_ref, tail_ref):
     v, rows, cols = a_ref.shape
     pad = jnp.zeros((LANES - v, cols), F32)
     for r in range(rows):
         x = jnp.concatenate([a_ref[:, r, :], pad], axis=0).T
         at_ref[r] = x
-        half = x.astype(BF16)
-        s_ref[r] = half
-        edges(half, r, rows, HALO, first_ref, last_ref, head_ref, tail_ref)
+        edges(x.astype(BF16), r, rows, HALO, first_ref, last_ref, head_ref, tail_ref)
 
 
 def sides_body(top_ref, bottom_ref, first_ref, last_ref, near_ref, far_ref):
@@ -108,16 +107,33 @@
 def unpack_body(order_ref, count_ref, got_ref, obs_ref, prec_ref, out_ref):
     tiles, per, _ = got_ref.shape
     prec = prec_ref[...]
-    slot = lax.broadcasted_iota(jnp.int32, (per, LANES), 0) * tiles
-
-    def one(p, c):
-        h = order_ref[p]
-        obs = obs_ref[pl.ds(p, per, stride=tiles), :]
-        dep = (got_ref[h].astype(F32) - obs) * prec
-        out_ref[pl.ds(p, per, stride=tiles), :] = jnp.where(slot + p < count_ref[0], dep, 0.0)
-        return c
-
-    lax.fori_loop(0, tiles, one, 0, unroll=8)
+    slot = (lax.broadcasted_iota(jnp.int32, (per, LANES), 0) + pl.program_id(0) * per) * tiles
+    for p in range(tiles):
+        at = pl.ds(p, per, stride=tiles)
+        dep = (got_ref[order_ref[p]].astype(F32) - obs_ref[at, :]) * prec
+        out_ref[at, :] = jnp.where(slot + p < count_ref[0], dep, 0.0)
+
+
+def unpack(order, count, got, obs, prec):
+    tiles, per, nch = got.shape
+    chunk = min(per, CHUNK)
+    rows = pl.BlockSpec((chunk * tiles, nch), lambda k: (k, 0))
+    small = pl.BlockSpec(memory_space=SMEM)
+    return pl.pallas_call(
+        unpack_body,
+        grid=(per // chunk,),
+        out_shape=jax.ShapeDtypeStruct(obs.shape, F32),
+        in_specs=[
+            small,
+            small,
+            pl.BlockSpec((tiles, chunk, nch), lambda k: (0, k, 0)),
+            rows,
+            pl.BlockSpec((1, nch), lambda k: (0, 0)),
+        ],
+        out_specs=rows,
+        compiler_params=pltpu.CompilerParams(vmem_limit_bytes=53 * 2**20),
+        name="unpack",
+    )(order, count, got, obs, prec)
 
 
 def shift_pairs(size, wrap):
@@ -206,19 +222,20 @@
 
 
 def forward_body(
-    n_lat, lat_ref, mid_ref, top_ref, bottom_ref, right_ref, left_ref, at_ref, enc_in, w_ref, ro_in,
+    n_lat, lat_ref, top_ref, bottom_ref, right_ref, left_ref, at_ref, enc_in, w_ref, ro_in,
     cols_ref, slope0_out, slope1_out,
     a0, a1, nat, back, enc_ref, ro_ref, w_v, at_v, slope0_ref, slope1_ref, sem,
 ):
+    at_in = fetch(at_ref, at_v, sem.at[2])
     w0 = fetch(w_ref.at[0], w_v.at[0], sem.at[0])
     w1 = fetch(w_ref.at[1], w_v.at[1], sem.at[1])
-    at_in = fetch(at_ref, at_v, sem.at[2])
     padded(enc_ref, enc_in)
     padded(ro_ref, ro_in)
-    rows, cols, _ = mid_ref.shape
+    rows, cols, _ = at_v.shape
+    at_in.wait()
     q_n = a0.shape[1] - 2
     n = q_n * SUB
-    for e, (src, r) in enumerate(bands(mid_ref, top_ref, bottom_ref, HALO)):
+    for e, (src, r) in enumerate(bands(at_v, top_ref, bottom_ref, HALO)):
         nat[e, 0:cols, :] = src[r].astype(F32)
         nat[e, cols : cols + EDGE, :] = right_ref[e].astype(F32)
         nat[e, cols + EDGE :, :] = left_ref[e].astype(F32)
@@ -258,41 +275,45 @@
         first(e)
     out0 = fetch(slope0_ref, slope0_out, sem.at[3])
     w1.wait()
-    at_in.wait()
-    for e in range(0, rows + 2 * HALO - 4, STEP):
+    half = (rows + 2 * HALO - 4) // 2
+    for e in range(0, half, STEP):
         second(e)
-    out1 = fetch(slope1_ref, slope1_out, sem.at[4])
+    out1 = fetch(slope1_ref.at[0:half], slope1_out.at[0:half], sem.at[4])
+    for e in range(half, 2 * half, STEP):
+        second(e)
+    out2 = fetch(slope1_ref.at[half:], slope1_out.at[half:], sem.at[5])
     out0.wait()
     out1.wait()
+    out2.wait()
 
 
 def adjoint_body(
-    n_lat, lat_ref, mid_ref, top_ref, bottom_ref, right_ref, left_ref, adj_in, slope0_in, slope1_in,
+    n_lat, lat_ref, top_ref, bottom_ref, right_ref, left_ref, adj_in, slope0_in, slope1_in,
     rot_in, w_in, enc_in, state_in, prior_in, prec_in,
     out_ref, b1, b0, adj2, adj1, nat, back, rot_ref, enc_ref, prec_pad,
     adj_ref, slope0_ref, slope1_ref, w_ref, state_ref, prior_ref, sem,
 ):
+    adj_got = fetch(adj_in, adj_ref, sem.at[4])
     slope1_got = fetch(slope1_in, slope1_ref, sem.at[0])
     w1 = fetch(w_in.at[1], w_ref.at[1], sem.at[1])
     slope0_got = fetch(slope0_in, slope0_ref, sem.at[2])
     w0 = fetch(w_in.at[0], w_ref.at[0], sem.at[3])
     late = [
-        fetch(src, dst, sem.at[4 + i])
-        for i, (src, dst) in enumerate(
-            ((adj_in, adj_ref), (state_in, state_ref), (prior_in, prior_ref))
-        )
+        fetch(state_in, state_ref, sem.at[5]),
+        fetch(prior_in, prior_ref, sem.at[6]),
     ]
     padded(rot_ref, rot_in)
     padded(enc_ref, enc_in)
     prec_pad[...] = jnp.zeros_like(prec_pad)
     prec_pad[0:1, 0 : prec_in.shape[1]] = prec_in[...]
-    rows, cols, _ = mid_ref.shape
+    rows, cols, _ = adj_ref.shape
     q_n = b1.shape[1] - 2
     n = q_n * SUB
     v = out_ref.shape[0]
     prec = jnp.broadcast_to(prec_pad[0:1, :], (LANES, LANES)).T[0:v, :]
+    adj_got.wait()
     slope1_got.wait()
-    for e, (src, r) in enumerate(bands(mid_ref, top_ref, bottom_ref, BACK)):
+    for e, (src, r) in enumerate(bands(adj_ref, top_ref, bottom_ref, BACK)):
         nat[e, 0:cols, :] = src[r].astype(F32)
         nat[e, cols : cols + EDGE, :] = right_ref[e].astype(F32)
         nat[e, cols + EDGE :, :] = left_ref[e].astype(F32)
@@ -331,7 +352,7 @@
 
 def observe_body(
     table_ref, cols_ref, got_in, win_ref, wout_ref, prec_ref,
-    adj_ref, half_ref, first_ref, last_ref, head_ref, tail_ref, pred_ref,
+    adj_ref, first_ref, last_ref, head_ref, tail_ref, pred_ref,
     xs, slope, grid, hot, weights, fa, meta, got_ref, sem,
 ):
     got = fetch(got_in, got_ref, sem.at[0])
@@ -378,6 +399,7 @@
         lane = lax.broadcasted_iota(jnp.int32, (LANES, LANES), 1).astype(F32)
         sub = lax.broadcasted_iota(jnp.int32, (LANES, LANES), 0).astype(F32)
         top = float(rows // 2)
+        one16, zero16 = jnp.ones((LANES, LANES), BF16), jnp.zeros((LANES, LANES), BF16)
 
         def gather(m, c):
             mine = meta[m, 2:3, :] == code
@@ -385,9 +407,9 @@
             col = jnp.broadcast_to(meta[m, 1:2, :], (LANES, LANES))
             row_t, col_t = row.T, col.T
             local = jnp.where(row_t < top, row_t, row_t - top)
-            value = jnp.where(col_t == lane, local, -1.0)
+            value = jnp.where(col_t == lane, local, -1.0).astype(BF16)
             sel = jnp.concatenate(
-                [jnp.where(value == float(t), 1.0, 0.0).astype(BF16) for t in range(rows // 2)],
+                [jnp.where(value == jnp.asarray(t, BF16), one16, zero16) for t in range(rows // 2)],
                 axis=1,
             )
             out = dot(sel, both)
@@ -402,23 +424,17 @@
             pred = pred.reshape(group, per, nch)
             where = pl.ds(m * group, group)
 
-            @pl.when(cls == 0)
-            def _():
-                pred_ref[where] = pred.astype(BF16)
-
-            @pl.when(cls > 0)
-            def _():
-                pred_ref[where] = (pred_ref[where].astype(F32) + pred).astype(BF16)
-
+            before = jnp.where(cls > 0, pred_ref[where].astype(F32), 0.0)
+            pred_ref[where] = (before + pred).astype(BF16)
             local = jnp.where(row < top, row, row - top)
-            value = jnp.where(col == sub, local, -1.0)
+            value = jnp.where(col == sub, local, -1.0).astype(BF16)
             for t in range(rows // 2):
                 hot[t * LANES : (t + 1) * LANES, pl.ds(pl.multiple_of(m * LANES, LANES), LANES)] = (
-                    jnp.where(value == float(t), 1.0, 0.0).astype(BF16)
+                    jnp.where(value == jnp.asarray(t, BF16), one16, zero16)
                 )
             return c
 
-        lax.fori_loop(0, obs_n // LANES, gather, 0)
+        lax.fori_loop(0, obs_n // LANES, gather, 0, unroll=4)
 
         def scatter(k, c):
             at = pl.ds(k * BLOCK, BLOCK)
@@ -450,7 +466,6 @@
     total = total.reshape(rows, cols, LANES)
     adj_ref[...] = total
     total = total.astype(BF16)
-    half_ref[...] = total
     for r in range(rows):
         edges(total[r], r, rows, BACK, first_ref, last_ref, head_ref, tail_ref)
 
@@ -491,9 +506,9 @@
     lat_id = lat.reshape(1)
 
     strip = (rows, EDGE, LANES)
-    at, s16, *rim = call(
+    at, *rim = call(
         state_body,
-        [((rows, cols, LANES), F32), ((rows, cols, LANES), BF16)]
+        [((rows, cols, LANES), F32)]
         + [(strip, BF16)] * 2 + [((HALO, cols, LANES), BF16)] * 2,
         1, moved=cells * v * 8,
     )(analysis_vector)
@@ -534,7 +549,7 @@
             ((rows + 2 * HALO - 2, width, ch), BF16),
             ((rows + 2 * HALO - 4, width, ch), BF16),
         ],
-        10,
+        9,
         [
             VMEM((rows + 2 * HALO, width // SUB + 2, SUB, ch), BF16),
             VMEM((rows + 2 * HALO - 2, width // SUB + 2, SUB, ch), BF16),
@@ -546,14 +561,14 @@
             VMEM((rows, cols, LANES), F32),
             VMEM((rows + 2 * HALO - 2, width, ch), BF16),
             VMEM((rows + 2 * HALO - 4, width, ch), BF16),
-            pltpu.SemaphoreType.DMA((5,)),
+            pltpu.SemaphoreType.DMA((6,)),
         ],
-        (0,), 3 * conv_flops, cells * ch * 8, far=(6, 8), far_out=(1, 2),
-    )(lat_id, s16, top, bottom, right, left, at, encoder_weight, w_fwd, rot)
-
-    adj, adj16, *rim, pred = call(
+        (0,), 3 * conv_flops, cells * ch * 8, far=(5, 7), far_out=(1, 2),
+    )(lat_id, top, bottom, right, left, at, encoder_weight, w_fwd, rot)
+
+    adj, *rim, pred = call(
         observe_body,
-        [((rows, cols, LANES), F32), ((rows, cols, LANES), BF16)]
+        [((rows, cols, LANES), F32)]
         + [(strip, BF16)] * 2 + [((BACK, cols, LANES), BF16)] * 2 + [((tiles, per, nch), BF16)],
         6,
         [
@@ -567,7 +582,7 @@
             VMEM(got.shape, BF16),
             pltpu.SemaphoreType.DMA((1,)),
         ],
-        (0,), 4 * cells * hid * (foot * LANES + nch), cells * hid * 4, far=(2,),
+        (0,), 4 * cells * hid * (foot * LANES + nch), cells * hid * 4, limit=50, far=(2,),
     )(
         jnp.array(arrangement_table(), jnp.int32), cols16, got, win, obs_out_weight,
         obs_precision[None, :],
@@ -579,7 +594,7 @@
     (derivative,) = call(
         functools.partial(adjoint_body, n_lat),
         [((v, rows, cols), F32)],
-        15,
+        14,
         [
             VMEM((rows + 2 * BACK, width // SUB + 2, SUB, ch), BF16),
             VMEM((rows + 2, width // SUB + 2, SUB, ch), BF16),
@@ -598,14 +613,12 @@
             VMEM((v, rows, cols), F32),
             pltpu.SemaphoreType.DMA((7,)),
         ],
-        (0,), 3 * conv_flops, cells * ch * 8, far=(6, 7, 8, 10, 12, 13),
+        (0,), 3 * conv_flops, cells * ch * 8, far=(5, 6, 7, 9, 11, 12),
     )(
-        lat_id, adj16, top, bottom, right, left, adj, slope0, slope1, rot, w_fwd, encoder_weight,
+        lat_id, top, bottom, right, left, adj, slope0, slope1, rot, w_fwd, encoder_weight,
         analysis_vector, prior_estimate, prior_precision[None, :],
     )
-    (departures,) = call(
-        unpack_body, [((obs_n, nch), F32)], 5, smem=(0, 1), moved=obs_n * nch * 10
-    )(order, obs_count, back, obs_values, obs_precision[None, :])
+    departures = unpack(order, obs_count, back, obs_values, obs_precision[None, :])
     return departures, derivative
 
 

time: 118 us -> 110 us (0.932)
  Pallas kernels: 58.8 us -> 52.6 us
  local copies, waits for them, and re-layouts: 5.54 us -> 4.12 us
    pallas_call x4, Pallas kernels: 40 us -> 34.8 us  [the longest x1 15.8 us: on_device(): call(observe_body, [((rows, cols, LANES), F32)] + [(strip, BF16)] * 2 + [...]
    unnamed x23 -> x21, local copies, waits for them, and re-layouts: 3.66 us -> 2.23 us
  transfers between devices with their start and end apart: 10 -> 10, of which waited for: 7 -> 7; matrix products, arithmetic and copies ran while one was open for 3% -> 3% of each run, Pallas kernels for 28% -> 29%
where the time goes in v4:
time: 110 us
  Pallas kernels  52.6 us (48%)
  starting transfers between devices  29.5 us (27%)
  waiting for transfers between devices  20.9 us (19%)
  local copies, waits for them, and re-layouts  4.12 us (4%)
  between operations  1.57 us (1%)
    pallas_call x1, Pallas kernels, on_device(): call(observe_body, [((rows, cols, LANES), F32)] + [(strip, BF16)] * 2 + [...  15.8 us
    pallas_call x1, Pallas kernels, on_device(): call(functools.partial(forward_body, n_lat), [((rows, cols, LANES), BF16)...  14.9 us
    pallas_call x1, Pallas kernels, on_device(): call(functools.partial(adjoint_body, n_lat), [((v, rows, cols), F32)], 14...  14.5 us
    ppermute x2, starting transfers between devices, halo_rows(): top = lax.ppermute(tail, 'lat', up)  8.54 us
    ppermute x2, waiting for transfers between devices, halo_columns(): right = lax.ppermute(near, 'lon', down)  8.2 us
    ppermute x2, waiting for transfers between devices, halo_columns(): left = lax.ppermute(far, 'lon', up)  6.93 us
    ppermute x2, starting transfers between devices, halo_columns(): right = lax.ppermute(near, 'lon', down)  6.55 us
    all_to_all x1, starting transfers between devices, on_device(): lax.all_to_all(send, ('lat', 'lon'), split_axis=0, concat_axis=0, tiled=T...  6.29 us
  transfers between devices with their start and end apart: 10, of which 7 were waited for; matrix products, arithmetic and copies ran while one was open for 3% of the time, Pallas kernels for 29%

profile of v4, /device:TPU:0, one launch (start us, length us, event | category | flops | bytes accessed | tf_op | source)
XLA Modules:
  0.0 109.9 jit_solution(1678590958868112467)
XLA Ops:
  0.6 0.0 copy-start
  0.6 1.0 copy-done
  1.7 1.4 %shard_map.140 = (f32[16,128,128]{2,1,0:T(8,128)}, bf16[16,8,128]{2,1,0:T(8,128)(2,1)S(1)}, bf16[16,8,128]{2,1,0:T(8,128)(2,1)S(1)}, bf16[4,128,128]{2,1,0:T(8,128)(2,1)S(1)}, bf16[4,128,128]{2,1,0:T(8,128)(2,1)S(1)}) custom-call(f32[69,16,128]{2,1,0:T(8,128)S(1)} %copy-done), custom_call_target="tpu_custom_call" | custom-call | bytes 1130496 | tf_op jit(solution)/shard_map/pallas_call | solution.py:509
  3.1 4.9 %collective-permute-start = (bf16[4,128,128]{2,1,0:T(8,128)(2,1)S(1)}, bf16[4,128,128]{2,1,0:T(8,128)(2,1)S(1)}, u32[]{:S(2)}, u32[]{:S(2)}) collective-permute-start(bf16[4,128,128]{2,1,0:T(8,128)(2,1)S(1)} %get-tuple-element.34), channel_id=1, source_target_pairs={{0,8},{8,16},{16,24},{1,9},{9,17},{17,25},{2,10},{10,18},{18,26},{... | collective-permute-start | bytes 393224 | tf_op jit(solution)/shard_map/ppermute | solution.py:146
  7.9 1.3 %collective-permute-start.1 = (bf16[4,128,128]{2,1,0:T(8,128)(2,1)S(1)}, bf16[4,128,128]{2,1,0:T(8,128)(2,1)S(1)}, u32[]{:S(2)}, u32[]{:S(2)}) collective-permute-start(bf16[4,128,128]{2,1,0:T(8,128)(2,1)S(1)} %get-tuple-element.35), channel_id=1, source_target_pairs={{8,0},{16,8},{24,16},{9,1},{17,9},{25,17},{10,2},{18,10},{26,18},{... | collective-permute-start | bytes 393224 | tf_op jit(solution)/shard_map/ppermute | solution.py:147
  9.9 0.1 broadcast_in_dim.46
  10.0 0.1 broadcast_in_dim.47
  10.1 0.9 fusion.18
  11.0 0.1 reduce_min.23
  11.0 0.1 reduce_min.25
  11.1 0.1 multiply_reduce_fusion
  11.2 0.1 stack.8
  11.3 0.1 copy.23
  11.4 0.1 copy.17
  11.5 0.1 copy.20
  11.6 0.1 convolution_convert_fusion
  11.8 0.1 broadcast_in_dim.50
  11.9 0.0 copy-start.9
  11.9 2.8 %shard_map.141 = bf16[32,72,128]{2,1,0:T(8,128)(2,1)} custom-call(s32[32]{0:T(128)S(1)} %fusion.16.order_ref, f32[2048,128]{1,0:T(8,128)} %obs_ref.2, bf16[32,8,128]{2,1,0:T(8,128)(2,1)S(1)} %pad.8.meta_ref), custom_call_target="tpu_custom_call" | custom-call | bytes 1572864 | tf_op jit(solution)/shard_map/pallas_call | solution.py:533
  14.7 0.0 collective-permute-done.top_ref
  14.7 0.7 collective-permute-done.1.bottom_ref
  15.4 6.3 %all-to-all-start = ((bf16[32,72,128]{2,1,0:T(8,128)(2,1)}), bf16[32,72,128]{2,1,0:T(8,128)(2,1)S(1)}, u32[]{:S(2)}, u32[]{:S(2)}) async-start(bf16[32,72,128]{2,1,0:T(8,128)(2,1)} %shard_map.141), calls=%async_computation | async-start | bytes 1179648 | tf_op jit(solution)/shard_map/all_to_all | solution.py:538
  21.7 0.0 copy-start.4
  21.7 0.0 copy-start.5
  21.8 3.4 %collective-permute-start.2 = (bf16[24,8,128]{2,1,0:T(8,128)(2,1)S(1)}, bf16[24,8,128]{2,1,0:T(8,128)(2,1)S(1)}, u32[]{:S(2)}, u32[]{:S(2)}) collective-permute-start(bf16[24,8,128]{2,1,0:T(8,128)(2,1)S(1)} %get-tuple-element.41), channel_id=1, source_target_pairs={{1,0},{2,1},{3,2},{4,3},{5,4},{6,5},{7,6},{0,7},{9,8},{10,9},{11,1... | collective-permute-start | bytes 147464 | tf_op jit(solution)/shard_map/ppermute | solution.py:158
  25.2 0.0 collective-permute-start.3
  25.2 0.0 copy-done.9
  25.2 0.2 copy.26
  25.3 1.1 %pad.9.clone = bf16[4,128,1024]{2,1,0:T(8,128)(2,1)} pad(bf16[4,69,1024]{2,1,0:T(8,128)(2,1)S(1)} %copy.26, bf16[]{:T(256)} %constant.122.clone.1), padding=0_0x0_59x0_0 | pad | bytes 1613826 | tf_op jit(solution)/shard_map/jit(_pad)/pad | solution.py:541
  26.5 6.5 %collective-permute-done.2.right_ref = bf16[24,8,128]{2,1,0:T(8,128)(2,1)S(1)} collective-permute-done((bf16[24,8,128]{2,1,0:T(8,128)(2,1)S(1)}, bf16[24,8,128]{2,1,0:T(8,128)(2,1)S(1)}, u32[]{:S(2)}, u32[]{:S(2)}) %collective-permute-start.2) | collective-permute-done | bytes 49184 | tf_op jit(solution)/shard_map/ppermute | solution.py:158
  33.0 3.4 %collective-permute-done.3.left_ref = bf16[24,8,128]{2,1,0:T(8,128)(2,1)S(1)} collective-permute-done((bf16[24,8,128]{2,1,0:T(8,128)(2,1)S(1)}, bf16[24,8,128]{2,1,0:T(8,128)(2,1)S(1)}, u32[]{:S(2)}, u32[]{:S(2)}) %collective-permute-start.3) | collective-permute-done | bytes 49184 | tf_op jit(solution)/shard_map/ppermute | solution.py:157
  36.4 0.0 copy-done.4
  36.4 0.0 copy-done.5
  36.4 0.0 copy-start.2
  36.4 0.0 copy-start.3
  36.4 0.0 copy-start.7
  36.4 14.9 %shard_map.143 = (bf16[16,128,128]{2,1,0:T(8,128)(2,1)S(1)}, bf16[22,144,256]{2,1,0:T(8,128)(2,1)}, bf16[20,144,256]{2,1,0:T(8,128)(2,1)}) custom-call(s32[1]{0:T(128)} %bitcast.2.lat_ref, bf16[4,128,128]{2,1,0:T(8,128)(2,1)S(1)} %collective-permute-done.top_ref, bf16[4,128,128]{2,1,0:T(8,128)(2,1)S(1)} %collective-permute-done.1.bottom_ref, ...), custom_call_target="tpu_custom_call" | custom-call | flops 7247757312 | bytes 4194304 | tf_op jit(solution)/shard_map/pallas_call | solution.py:545
  51.4 0.0 all-to-all-done.got_in
  51.4 0.0 copy-done.2
  51.4 0.0 copy-done.3
  51.4 0.0 copy-done.7
  51.4 0.0 copy-start.1
  51.4 0.0 copy-start.6
  51.4 15.8 %shard_map.144 = (f32[16,128,128]{2,1,0:T(8,128)S(1)}, bf16[16,8,128]{2,1,0:T(8,128)(2,1)S(1)}, bf16[16,8,128]{2,1,0:T(8,128)(2,1)S(1)}, bf16[2,128,128]{2,1,0:T...) custom-call(s32[24,5]{1,0:T(8,128)S(1)} %copy-done.7, ...), custom_call_target="tpu_custom_call" | custom-call | flops 5368709120 | bytes 8388608 | tf_op jit(solution)/shard_map/pallas_call | solution.py:569
  67.2 0.0 copy-start.8
  67.2 1.0 copy-done.8
  68.2 5.5 %all-to-all-start.1 = ((bf16[32,64,128]{2,1,0:T(8,128)(2,1)}), bf16[32,64,128]{2,1,0:T(8,128)(2,1)S(1)}, u32[]{:S(2)}, u32[]{:S(2)}) async-start(bf16[32,64,128]{2,1,0:T(8,128)(2,1)} %get-tuple-element.46), calls=%async_computation.1 | async-start | bytes 1048576 | tf_op jit(solution)/shard_map/all_to_all | solution.py:590
  73.7 3.7 %collective-permute-start.4 = (bf16[2,128,128]{2,1,0:T(8,128)(2,1)S(1)}, bf16[2,128,128]{2,1,0:T(8,128)(2,1)S(1)}, u32[]{:S(2)}, u32[]{:S(2)}) collective-permute-start(bf16[2,128,128]{2,1,0:T(8,128)(2,1)S(1)} %get-tuple-element.47), channel_id=1, source_target_pairs={{0,8},{8,16},{16,24},{1,9},{9,17},{17,25},{2,10},{10,18},{18,26},{... | collective-permute-start | bytes 196616 | tf_op jit(solution)/shard_map/ppermute | solution.py:146
  77.4 1.3 %collective-permute-start.5 = (bf16[2,128,128]{2,1,0:T(8,128)(2,1)S(1)}, bf16[2,128,128]{2,1,0:T(8,128)(2,1)S(1)}, u32[]{:S(2)}, u32[]{:S(2)}) collective-permute-start(bf16[2,128,128]{2,1,0:T(8,128)(2,1)S(1)} %get-tuple-element.48), channel_id=1, source_target_pairs={{8,0},{16,8},{24,16},{9,1},{17,9},{25,17},{10,2},{18,10},{26,18},{... | collective-permute-start | bytes 196616 | tf_op jit(solution)/shard_map/ppermute | solution.py:147
  78.7 1.3 %collective-permute-done.4.top_ref = bf16[2,128,128]{2,1,0:T(8,128)(2,1)S(1)} collective-permute-done((bf16[2,128,128]{2,1,0:T(8,128)(2,1)S(1)}, bf16[2,128,128]{2,1,0:T(8,128)(2,1)S(1)}, u32[]{:S(2)}, u32[]{:S(2)}) %collective-permute-start.4) | collective-permute-done | bytes 65568 | tf_op jit(solution)/shard_map/ppermute | solution.py:146
  80.0 3.8 %collective-permute-done.5.bottom_ref = bf16[2,128,128]{2,1,0:T(8,128)(2,1)S(1)} collective-permute-done((bf16[2,128,128]{2,1,0:T(8,128)(2,1)S(1)}, bf16[2,128,128]{2,1,0:T(8,128)(2,1)S(1)}, u32[]{:S(2)}, u32[]{:S(2)}) %collective-permute-start.5) | collective-permute-done | bytes 65568 | tf_op jit(solution)/shard_map/ppermute | solution.py:147
  83.8 3.1 %collective-permute-start.6 = (bf16[20,8,128]{2,1,0:T(8,128)(2,1)S(1)}, bf16[20,8,128]{2,1,0:T(8,128)(2,1)S(1)}, u32[]{:S(2)}, u32[]{:S(2)}) collective-permute-start(bf16[20,8,128]{2,1,0:T(8,128)(2,1)S(1)} %get-tuple-element.51), channel_id=1, source_target_pairs={{1,0},{2,1},{3,2},{4,3},{5,4},{6,5},{7,6},{0,7},{9,8},{10,9},{11,1... | collective-permute-start | bytes 122888 | tf_op jit(solution)/shard_map/ppermute | solution.py:158
  86.9 0.0 collective-permute-start.7
  86.9 1.7 %collective-permute-done.6.right_ref = bf16[20,8,128]{2,1,0:T(8,128)(2,1)S(1)} collective-permute-done((bf16[20,8,128]{2,1,0:T(8,128)(2,1)S(1)}, bf16[20,8,128]{2,1,0:T(8,128)(2,1)S(1)}, u32[]{:S(2)}, u32[]{:S(2)}) %collective-permute-start.6) | collective-permute-done | bytes 40992 | tf_op jit(solution)/shard_map/ppermute | solution.py:158
  88.6 3.5 %collective-permute-done.7.left_ref = bf16[20,8,128]{2,1,0:T(8,128)(2,1)S(1)} collective-permute-done((bf16[20,8,128]{2,1,0:T(8,128)(2,1)S(1)}, bf16[20,8,128]{2,1,0:T(8,128)(2,1)S(1)}, u32[]{:S(2)}, u32[]{:S(2)}) %collective-permute-start.7) | collective-permute-done | bytes 40992 | tf_op jit(solution)/shard_map/ppermute | solution.py:157
  92.2 0.0 copy-done.1
  92.2 0.0 copy-done.6
  92.2 14.5 %shard_map.146 = f32[69,16,128]{2,1,0:T(8,128)} custom-call(s32[1]{0:T(128)} %bitcast.2.lat_ref, bf16[2,128,128]{2,1,0:T(8,128)(2,1)S(1)} %collective-permute-done.4.top_ref, bf16[2,128,128]{2,1,0:T(8,128)(2,1)S(1)} %collective-permute-done.5.bottom_ref, bf16[20,8,128]{2,1,0:T(8,128)(2,1)S(1)} %collective-permute-done.6.right_ref, ...), custom_call_target="tpu_custom_call" | custom-call | flops 7247757312 | bytes 4194304 | tf_op jit(solution)/shard_map/pallas_call | solution.py:594
  106.7 0.0 all-to-all-done.1.got_ref
  106.7 3.2 %unpack.1 = f32[2048,128]{1,0:T(8,128)} custom-call(s32[32]{0:T(128)S(1)} %fusion.16.order_ref, s32[1]{0:T(128)} %copy.28.count_ref, bf16[32,64,128]{2,1,0:T(8,128)(2,1)S(1)} %all-to-all-done.1.got_ref, f32[2048,128]{1,0:T(8,128)} %obs_ref.2, f32[1,128]{1,0:T(1,128)S(1)} %bitcast.22), custom_call_target="tpu_custom_call" | custom-call | tf_op jit(solution)/shard_map/unpack/pallas_call | solution.py:122
  (10 shorter events, 0.2 us)
Async XLA Ops:
  0.6 1.1 copy-start
  3.1 11.6 %collective-permute-start = (bf16[4,128,128]{2,1,0:T(8,128)(2,1)S(1)}, bf16[4,128,128]{2,1,0:T(8,128)(2,1)S(1)}, u32[]{:S(2)}, u32[]{:S(2)}) collective-permute-start(bf16[4,128,128]{2,1,0:T(8,128)(2,1)S(1)} %get-tuple-element.34), channel_id=1, source_target_pairs={{0,8},{8,16},{16,24},{1,9},{9,17},{17,25},{2,10},{10,18},{18,26},{... | collective-permute-start | bytes 393224 | tf_op jit(solution)/shard_map/ppermute | solution.py:146
  7.9 7.5 %collective-permute-start.1 = (bf16[4,128,128]{2,1,0:T(8,128)(2,1)S(1)}, bf16[4,128,128]{2,1,0:T(8,128)(2,1)S(1)}, u32[]{:S(2)}, u32[]{:S(2)}) collective-permute-start(bf16[4,128,128]{2,1,0:T(8,128)(2,1)S(1)} %get-tuple-element.35), channel_id=1, source_target_pairs={{8,0},{16,8},{24,16},{9,1},{17,9},{25,17},{10,2},{18,10},{26,18},{... | collective-permute-start | bytes 393224 | tf_op jit(solution)/shard_map/ppermute | solution.py:147
  11.9 13.3 %copy-start.9 = (bf16[4,69,1024]{2,0,1:T(4,128)(2,1)S(1)}, bf16[4,69,1024]{2,0,1:T(4,128)(2,1)}, u32[]{:S(2)}) copy-start(bf16[4,69,1024]{2,0,1:T(4,128)(2,1)} %param.19) | copy-start | bytes 1695748
  15.4 35.9 %all-to-all-start = ((bf16[32,72,128]{2,1,0:T(8,128)(2,1)}), bf16[32,72,128]{2,1,0:T(8,128)(2,1)S(1)}, u32[]{:S(2)}, u32[]{:S(2)}) async-start(bf16[32,72,128]{2,1,0:T(8,128)(2,1)} %shard_map.141), calls=%async_computation | async-start | bytes 1179648 | tf_op jit(solution)/shard_map/all_to_all | solution.py:538
  21.7 14.7 %copy-start.4 = (bf16[69,256]{1,0:T(8,128)(2,1)S(1)}, bf16[69,256]{1,0:T(8,128)(2,1)}, u32[]{:S(2)}) copy-start(bf16[69,256]{1,0:T(8,128)(2,1)} %enc_in.3) | copy-start | bytes 105988
  21.7 14.6 %copy-start.5 = (bf16[256,69]{0,1:T(8,128)(2,1)S(1)}, bf16[256,69]{0,1:T(8,128)(2,1)}, u32[]{:S(2)}) copy-start(bf16[256,69]{0,1:T(8,128)(2,1)} %param.18) | copy-start | bytes 105988
  21.8 11.2 %collective-permute-start.2 = (bf16[24,8,128]{2,1,0:T(8,128)(2,1)S(1)}, bf16[24,8,128]{2,1,0:T(8,128)(2,1)S(1)}, u32[]{:S(2)}, u32[]{:S(2)}) collective-permute-start(bf16[24,8,128]{2,1,0:T(8,128)(2,1)S(1)} %get-tuple-element.41), channel_id=1, source_target_pairs={{1,0},{2,1},{3,2},{4,3},{5,4},{6,5},{7,6},{0,7},{9,8},{10,9},{11,1... | collective-permute-start | bytes 147464 | tf_op jit(solution)/shard_map/ppermute | solution.py:158
  25.2 11.2 %collective-permute-start.3 = (bf16[24,8,128]{2,1,0:T(8,128)(2,1)S(1)}, bf16[24,8,128]{2,1,0:T(8,128)(2,1)S(1)}, u32[]{:S(2)}, u32[]{:S(2)}) collective-permute-start(bf16[24,8,128]{2,1,0:T(8,128)(2,1)S(1)} %get-tuple-element.42), channel_id=1, source_target_pairs={{0,1},{1,2},{2,3},{3,4},{4,5},{5,6},{6,7},{7,0},{8,9},{9,10},{10,1... | collective-permute-start | bytes 147464 | tf_op jit(solution)/shard_map/ppermute | solution.py:157
  36.4 15.0 %copy-start.2 = (f32[128]{0:T(128)S(1)}, f32[128]{0:T(128)}, u32[]{:S(2)}) copy-start(f32[128]{0:T(128)} %param.22) | copy-start | bytes 1540
  36.4 15.0 %copy-start.3 = (bf16[1024,128]{1,0:T(8,128)(2,1)S(1)}, bf16[1024,128]{1,0:T(8,128)(2,1)}, u32[]{:S(2)}) copy-start(bf16[1024,128]{1,0:T(8,128)(2,1)} %wout_ref.1) | copy-start | bytes 786436
  36.4 15.0 %copy-start.7 = (s32[24,5]{1,0:T(8,128)S(1)}, s32[24,5]{1,0:T(8,128)}, u32[]{:S(2)}) copy-start(s32[24,5]{1,0:T(8,128)} %constant.123.clone.table_ref) | copy-start | bytes 1444
  51.4 40.7 %copy-start.1 = (f32[69,16,128]{2,1,0:T(8,128)S(1)}, f32[69,16,128]{2,1,0:T(8,128)}, u32[]{:S(2)}) copy-start(f32[69,16,128]{2,1,0:T(8,128)} %state_in.1) | copy-start | bytes 1695748
  51.4 40.7 %copy-start.6 = (f32[69]{0:T(128)S(1)}, f32[69]{0:T(128)}, u32[]{:S(2)}) copy-start(f32[69]{0:T(128)} %param.15) | copy-start | bytes 832
  67.2 1.0 copy-start.8
  68.2 38.5 %all-to-all-start.1 = ((bf16[32,64,128]{2,1,0:T(8,128)(2,1)}), bf16[32,64,128]{2,1,0:T(8,128)(2,1)S(1)}, u32[]{:S(2)}, u32[]{:S(2)}) async-start(bf16[32,64,128]{2,1,0:T(8,128)(2,1)} %get-tuple-element.46), calls=%async_computation.1 | async-start | bytes 1048576 | tf_op jit(solution)/shard_map/all_to_all | solution.py:590
  73.7 6.2 %collective-permute-start.4 = (bf16[2,128,128]{2,1,0:T(8,128)(2,1)S(1)}, bf16[2,128,128]{2,1,0:T(8,128)(2,1)S(1)}, u32[]{:S(2)}, u32[]{:S(2)}) collective-permute-start(bf16[2,128,128]{2,1,0:T(8,128)(2,1)S(1)} %get-tuple-element.47), channel_id=1, source_target_pairs={{0,8},{8,16},{16,24},{1,9},{9,17},{17,25},{2,10},{10,18},{18,26},{... | collective-permute-start | bytes 196616 | tf_op jit(solution)/shard_map/ppermute | solution.py:146
  77.4 6.4 %collective-permute-start.5 = (bf16[2,128,128]{2,1,0:T(8,128)(2,1)S(1)}, bf16[2,128,128]{2,1,0:T(8,128)(2,1)S(1)}, u32[]{:S(2)}, u32[]{:S(2)}) collective-permute-start(bf16[2,128,128]{2,1,0:T(8,128)(2,1)S(1)} %get-tuple-element.48), channel_id=1, source_target_pairs={{8,0},{16,8},{24,16},{9,1},{17,9},{25,17},{10,2},{18,10},{26,18},{... | collective-permute-start | bytes 196616 | tf_op jit(solution)/shard_map/ppermute | solution.py:147
  83.8 4.8 %collective-permute-start.6 = (bf16[20,8,128]{2,1,0:T(8,128)(2,1)S(1)}, bf16[20,8,128]{2,1,0:T(8,128)(2,1)S(1)}, u32[]{:S(2)}, u32[]{:S(2)}) collective-permute-start(bf16[20,8,128]{2,1,0:T(8,128)(2,1)S(1)} %get-tuple-element.51), channel_id=1, source_target_pairs={{1,0},{2,1},{3,2},{4,3},{5,4},{6,5},{7,6},{0,7},{9,8},{10,9},{11,1... | collective-permute-start | bytes 122888 | tf_op jit(solution)/shard_map/ppermute | solution.py:158
  86.9 5.2 %collective-permute-start.7 = (bf16[20,8,128]{2,1,0:T(8,128)(2,1)S(1)}, bf16[20,8,128]{2,1,0:T(8,128)(2,1)S(1)}, u32[]{:S(2)}, u32[]{:S(2)}) collective-permute-start(bf16[20,8,128]{2,1,0:T(8,128)(2,1)S(1)} %get-tuple-element.52), channel_id=1, source_target_pairs={{0,1},{1,2},{2,3},{3,4},{4,5},{5,6},{6,7},{7,0},{8,9},{9,10},{10,1... | collective-permute-start | bytes 122888 | tf_op jit(solution)/shard_map/ppermute | solution.py:157

commit v5 on v4

--- a/solution.py
+++ b/solution.py
@@ -90,13 +90,15 @@
     far_ref[width + rows :] = bottom_ref[:, cols - EDGE :]
 
 
-def pack_body(order_ref, obs_ref, meta_ref, out_ref):
+def pack_body(order_ref, obs_ref, meta_ref, out_ref, kept_ref):
     tiles = out_ref.shape[0]
     per = out_ref.shape[1] - META
 
     def one(p, c):
         h = order_ref[p]
-        out_ref[h, 0:per, :] = obs_ref[pl.ds(p, per, stride=tiles), :].astype(BF16)
+        obs = obs_ref[pl.ds(p, per, stride=tiles), :]
+        kept_ref[h] = obs
+        out_ref[h, 0:per, :] = obs.astype(BF16)
         return c
 
     lax.fori_loop(0, tiles, one, 0, unroll=8)
@@ -110,27 +112,28 @@
     slot = (lax.broadcasted_iota(jnp.int32, (per, LANES), 0) + pl.program_id(0) * per) * tiles
     for p in range(tiles):
         at = pl.ds(p, per, stride=tiles)
-        dep = (got_ref[order_ref[p]].astype(F32) - obs_ref[at, :]) * prec
+        h = order_ref[p]
+        dep = (got_ref[h].astype(F32) - obs_ref[h]) * prec
         out_ref[at, :] = jnp.where(slot + p < count_ref[0], dep, 0.0)
 
 
 def unpack(order, count, got, obs, prec):
     tiles, per, nch = got.shape
     chunk = min(per, CHUNK)
-    rows = pl.BlockSpec((chunk * tiles, nch), lambda k: (k, 0))
+    rows = pl.BlockSpec((tiles, chunk, nch), lambda k: (0, k, 0))
     small = pl.BlockSpec(memory_space=SMEM)
     return pl.pallas_call(
         unpack_body,
         grid=(per // chunk,),
-        out_shape=jax.ShapeDtypeStruct(obs.shape, F32),
+        out_shape=jax.ShapeDtypeStruct((tiles * per, nch), F32),
         in_specs=[
             small,
             small,
-            pl.BlockSpec((tiles, chunk, nch), lambda k: (0, k, 0)),
+            rows,
             rows,
             pl.BlockSpec((1, nch), lambda k: (0, 0)),
         ],
-        out_specs=rows,
+        out_specs=pl.BlockSpec((chunk * tiles, nch), lambda k: (k, 0)),
         compiler_params=pltpu.CompilerParams(vmem_limit_bytes=53 * 2**20),
         name="unpack",
     )(order, count, got, obs, prec)
@@ -351,11 +354,10 @@
 
 
 def observe_body(
-    table_ref, cols_ref, got_in, win_ref, wout_ref, prec_ref,
+    table_ref, cols_ref, got_ref, win_ref, wout_ref, prec_ref,
     adj_ref, first_ref, last_ref, head_ref, tail_ref, pred_ref,
-    xs, slope, grid, hot, weights, fa, meta, got_ref, sem,
+    xs, slope, grid, hot, weights, fa, meta,
 ):
-    got = fetch(got_in, got_ref, sem.at[0])
     rows, cols, _ = cols_ref.shape
     cells = rows * cols
     half = cells // 2
@@ -370,7 +372,6 @@
     xs[2] = jnp.concatenate([c0[cols:], c0[:cols]], axis=0)
     xs[3] = jnp.concatenate([c1[cols:], c1[:cols]], axis=0)
     rest = jnp.zeros((1, LANES), F32)
-    got.wait()
     for m in range(obs_n // LANES):
         total = got_ref[m * group, per : per + META, :].astype(F32)
         for g in range(1, group):
@@ -378,7 +379,6 @@
         meta[m] = total
         rest += jnp.where(total[2:3] == table_ref[0, 4].astype(F32), 0.0, 1.0)
     trips = jnp.where(jnp.sum(rest) > 0.0, table_ref.shape[0], 1)
-    fa[...] = jnp.zeros_like(fa)
 
     def arrangement(cls, carry):
         place = [table_ref[cls, f] for f in range(4)]
@@ -451,7 +451,8 @@
             inner = (act * slope[at, :].astype(F32)).astype(BF16)
             x = dot_t(inner, win_ref[...])
             for f in range(4):
-                fa[place[f], at, :] += x[:, f * LANES : (f + 1) * LANES]
+                before = jnp.where(cls > 0, fa[place[f], at, :], 0.0)
+                fa[place[f], at, :] = before + x[:, f * LANES : (f + 1) * LANES]
             return c
 
         lax.fori_loop(0, cells // BLOCK, backward, 0)
@@ -530,8 +531,8 @@
     mine = jnp.arange(group) == (lat * n_lon + lon) % group
     meta = jnp.where(mine[:, None], meta[:, :, None, :], jnp.zeros((), BF16)).reshape(tiles, 3, LANES)
     meta = jnp.pad(meta, ((0, 0), (0, META - 3), (0, 0)))
-    (send,) = call(
-        pack_body, [((tiles, per + META, nch), BF16)], 3, smem=(0,), moved=obs_n * nch * 6
+    send, kept = call(
+        pack_body, [((tiles, per + META, nch), BF16), ((tiles, per, nch), F32)], 3, smem=(0,), moved=obs_n * nch * 6
     )(order, obs_sent, meta)
     send, near, far = lax.optimization_barrier((send, near, far))
     right, left = halo_columns(near, far)
@@ -579,10 +580,8 @@
             VMEM((obs_n, 2 * nch), BF16),
             VMEM((4, cells, LANES), F32),
             VMEM((obs_n // LANES, META, LANES), F32),
-            VMEM(got.shape, BF16),
-            pltpu.SemaphoreType.DMA((1,)),
         ],
-        (0,), 4 * cells * hid * (foot * LANES + nch), cells * hid * 4, limit=50, far=(2,),
+        (0,), 4 * cells * hid * (foot * LANES + nch), cells * hid * 4, limit=51,
     )(
         jnp.array(arrangement_table(), jnp.int32), cols16, got, win, obs_out_weight,
         obs_precision[None, :],
@@ -618,7 +617,7 @@
         lat_id, top, bottom, right, left, adj, slope0, slope1, rot, w_fwd, encoder_weight,
         analysis_vector, prior_estimate, prior_precision[None, :],
     )
-    departures = unpack(order, obs_count, back, obs_values, obs_precision[None, :])
+    departures = unpack(order, obs_count, back, kept, obs_precision[None, :])
     return departures, derivative
 
 

time: 110 us -> 110 us (level)
    unnamed x21 -> x19, local copies, waits for them, and re-layouts: 2.23 us -> 1.27 us
  transfers between devices with their start and end apart: 10 -> 10, of which waited for: 7 -> 7; matrix products, arithmetic and copies ran while one was open for 3% -> 3% of each run, Pallas kernels for 29% -> 30%
where the time goes in v5:
time: 110 us; the launch traced here: 109 us
  Pallas kernels  53 us (48%)
  starting transfers between devices  29.8 us (27%)
  waiting for transfers between devices  20.6 us (19%)
  local copies, waits for them, and re-layouts  3.13 us (3%)
  between operations  1.55 us (1%)
    pallas_call x1, Pallas kernels, on_device(): call(observe_body, [((rows, cols, LANES), F32)] + [(strip, BF16)] * 2 + [...  16 us
    pallas_call x1, Pallas kernels, on_device(): call(functools.partial(forward_body, n_lat), [((rows, cols, LANES), BF16)...  14.9 us
    pallas_call x1, Pallas kernels, on_device(): call(functools.partial(adjoint_body, n_lat), [((v, rows, cols), F32)], 14...  14.5 us
    ppermute x2, starting transfers between devices, halo_rows(): top = lax.ppermute(tail, 'lat', up)  8.54 us
    ppermute x2, waiting for transfers between devices, halo_columns(): right = lax.ppermute(near, 'lon', down)  8.23 us
    ppermute x2, waiting for transfers between devices, halo_columns(): left = lax.ppermute(far, 'lon', up)  6.93 us
    all_to_all x1, starting transfers between devices, on_device(): lax.all_to_all(send, ('lat', 'lon'), split_axis=0, concat_axis=0, tiled=T...  6.67 us
    ppermute x2, starting transfers between devices, halo_columns(): right = lax.ppermute(near, 'lon', down)  6.55 us
  transfers between devices with their start and end apart: 10, of which 7 were waited for; matrix products, arithmetic and copies ran while one was open for 3% of the time, Pallas kernels for 30%

profile of v5, /device:TPU:0, one launch (start us, length us, event | category | flops | bytes accessed | tf_op | source)
XLA Modules:
  0.0 109.3 jit_solution(12895495881371643248)
XLA Ops:
  0.6 0.0 copy-start
  0.6 1.0 copy-done
  1.7 1.4 %shard_map.140 = (f32[16,128,128]{2,1,0:T(8,128)}, bf16[16,8,128]{2,1,0:T(8,128)(2,1)S(1)}, bf16[16,8,128]{2,1,0:T(8,128)(2,1)S(1)}, bf16[4,128,128]{2,1,0:T(8,128)(2,1)S(1)}, bf16[4,128,128]{2,1,0:T(8,128)(2,1)S(1)}) custom-call(f32[69,16,128]{2,1,0:T(8,128)S(1)} %copy-done), custom_call_target="tpu_custom_call" | custom-call | bytes 1130496 | tf_op jit(solution)/shard_map/pallas_call | solution.py:510
  3.1 4.9 %collective-permute-start = (bf16[4,128,128]{2,1,0:T(8,128)(2,1)S(1)}, bf16[4,128,128]{2,1,0:T(8,128)(2,1)S(1)}, u32[]{:S(2)}, u32[]{:S(2)}) collective-permute-start(bf16[4,128,128]{2,1,0:T(8,128)(2,1)S(1)} %get-tuple-element.36), channel_id=1, source_target_pairs={{0,8},{8,16},{16,24},{1,9},{9,17},{17,25},{2,10},{10,18},{18,26},{... | collective-permute-start | bytes 393224 | tf_op jit(solution)/shard_map/ppermute | solution.py:149
  7.9 1.3 %collective-permute-start.1 = (bf16[4,128,128]{2,1,0:T(8,128)(2,1)S(1)}, bf16[4,128,128]{2,1,0:T(8,128)(2,1)S(1)}, u32[]{:S(2)}, u32[]{:S(2)}) collective-permute-start(bf16[4,128,128]{2,1,0:T(8,128)(2,1)S(1)} %get-tuple-element.37), channel_id=1, source_target_pairs={{8,0},{16,8},{24,16},{9,1},{17,9},{25,17},{10,2},{18,10},{26,18},{... | collective-permute-start | bytes 393224 | tf_op jit(solution)/shard_map/ppermute | solution.py:150
  9.9 0.1 broadcast_in_dim.46
  10.0 0.1 broadcast_in_dim.47
  10.1 0.9 fusion.18
  11.0 0.1 reduce_min.23
  11.0 0.1 reduce_min.25
  11.1 0.1 multiply_reduce_fusion
  11.2 0.0 copy-start.8
  11.3 0.1 stack.8
  11.3 0.1 copy.23
  11.4 0.1 copy.17
  11.5 0.1 copy.20
  11.6 0.1 convolution_convert_fusion
  11.8 0.1 broadcast_in_dim.50
  11.9 3.1 %shard_map.141 = (bf16[32,72,128]{2,1,0:T(8,128)(2,1)}, f32[32,64,128]{2,1,0:T(8,128)}) custom-call(s32[32]{0:T(128)S(1)} %fusion.16.order_ref, f32[2048,128]{1,0:T(8,128)} %obs_ref, bf16[32,8,128]{2,1,0:T(8,128)(2,1)S(1)} %pad.8.meta_ref), custom_call_target="tpu_custom_call" | custom-call | bytes 1572864 | tf_op jit(solution)/shard_map/pallas_call | solution.py:534
  15.1 0.0 collective-permute-done.top_ref
  15.1 0.3 collective-permute-done.1.bottom_ref
  15.4 6.7 %all-to-all-start = ((bf16[32,72,128]{2,1,0:T(8,128)(2,1)}), bf16[32,72,128]{2,1,0:T(8,128)(2,1)S(1)}, u32[]{:S(2)}, u32[]{:S(2)}) async-start(bf16[32,72,128]{2,1,0:T(8,128)(2,1)} %get-tuple-element.48), calls=%async_computation | async-start | bytes 1179648 | tf_op jit(solution)/shard_map/all_to_all | solution.py:539
  22.1 0.0 copy-start.4
  22.1 0.0 copy-start.5
  22.1 3.4 %collective-permute-start.2 = (bf16[24,8,128]{2,1,0:T(8,128)(2,1)S(1)}, bf16[24,8,128]{2,1,0:T(8,128)(2,1)S(1)}, u32[]{:S(2)}, u32[]{:S(2)}) collective-permute-start(bf16[24,8,128]{2,1,0:T(8,128)(2,1)S(1)} %get-tuple-element.44), channel_id=1, source_target_pairs={{1,0},{2,1},{3,2},{4,3},{5,4},{6,5},{7,6},{0,7},{9,8},{10,9},{11,1... | collective-permute-start | bytes 147464 | tf_op jit(solution)/shard_map/ppermute | solution.py:161
  25.5 0.0 collective-permute-start.3
  25.5 0.0 copy-done.8
  25.5 0.2 copy.26
  25.7 1.1 %pad.9.clone = bf16[4,128,1024]{2,1,0:T(8,128)(2,1)} pad(bf16[4,69,1024]{2,1,0:T(8,128)(2,1)S(1)} %copy.26, bf16[]{:T(256)} %constant.122.clone.1), padding=0_0x0_59x0_0 | pad | bytes 1613826 | tf_op jit(solution)/shard_map/jit(_pad)/pad | solution.py:542
  26.8 6.6 %collective-permute-done.2.right_ref = bf16[24,8,128]{2,1,0:T(8,128)(2,1)S(1)} collective-permute-done((bf16[24,8,128]{2,1,0:T(8,128)(2,1)S(1)}, bf16[24,8,128]{2,1,0:T(8,128)(2,1)S(1)}, u32[]{:S(2)}, u32[]{:S(2)}) %collective-permute-start.2) | collective-permute-done | bytes 49184 | tf_op jit(solution)/shard_map/ppermute | solution.py:161
  33.4 3.4 %collective-permute-done.3.left_ref = bf16[24,8,128]{2,1,0:T(8,128)(2,1)S(1)} collective-permute-done((bf16[24,8,128]{2,1,0:T(8,128)(2,1)S(1)}, bf16[24,8,128]{2,1,0:T(8,128)(2,1)S(1)}, u32[]{:S(2)}, u32[]{:S(2)}) %collective-permute-start.3) | collective-permute-done | bytes 49184 | tf_op jit(solution)/shard_map/ppermute | solution.py:160
  36.8 0.0 copy-done.4
  36.8 0.0 copy-done.5
  36.8 0.0 copy-start.2
  36.8 0.0 copy-start.3
  36.8 0.0 copy-start.7
  36.8 14.9 %shard_map.143 = (bf16[16,128,128]{2,1,0:T(8,128)(2,1)S(1)}, bf16[22,144,256]{2,1,0:T(8,128)(2,1)}, bf16[20,144,256]{2,1,0:T(8,128)(2,1)}) custom-call(s32[1]{0:T(128)} %bitcast.2.lat_ref, bf16[4,128,128]{2,1,0:T(8,128)(2,1)S(1)} %collective-permute-done.top_ref, bf16[4,128,128]{2,1,0:T(8,128)(2,1)S(1)} %collective-permute-done.1.bottom_ref, ...), custom_call_target="tpu_custom_call" | custom-call | flops 7247757312 | bytes 4194304 | tf_op jit(solution)/shard_map/pallas_call | solution.py:546
  51.7 0.0 all-to-all-done.got_ref
  51.8 0.0 copy-done.2
  51.8 0.0 copy-done.3
  51.8 0.0 copy-done.7
  51.8 0.0 copy-start.1
  51.8 0.0 copy-start.6
  51.8 16.0 %shard_map.144 = (f32[16,128,128]{2,1,0:T(8,128)}, bf16[16,8,128]{2,1,0:T(8,128)(2,1)S(1)}, bf16[16,8,128]{2,1,0:T(8,128)(2,1)S(1)}, bf16[2,128,128]{2,1,0:T(8,1...) custom-call(s32[24,5]{1,0:T(8,128)S(1)} %copy-done.7, ...), custom_call_target="tpu_custom_call" | custom-call | flops 5368709120 | bytes 8388608 | tf_op jit(solution)/shard_map/pallas_call | solution.py:570
  67.8 5.5 %all-to-all-start.1 = ((bf16[32,64,128]{2,1,0:T(8,128)(2,1)}), bf16[32,64,128]{2,1,0:T(8,128)(2,1)S(1)}, u32[]{:S(2)}, u32[]{:S(2)}) async-start(bf16[32,64,128]{2,1,0:T(8,128)(2,1)} %get-tuple-element.49), calls=%async_computation.1 | async-start | bytes 1048576 | tf_op jit(solution)/shard_map/all_to_all | solution.py:589
  73.3 3.7 %collective-permute-start.4 = (bf16[2,128,128]{2,1,0:T(8,128)(2,1)S(1)}, bf16[2,128,128]{2,1,0:T(8,128)(2,1)S(1)}, u32[]{:S(2)}, u32[]{:S(2)}) collective-permute-start(bf16[2,128,128]{2,1,0:T(8,128)(2,1)S(1)} %get-tuple-element.51), channel_id=1, source_target_pairs={{0,8},{8,16},{16,24},{1,9},{9,17},{17,25},{2,10},{10,18},{18,26},{... | collective-permute-start | bytes 196616 | tf_op jit(solution)/shard_map/ppermute | solution.py:149
  77.0 1.3 %collective-permute-start.5 = (bf16[2,128,128]{2,1,0:T(8,128)(2,1)S(1)}, bf16[2,128,128]{2,1,0:T(8,128)(2,1)S(1)}, u32[]{:S(2)}, u32[]{:S(2)}) collective-permute-start(bf16[2,128,128]{2,1,0:T(8,128)(2,1)S(1)} %get-tuple-element.52), channel_id=1, source_target_pairs={{8,0},{16,8},{24,16},{9,1},{17,9},{25,17},{10,2},{18,10},{26,18},{... | collective-permute-start | bytes 196616 | tf_op jit(solution)/shard_map/ppermute | solution.py:150
  78.3 1.3 %collective-permute-done.4.top_ref = bf16[2,128,128]{2,1,0:T(8,128)(2,1)S(1)} collective-permute-done((bf16[2,128,128]{2,1,0:T(8,128)(2,1)S(1)}, bf16[2,128,128]{2,1,0:T(8,128)(2,1)S(1)}, u32[]{:S(2)}, u32[]{:S(2)}) %collective-permute-start.4) | collective-permute-done | bytes 65568 | tf_op jit(solution)/shard_map/ppermute | solution.py:149
  79.6 3.8 %collective-permute-done.5.bottom_ref = bf16[2,128,128]{2,1,0:T(8,128)(2,1)S(1)} collective-permute-done((bf16[2,128,128]{2,1,0:T(8,128)(2,1)S(1)}, bf16[2,128,128]{2,1,0:T(8,128)(2,1)S(1)}, u32[]{:S(2)}, u32[]{:S(2)}) %collective-permute-start.5) | collective-permute-done | bytes 65568 | tf_op jit(solution)/shard_map/ppermute | solution.py:150
  83.4 3.1 %collective-permute-start.6 = (bf16[20,8,128]{2,1,0:T(8,128)(2,1)S(1)}, bf16[20,8,128]{2,1,0:T(8,128)(2,1)S(1)}, u32[]{:S(2)}, u32[]{:S(2)}) collective-permute-start(bf16[20,8,128]{2,1,0:T(8,128)(2,1)S(1)} %get-tuple-element.55), channel_id=1, source_target_pairs={{1,0},{2,1},{3,2},{4,3},{5,4},{6,5},{7,6},{0,7},{9,8},{10,9},{11,1... | collective-permute-start | bytes 122888 | tf_op jit(solution)/shard_map/ppermute | solution.py:161
  86.6 0.0 collective-permute-start.7
  86.6 1.7 %collective-permute-done.6.right_ref = bf16[20,8,128]{2,1,0:T(8,128)(2,1)S(1)} collective-permute-done((bf16[20,8,128]{2,1,0:T(8,128)(2,1)S(1)}, bf16[20,8,128]{2,1,0:T(8,128)(2,1)S(1)}, u32[]{:S(2)}, u32[]{:S(2)}) %collective-permute-start.6) | collective-permute-done | bytes 40992 | tf_op jit(solution)/shard_map/ppermute | solution.py:161
  88.2 3.5 %collective-permute-done.7.left_ref = bf16[20,8,128]{2,1,0:T(8,128)(2,1)S(1)} collective-permute-done((bf16[20,8,128]{2,1,0:T(8,128)(2,1)S(1)}, bf16[20,8,128]{2,1,0:T(8,128)(2,1)S(1)}, u32[]{:S(2)}, u32[]{:S(2)}) %collective-permute-start.7) | collective-permute-done | bytes 40992 | tf_op jit(solution)/shard_map/ppermute | solution.py:160
  91.8 0.0 copy-done.1
  91.8 0.0 copy-done.6
  91.8 14.5 %shard_map.146 = f32[69,16,128]{2,1,0:T(8,128)} custom-call(s32[1]{0:T(128)} %bitcast.2.lat_ref, bf16[2,128,128]{2,1,0:T(8,128)(2,1)S(1)} %collective-permute-done.4.top_ref, bf16[2,128,128]{2,1,0:T(8,128)(2,1)S(1)} %collective-permute-done.5.bottom_ref, bf16[20,8,128]{2,1,0:T(8,128)(2,1)S(1)} %collective-permute-done.6.right_ref, ...), custom_call_target="tpu_custom_call" | custom-call | flops 7247757312 | bytes 4194304 | tf_op jit(solution)/shard_map/pallas_call | solution.py:593
  106.3 0.0 all-to-all-done.1.got_ref
  106.3 3.0 %unpack.1 = f32[2048,128]{1,0:T(8,128)} custom-call(s32[32]{0:T(128)S(1)} %fusion.16.order_ref, s32[1]{0:T(128)} %copy.28.count_ref, bf16[32,64,128]{2,1,0:T(8,128)(2,1)S(1)} %all-to-all-done.1.got_ref, f32[32,64,128]{2,1,0:T(8,128)} %get-tuple-element.50.obs_ref, f32[1,128]{1,0:T(1,128)S(1)} %bitcast.22), custom_call_target="tpu_custom_call" | custom-call | tf_op jit(solution)/shard_map/unpack/pallas_call | solution.py:125
  (10 shorter events, 0.2 us)
Async XLA Ops:
  0.6 1.1 copy-start
  3.1 12.0 %collective-permute-start = (bf16[4,128,128]{2,1,0:T(8,128)(2,1)S(1)}, bf16[4,128,128]{2,1,0:T(8,128)(2,1)S(1)}, u32[]{:S(2)}, u32[]{:S(2)}) collective-permute-start(bf16[4,128,128]{2,1,0:T(8,128)(2,1)S(1)} %get-tuple-element.36), channel_id=1, source_target_pairs={{0,8},{8,16},{16,24},{1,9},{9,17},{17,25},{2,10},{10,18},{18,26},{... | collective-permute-start | bytes 393224 | tf_op jit(solution)/shard_map/ppermute | solution.py:149
  7.9 7.5 %collective-permute-start.1 = (bf16[4,128,128]{2,1,0:T(8,128)(2,1)S(1)}, bf16[4,128,128]{2,1,0:T(8,128)(2,1)S(1)}, u32[]{:S(2)}, u32[]{:S(2)}) collective-permute-start(bf16[4,128,128]{2,1,0:T(8,128)(2,1)S(1)} %get-tuple-element.37), channel_id=1, source_target_pairs={{8,0},{16,8},{24,16},{9,1},{17,9},{25,17},{10,2},{18,10},{26,18},{... | collective-permute-start | bytes 393224 | tf_op jit(solution)/shard_map/ppermute | solution.py:150
  11.2 14.3 %copy-start.8 = (bf16[4,69,1024]{2,0,1:T(4,128)(2,1)S(1)}, bf16[4,69,1024]{2,0,1:T(4,128)(2,1)}, u32[]{:S(2)}) copy-start(bf16[4,69,1024]{2,0,1:T(4,128)(2,1)} %param.19) | copy-start | bytes 1695748
  15.4 36.3 %all-to-all-start = ((bf16[32,72,128]{2,1,0:T(8,128)(2,1)}), bf16[32,72,128]{2,1,0:T(8,128)(2,1)S(1)}, u32[]{:S(2)}, u32[]{:S(2)}) async-start(bf16[32,72,128]{2,1,0:T(8,128)(2,1)} %get-tuple-element.48), calls=%async_computation | async-start | bytes 1179648 | tf_op jit(solution)/shard_map/all_to_all | solution.py:539
  22.1 14.7 %copy-start.4 = (bf16[69,256]{1,0:T(8,128)(2,1)S(1)}, bf16[69,256]{1,0:T(8,128)(2,1)}, u32[]{:S(2)}) copy-start(bf16[69,256]{1,0:T(8,128)(2,1)} %enc_in.3) | copy-start | bytes 105988
  22.1 14.6 %copy-start.5 = (bf16[256,69]{0,1:T(8,128)(2,1)S(1)}, bf16[256,69]{0,1:T(8,128)(2,1)}, u32[]{:S(2)}) copy-start(bf16[256,69]{0,1:T(8,128)(2,1)} %param.18) | copy-start | bytes 105988
  22.1 11.2 %collective-permute-start.2 = (bf16[24,8,128]{2,1,0:T(8,128)(2,1)S(1)}, bf16[24,8,128]{2,1,0:T(8,128)(2,1)S(1)}, u32[]{:S(2)}, u32[]{:S(2)}) collective-permute-start(bf16[24,8,128]{2,1,0:T(8,128)(2,1)S(1)} %get-tuple-element.44), channel_id=1, source_target_pairs={{1,0},{2,1},{3,2},{4,3},{5,4},{6,5},{7,6},{0,7},{9,8},{10,9},{11,1... | collective-permute-start | bytes 147464 | tf_op jit(solution)/shard_map/ppermute | solution.py:161
  25.5 11.2 %collective-permute-start.3 = (bf16[24,8,128]{2,1,0:T(8,128)(2,1)S(1)}, bf16[24,8,128]{2,1,0:T(8,128)(2,1)S(1)}, u32[]{:S(2)}, u32[]{:S(2)}) collective-permute-start(bf16[24,8,128]{2,1,0:T(8,128)(2,1)S(1)} %get-tuple-element.45), channel_id=1, source_target_pairs={{0,1},{1,2},{2,3},{3,4},{4,5},{5,6},{6,7},{7,0},{8,9},{9,10},{10,1... | collective-permute-start | bytes 147464 | tf_op jit(solution)/shard_map/ppermute | solution.py:160
  36.8 15.0 %copy-start.2 = (f32[128]{0:T(128)S(1)}, f32[128]{0:T(128)}, u32[]{:S(2)}) copy-start(f32[128]{0:T(128)} %param.22) | copy-start | bytes 1540
  36.8 15.0 %copy-start.3 = (bf16[1024,128]{1,0:T(8,128)(2,1)S(1)}, bf16[1024,128]{1,0:T(8,128)(2,1)}, u32[]{:S(2)}) copy-start(bf16[1024,128]{1,0:T(8,128)(2,1)} %wout_ref.1) | copy-start | bytes 786436
  36.8 15.0 %copy-start.7 = (s32[24,5]{1,0:T(8,128)S(1)}, s32[24,5]{1,0:T(8,128)}, u32[]{:S(2)}) copy-start(s32[24,5]{1,0:T(8,128)} %constant.123.clone.table_ref) | copy-start | bytes 1444
  51.8 40.0 %copy-start.1 = (f32[69,16,128]{2,1,0:T(8,128)S(1)}, f32[69,16,128]{2,1,0:T(8,128)}, u32[]{:S(2)}) copy-start(f32[69,16,128]{2,1,0:T(8,128)} %state_in.1) | copy-start | bytes 1695748
  51.8 40.0 %copy-start.6 = (f32[69]{0:T(128)S(1)}, f32[69]{0:T(128)}, u32[]{:S(2)}) copy-start(f32[69]{0:T(128)} %param.15) | copy-start | bytes 832
  67.8 38.5 %all-to-all-start.1 = ((bf16[32,64,128]{2,1,0:T(8,128)(2,1)}), bf16[32,64,128]{2,1,0:T(8,128)(2,1)S(1)}, u32[]{:S(2)}, u32[]{:S(2)}) async-start(bf16[32,64,128]{2,1,0:T(8,128)(2,1)} %get-tuple-element.49), calls=%async_computation.1 | async-start | bytes 1048576 | tf_op jit(solution)/shard_map/all_to_all | solution.py:589
  73.3 6.2 %collective-permute-start.4 = (bf16[2,128,128]{2,1,0:T(8,128)(2,1)S(1)}, bf16[2,128,128]{2,1,0:T(8,128)(2,1)S(1)}, u32[]{:S(2)}, u32[]{:S(2)}) collective-permute-start(bf16[2,128,128]{2,1,0:T(8,128)(2,1)S(1)} %get-tuple-element.51), channel_id=1, source_target_pairs={{0,8},{8,16},{16,24},{1,9},{9,17},{17,25},{2,10},{10,18},{18,26},{... | collective-permute-start | bytes 196616 | tf_op jit(solution)/shard_map/ppermute | solution.py:149
  77.0 6.4 %collective-permute-start.5 = (bf16[2,128,128]{2,1,0:T(8,128)(2,1)S(1)}, bf16[2,128,128]{2,1,0:T(8,128)(2,1)S(1)}, u32[]{:S(2)}, u32[]{:S(2)}) collective-permute-start(bf16[2,128,128]{2,1,0:T(8,128)(2,1)S(1)} %get-tuple-element.52), channel_id=1, source_target_pairs={{8,0},{16,8},{24,16},{9,1},{17,9},{25,17},{10,2},{18,10},{26,18},{... | collective-permute-start | bytes 196616 | tf_op jit(solution)/shard_map/ppermute | solution.py:150
  83.4 4.8 %collective-permute-start.6 = (bf16[20,8,128]{2,1,0:T(8,128)(2,1)S(1)}, bf16[20,8,128]{2,1,0:T(8,128)(2,1)S(1)}, u32[]{:S(2)}, u32[]{:S(2)}) collective-permute-start(bf16[20,8,128]{2,1,0:T(8,128)(2,1)S(1)} %get-tuple-element.55), channel_id=1, source_target_pairs={{1,0},{2,1},{3,2},{4,3},{5,4},{6,5},{7,6},{0,7},{9,8},{10,9},{11,1... | collective-permute-start | bytes 122888 | tf_op jit(solution)/shard_map/ppermute | solution.py:161
  86.6 5.2 %collective-permute-start.7 = (bf16[20,8,128]{2,1,0:T(8,128)(2,1)S(1)}, bf16[20,8,128]{2,1,0:T(8,128)(2,1)S(1)}, u32[]{:S(2)}, u32[]{:S(2)}) collective-permute-start(bf16[20,8,128]{2,1,0:T(8,128)(2,1)S(1)} %get-tuple-element.56), channel_id=1, source_target_pairs={{0,1},{1,2},{2,3},{3,4},{4,5},{5,6},{6,7},{7,0},{8,9},{9,10},{10,1... | collective-permute-start | bytes 122888 | tf_op jit(solution)/shard_map/ppermute | solution.py:160

commit v6 on v5

--- a/solution.py
+++ b/solution.py
@@ -16,7 +16,8 @@
 HALO = 4
 BACK = 2
 META = 8
-CHUNK = 32
+CHUNK = 16
+UNPACK = 50
 VMEM = pltpu.VMEM
 SMEM = pltpu.SMEM
 
@@ -106,37 +107,25 @@
         out_ref[h, per : per + META, :] = meta_ref[h]
 
 
-def unpack_body(order_ref, count_ref, got_ref, obs_ref, prec_ref, out_ref):
+def unpack_body(order_ref, count_ref, got_ref, obs_ref, prec_ref, out_ref, out_v, sem):
     tiles, per, _ = got_ref.shape
+    chunk = min(per, CHUNK)
     prec = prec_ref[...]
-    slot = (lax.broadcasted_iota(jnp.int32, (per, LANES), 0) + pl.program_id(0) * per) * tiles
-    for p in range(tiles):
-        at = pl.ds(p, per, stride=tiles)
-        h = order_ref[p]
-        dep = (got_ref[h].astype(F32) - obs_ref[h]) * prec
-        out_ref[at, :] = jnp.where(slot + p < count_ref[0], dep, 0.0)
-
-
-def unpack(order, count, got, obs, prec):
-    tiles, per, nch = got.shape
-    chunk = min(per, CHUNK)
-    rows = pl.BlockSpec((tiles, chunk, nch), lambda k: (0, k, 0))
-    small = pl.BlockSpec(memory_space=SMEM)
-    return pl.pallas_call(
-        unpack_body,
-        grid=(per // chunk,),
-        out_shape=jax.ShapeDtypeStruct((tiles * per, nch), F32),
-        in_specs=[
-            small,
-            small,
-            rows,
-            rows,
-            pl.BlockSpec((1, nch), lambda k: (0, 0)),
-        ],
-        out_specs=pl.BlockSpec((chunk * tiles, nch), lambda k: (k, 0)),
-        compiler_params=pltpu.CompilerParams(vmem_limit_bytes=53 * 2**20),
-        name="unpack",
-    )(order, count, got, obs, prec)
+    slot = lax.broadcasted_iota(jnp.int32, (chunk, LANES), 0) * tiles
+    sent = []
+    for k in range(per // chunk):
+        for p in range(tiles):
+            h = order_ref[p]
+            ks = slice(k * chunk, (k + 1) * chunk)
+            dep = (got_ref[h, ks, :].astype(F32) - obs_ref[h, ks, :]) * prec
+            first = k * chunk * tiles + p
+            out_v[pl.ds(first, chunk, stride=tiles), :] = jnp.where(
+                slot + first < count_ref[0], dep, 0.0
+            )
+        done = slice(k * chunk * tiles, (k + 1) * chunk * tiles)
+        sent.append(fetch(out_v.at[done], out_ref.at[done], sem.at[k]))
+    for copy in sent:
+        copy.wait()
 
 
 def shift_pairs(size, wrap):
@@ -351,6 +340,7 @@
 
 
 BLOCK = 1024
+BATCH = 8
 
 
 def observe_body(
@@ -401,18 +391,25 @@
         top = float(rows // 2)
         one16, zero16 = jnp.ones((LANES, LANES), BF16), jnp.zeros((LANES, LANES), BF16)
 
-        def gather(m, c):
+        def select(m):
             mine = meta[m, 2:3, :] == code
             row = jnp.broadcast_to(jnp.where(mine, meta[m, 0:1, :], float(rows)), (LANES, LANES))
             col = jnp.broadcast_to(meta[m, 1:2, :], (LANES, LANES))
             row_t, col_t = row.T, col.T
             local = jnp.where(row_t < top, row_t, row_t - top)
             value = jnp.where(col_t == lane, local, -1.0).astype(BF16)
-            sel = jnp.concatenate(
-                [jnp.where(value == jnp.asarray(t, BF16), one16, zero16) for t in range(rows // 2)],
-                axis=1,
-            )
-            out = dot(sel, both)
+            picks = [
+                jnp.where(value == jnp.asarray(t, BF16), one16, zero16) for t in range(rows // 2)
+            ]
+            local = jnp.where(row < top, row, row - top)
+            value = jnp.where(col == sub, local, -1.0).astype(BF16)
+            for t in range(rows // 2):
+                hot[t * LANES : (t + 1) * LANES, pl.ds(pl.multiple_of(m * LANES, LANES), LANES)] = (
+                    jnp.where(value == jnp.asarray(t, BF16), one16, zero16)
+                )
+            return row_t, jnp.concatenate(picks, axis=1)
+
+        def deposit(m, row_t, out):
             upper = row_t >= top
             pred = jnp.where(upper, out[:, nch:], out[:, :nch])
             pred = jnp.where(row_t < float(rows), pred, 0.0)
@@ -423,18 +420,17 @@
             weights[at, nch:] = jnp.where(upper, w, 0.0).astype(BF16)
             pred = pred.reshape(group, per, nch)
             where = pl.ds(m * group, group)
-
             before = jnp.where(cls > 0, pred_ref[where].astype(F32), 0.0)
             pred_ref[where] = (before + pred).astype(BF16)
-            local = jnp.where(row < top, row, row - top)
-            value = jnp.where(col == sub, local, -1.0).astype(BF16)
-            for t in range(rows // 2):
-                hot[t * LANES : (t + 1) * LANES, pl.ds(pl.multiple_of(m * LANES, LANES), LANES)] = (
-                    jnp.where(value == jnp.asarray(t, BF16), one16, zero16)
-                )
+
+        def gather(b, c):
+            found = [select(b * BATCH + i) for i in range(BATCH)]
+            out = dot(jnp.concatenate([picks for _, picks in found], axis=0), both)
+            for i, (row_t, _) in enumerate(found):
+                deposit(b * BATCH + i, row_t, out[i * LANES : (i + 1) * LANES])
             return c
 
-        lax.fori_loop(0, obs_n // LANES, gather, 0, unroll=4)
+        lax.fori_loop(0, obs_n // LANES // BATCH, gather, 0)
 
         def scatter(k, c):
             at = pl.ds(k * BLOCK, BLOCK)
@@ -617,7 +613,11 @@
         lat_id, top, bottom, right, left, adj, slope0, slope1, rot, w_fwd, encoder_weight,
         analysis_vector, prior_estimate, prior_precision[None, :],
     )
-    departures = unpack(order, obs_count, back, kept, obs_precision[None, :])
+    (departures,) = call(
+        unpack_body, [((obs_n, nch), F32)], 5,
+        [VMEM((obs_n, nch), F32), pltpu.SemaphoreType.DMA((per // min(per, CHUNK),))],
+        (0, 1), moved=obs_n * nch * 10, limit=UNPACK, far_out=(0,),
+    )(order, obs_count, back, kept, obs_precision[None, :])
     return departures, derivative
 
 

time: 110 us -> 109 us (level)
  Pallas kernels: 53 us -> 51.9 us
where the time goes in v6:
time: 109 us; the launch traced here: 108 us
  Pallas kernels  51.9 us (48%)
  starting transfers between devices  29.8 us (27%)
  waiting for transfers between devices  20.6 us (19%)
  local copies, waits for them, and re-layouts  3.13 us (3%)
  between operations  1.74 us (2%)
    pallas_call x1, Pallas kernels, on_device(): call(observe_body, [((rows, cols, LANES), F32)] + [(strip, BF16)] * 2 + [...  15.6 us
    pallas_call x1, Pallas kernels, on_device(): call(functools.partial(forward_body, n_lat), [((rows, cols, LANES), BF16)...  14.9 us
    pallas_call x1, Pallas kernels, on_device(): call(functools.partial(adjoint_body, n_lat), [((v, rows, cols), F32)], 14...  14.6 us
    ppermute x2, starting transfers between devices, halo_rows(): top = lax.ppermute(tail, 'lat', up)  8.54 us
    ppermute x2, waiting for transfers between devices, halo_columns(): right = lax.ppermute(near, 'lon', down)  8.23 us
    ppermute x2, waiting for transfers between devices, halo_columns(): left = lax.ppermute(far, 'lon', up)  6.93 us
    all_to_all x1, starting transfers between devices, on_device(): lax.all_to_all(send, ('lat', 'lon'), split_axis=0, concat_axis=0, tiled=T...  6.67 us
    ppermute x2, starting transfers between devices, halo_columns(): right = lax.ppermute(near, 'lon', down)  6.55 us
  transfers between devices with their start and end apart: 10, of which 7 were waited for; matrix products, arithmetic and copies ran while one was open for 3% of the time, Pallas kernels for 30%

profile of v6, /device:TPU:0, one launch (start us, length us, event | category | flops | bytes accessed | tf_op | source)
XLA Modules:
  0.0 108.4 jit_solution(1659922996040242222)
XLA Ops:
  0.6 0.0 copy-start.1
  0.6 1.0 copy-done.1
  1.7 1.4 %shard_map.140 = (f32[16,128,128]{2,1,0:T(8,128)}, bf16[16,8,128]{2,1,0:T(8,128)(2,1)S(1)}, bf16[16,8,128]{2,1,0:T(8,128)(2,1)S(1)}, bf16[4,128,128]{2,1,0:T(8,128)(2,1)S(1)}, bf16[4,128,128]{2,1,0:T(8,128)(2,1)S(1)}) custom-call(f32[69,16,128]{2,1,0:T(8,128)S(1)} %copy-done.1), custom_call_target="tpu_custom_call" | custom-call | bytes 1130496 | tf_op jit(solution)/shard_map/pallas_call | solution.py:506
  3.1 4.9 %collective-permute-start = (bf16[4,128,128]{2,1,0:T(8,128)(2,1)S(1)}, bf16[4,128,128]{2,1,0:T(8,128)(2,1)S(1)}, u32[]{:S(2)}, u32[]{:S(2)}) collective-permute-start(bf16[4,128,128]{2,1,0:T(8,128)(2,1)S(1)} %get-tuple-element.36), channel_id=1, source_target_pairs={{0,8},{8,16},{16,24},{1,9},{9,17},{17,25},{2,10},{10,18},{18,26},{... | collective-permute-start | bytes 393224 | tf_op jit(solution)/shard_map/ppermute | solution.py:138
  7.9 1.3 %collective-permute-start.1 = (bf16[4,128,128]{2,1,0:T(8,128)(2,1)S(1)}, bf16[4,128,128]{2,1,0:T(8,128)(2,1)S(1)}, u32[]{:S(2)}, u32[]{:S(2)}) collective-permute-start(bf16[4,128,128]{2,1,0:T(8,128)(2,1)S(1)} %get-tuple-element.37), channel_id=1, source_target_pairs={{8,0},{16,8},{24,16},{9,1},{17,9},{25,17},{10,2},{18,10},{26,18},{... | collective-permute-start | bytes 393224 | tf_op jit(solution)/shard_map/ppermute | solution.py:139
  9.9 0.1 broadcast_in_dim.46
  10.0 0.1 broadcast_in_dim.47
  10.1 0.9 fusion.18
  11.0 0.1 reduce_min.23
  11.0 0.1 reduce_min.25
  11.1 0.1 multiply_reduce_fusion
  11.2 0.0 copy-start.9
  11.3 0.1 stack.8
  11.3 0.1 copy.23
  11.4 0.1 copy.17
  11.5 0.1 copy.20
  11.6 0.1 convolution_convert_fusion
  11.8 0.1 broadcast_in_dim.50
  11.9 3.1 %shard_map.141 = (bf16[32,72,128]{2,1,0:T(8,128)(2,1)}, f32[32,64,128]{2,1,0:T(8,128)}) custom-call(s32[32]{0:T(128)S(1)} %fusion.16.order_ref, f32[2048,128]{1,0:T(8,128)} %obs_ref, bf16[32,8,128]{2,1,0:T(8,128)(2,1)S(1)} %pad.8.meta_ref), custom_call_target="tpu_custom_call" | custom-call | bytes 1572864 | tf_op jit(solution)/shard_map/pallas_call | solution.py:530
  15.1 0.0 collective-permute-done.top_ref
  15.1 0.3 collective-permute-done.1.bottom_ref
  15.4 6.7 %all-to-all-start = ((bf16[32,72,128]{2,1,0:T(8,128)(2,1)}), bf16[32,72,128]{2,1,0:T(8,128)(2,1)S(1)}, u32[]{:S(2)}, u32[]{:S(2)}) async-start(bf16[32,72,128]{2,1,0:T(8,128)(2,1)} %get-tuple-element.48), calls=%async_computation | async-start | bytes 1179648 | tf_op jit(solution)/shard_map/all_to_all | solution.py:535
  22.1 0.0 copy-start.5
  22.1 0.0 copy-start.6
  22.1 3.4 %collective-permute-start.2 = (bf16[24,8,128]{2,1,0:T(8,128)(2,1)S(1)}, bf16[24,8,128]{2,1,0:T(8,128)(2,1)S(1)}, u32[]{:S(2)}, u32[]{:S(2)}) collective-permute-start(bf16[24,8,128]{2,1,0:T(8,128)(2,1)S(1)} %get-tuple-element.44), channel_id=1, source_target_pairs={{1,0},{2,1},{3,2},{4,3},{5,4},{6,5},{7,6},{0,7},{9,8},{10,9},{11,1... | collective-permute-start | bytes 147464 | tf_op jit(solution)/shard_map/ppermute | solution.py:150
  25.5 0.0 collective-permute-start.3
  25.5 0.0 copy-done.9
  25.5 0.2 copy.26
  25.7 1.1 %pad.9.clone = bf16[4,128,1024]{2,1,0:T(8,128)(2,1)} pad(bf16[4,69,1024]{2,1,0:T(8,128)(2,1)S(1)} %copy.26, bf16[]{:T(256)} %constant.122.clone.1), padding=0_0x0_59x0_0 | pad | bytes 1613826 | tf_op jit(solution)/shard_map/jit(_pad)/pad | solution.py:538
  26.8 6.6 %collective-permute-done.2.right_ref = bf16[24,8,128]{2,1,0:T(8,128)(2,1)S(1)} collective-permute-done((bf16[24,8,128]{2,1,0:T(8,128)(2,1)S(1)}, bf16[24,8,128]{2,1,0:T(8,128)(2,1)S(1)}, u32[]{:S(2)}, u32[]{:S(2)}) %collective-permute-start.2) | collective-permute-done | bytes 49184 | tf_op jit(solution)/shard_map/ppermute | solution.py:150
  33.4 3.4 %collective-permute-done.3.left_ref = bf16[24,8,128]{2,1,0:T(8,128)(2,1)S(1)} collective-permute-done((bf16[24,8,128]{2,1,0:T(8,128)(2,1)S(1)}, bf16[24,8,128]{2,1,0:T(8,128)(2,1)S(1)}, u32[]{:S(2)}, u32[]{:S(2)}) %collective-permute-start.3) | collective-permute-done | bytes 49184 | tf_op jit(solution)/shard_map/ppermute | solution.py:149
  36.8 0.0 copy-done.5
  36.8 0.0 copy-done.6
  36.8 0.0 copy-start.3
  36.8 0.0 copy-start.4
  36.8 0.0 copy-start.8
  36.8 14.9 %shard_map.143 = (bf16[16,128,128]{2,1,0:T(8,128)(2,1)S(1)}, bf16[22,144,256]{2,1,0:T(8,128)(2,1)}, bf16[20,144,256]{2,1,0:T(8,128)(2,1)}) custom-call(s32[1]{0:T(128)} %bitcast.2.lat_ref, bf16[4,128,128]{2,1,0:T(8,128)(2,1)S(1)} %collective-permute-done.top_ref, bf16[4,128,128]{2,1,0:T(8,128)(2,1)S(1)} %collective-permute-done.1.bottom_ref, ...), custom_call_target="tpu_custom_call" | custom-call | flops 7247757312 | bytes 4194304 | tf_op jit(solution)/shard_map/pallas_call | solution.py:542
  51.7 0.0 all-to-all-done.got_ref
  51.7 0.0 copy-done.3
  51.8 0.0 copy-done.4
  51.8 0.0 copy-done.8
  51.8 0.0 copy-start.2
  51.8 0.0 copy-start.7
  51.8 15.6 %shard_map.144 = (f32[16,128,128]{2,1,0:T(8,128)}, bf16[16,8,128]{2,1,0:T(8,128)(2,1)S(1)}, bf16[16,8,128]{2,1,0:T(8,128)(2,1)S(1)}, bf16[2,128,128]{2,1,0:T(8,1...) custom-call(s32[24,5]{1,0:T(8,128)S(1)} %copy-done.8, ...), custom_call_target="tpu_custom_call" | custom-call | flops 5368709120 | bytes 8388608 | tf_op jit(solution)/shard_map/pallas_call | solution.py:566
  67.4 5.5 %all-to-all-start.1 = ((bf16[32,64,128]{2,1,0:T(8,128)(2,1)}), bf16[32,64,128]{2,1,0:T(8,128)(2,1)S(1)}, u32[]{:S(2)}, u32[]{:S(2)}) async-start(bf16[32,64,128]{2,1,0:T(8,128)(2,1)} %get-tuple-element.49), calls=%async_computation.1 | async-start | bytes 1048576 | tf_op jit(solution)/shard_map/all_to_all | solution.py:585
  72.9 3.7 %collective-permute-start.4 = (bf16[2,128,128]{2,1,0:T(8,128)(2,1)S(1)}, bf16[2,128,128]{2,1,0:T(8,128)(2,1)S(1)}, u32[]{:S(2)}, u32[]{:S(2)}) collective-permute-start(bf16[2,128,128]{2,1,0:T(8,128)(2,1)S(1)} %get-tuple-element.51), channel_id=1, source_target_pairs={{0,8},{8,16},{16,24},{1,9},{9,17},{17,25},{2,10},{10,18},{18,26},{... | collective-permute-start | bytes 196616 | tf_op jit(solution)/shard_map/ppermute | solution.py:138
  76.6 1.3 %collective-permute-start.5 = (bf16[2,128,128]{2,1,0:T(8,128)(2,1)S(1)}, bf16[2,128,128]{2,1,0:T(8,128)(2,1)S(1)}, u32[]{:S(2)}, u32[]{:S(2)}) collective-permute-start(bf16[2,128,128]{2,1,0:T(8,128)(2,1)S(1)} %get-tuple-element.52), channel_id=1, source_target_pairs={{8,0},{16,8},{24,16},{9,1},{17,9},{25,17},{10,2},{18,10},{26,18},{... | collective-permute-start | bytes 196616 | tf_op jit(solution)/shard_map/ppermute | solution.py:139
  77.9 1.3 %collective-permute-done.4.top_ref = bf16[2,128,128]{2,1,0:T(8,128)(2,1)S(1)} collective-permute-done((bf16[2,128,128]{2,1,0:T(8,128)(2,1)S(1)}, bf16[2,128,128]{2,1,0:T(8,128)(2,1)S(1)}, u32[]{:S(2)}, u32[]{:S(2)}) %collective-permute-start.4) | collective-permute-done | bytes 65568 | tf_op jit(solution)/shard_map/ppermute | solution.py:138
  79.2 3.8 %collective-permute-done.5.bottom_ref = bf16[2,128,128]{2,1,0:T(8,128)(2,1)S(1)} collective-permute-done((bf16[2,128,128]{2,1,0:T(8,128)(2,1)S(1)}, bf16[2,128,128]{2,1,0:T(8,128)(2,1)S(1)}, u32[]{:S(2)}, u32[]{:S(2)}) %collective-permute-start.5) | collective-permute-done | bytes 65568 | tf_op jit(solution)/shard_map/ppermute | solution.py:139
  83.0 3.1 %collective-permute-start.6 = (bf16[20,8,128]{2,1,0:T(8,128)(2,1)S(1)}, bf16[20,8,128]{2,1,0:T(8,128)(2,1)S(1)}, u32[]{:S(2)}, u32[]{:S(2)}) collective-permute-start(bf16[20,8,128]{2,1,0:T(8,128)(2,1)S(1)} %get-tuple-element.55), channel_id=1, source_target_pairs={{1,0},{2,1},{3,2},{4,3},{5,4},{6,5},{7,6},{0,7},{9,8},{10,9},{11,1... | collective-permute-start | bytes 122888 | tf_op jit(solution)/shard_map/ppermute | solution.py:150
  86.2 0.0 collective-permute-start.7
  86.2 1.7 %collective-permute-done.6.right_ref = bf16[20,8,128]{2,1,0:T(8,128)(2,1)S(1)} collective-permute-done((bf16[20,8,128]{2,1,0:T(8,128)(2,1)S(1)}, bf16[20,8,128]{2,1,0:T(8,128)(2,1)S(1)}, u32[]{:S(2)}, u32[]{:S(2)}) %collective-permute-start.6) | collective-permute-done | bytes 40992 | tf_op jit(solution)/shard_map/ppermute | solution.py:150
  87.8 3.5 %collective-permute-done.7.left_ref = bf16[20,8,128]{2,1,0:T(8,128)(2,1)S(1)} collective-permute-done((bf16[20,8,128]{2,1,0:T(8,128)(2,1)S(1)}, bf16[20,8,128]{2,1,0:T(8,128)(2,1)S(1)}, u32[]{:S(2)}, u32[]{:S(2)}) %collective-permute-start.7) | collective-permute-done | bytes 40992 | tf_op jit(solution)/shard_map/ppermute | solution.py:149
  91.4 0.0 copy-done.2
  91.4 0.0 copy-done.7
  91.4 0.0 copy-start
  91.4 14.6 %shard_map.147 = f32[69,16,128]{2,1,0:T(8,128)} custom-call(s32[1]{0:T(128)} %bitcast.2.lat_ref, bf16[2,128,128]{2,1,0:T(8,128)(2,1)S(1)} %collective-permute-done.4.top_ref, bf16[2,128,128]{2,1,0:T(8,128)(2,1)S(1)} %collective-permute-done.5.bottom_ref, bf16[20,8,128]{2,1,0:T(8,128)(2,1)S(1)} %collective-permute-done.6.right_ref, ...), custom_call_target="tpu_custom_call" | custom-call | flops 7247757312 | bytes 4194304 | tf_op jit(solution)/shard_map/pallas_call | solution.py:589
  106.0 0.0 all-to-all-done.1.got_ref
  106.0 0.0 copy-done
  106.0 2.2 %shard_map.145 = f32[2048,128]{1,0:T(8,128)} custom-call(s32[32]{0:T(128)S(1)} %fusion.16.order_ref, s32[1]{0:T(128)} %copy.28.count_ref, bf16[32,64,128]{2,1,0:T(8,128)(2,1)S(1)} %all-to-all-done.1.got_ref, f32[32,64,128]{2,1,0:T(8,128)S(1)} %copy-done, f32[1,128]{1,0:T(1,128)S(1)} %bitcast.22), custom_call_target="tpu_custom_call" | custom-call | bytes 2621440 | tf_op jit(solution)/shard_map/pallas_call | solution.py:616
  (10 shorter events, 0.2 us)
Async XLA Ops:
  0.6 1.1 copy-start.1
  3.1 12.0 %collective-permute-start = (bf16[4,128,128]{2,1,0:T(8,128)(2,1)S(1)}, bf16[4,128,128]{2,1,0:T(8,128)(2,1)S(1)}, u32[]{:S(2)}, u32[]{:S(2)}) collective-permute-start(bf16[4,128,128]{2,1,0:T(8,128)(2,1)S(1)} %get-tuple-element.36), channel_id=1, source_target_pairs={{0,8},{8,16},{16,24},{1,9},{9,17},{17,25},{2,10},{10,18},{18,26},{... | collective-permute-start | bytes 393224 | tf_op jit(solution)/shard_map/ppermute | solution.py:138
  7.9 7.5 %collective-permute-start.1 = (bf16[4,128,128]{2,1,0:T(8,128)(2,1)S(1)}, bf16[4,128,128]{2,1,0:T(8,128)(2,1)S(1)}, u32[]{:S(2)}, u32[]{:S(2)}) collective-permute-start(bf16[4,128,128]{2,1,0:T(8,128)(2,1)S(1)} %get-tuple-element.37), channel_id=1, source_target_pairs={{8,0},{16,8},{24,16},{9,1},{17,9},{25,17},{10,2},{18,10},{26,18},{... | collective-permute-start | bytes 393224 | tf_op jit(solution)/shard_map/ppermute | solution.py:139
  11.2 14.3 %copy-start.9 = (bf16[4,69,1024]{2,0,1:T(4,128)(2,1)S(1)}, bf16[4,69,1024]{2,0,1:T(4,128)(2,1)}, u32[]{:S(2)}) copy-start(bf16[4,69,1024]{2,0,1:T(4,128)(2,1)} %param.19) | copy-start | bytes 1695748
  15.4 36.3 %all-to-all-start = ((bf16[32,72,128]{2,1,0:T(8,128)(2,1)}), bf16[32,72,128]{2,1,0:T(8,128)(2,1)S(1)}, u32[]{:S(2)}, u32[]{:S(2)}) async-start(bf16[32,72,128]{2,1,0:T(8,128)(2,1)} %get-tuple-element.48), calls=%async_computation | async-start | bytes 1179648 | tf_op jit(solution)/shard_map/all_to_all | solution.py:535
  22.1 14.7 %copy-start.5 = (bf16[69,256]{1,0:T(8,128)(2,1)S(1)}, bf16[69,256]{1,0:T(8,128)(2,1)}, u32[]{:S(2)}) copy-start(bf16[69,256]{1,0:T(8,128)(2,1)} %enc_in.3) | copy-start | bytes 105988
  22.1 14.6 %copy-start.6 = (bf16[256,69]{0,1:T(8,128)(2,1)S(1)}, bf16[256,69]{0,1:T(8,128)(2,1)}, u32[]{:S(2)}) copy-start(bf16[256,69]{0,1:T(8,128)(2,1)} %param.18) | copy-start | bytes 105988
  22.1 11.2 %collective-permute-start.2 = (bf16[24,8,128]{2,1,0:T(8,128)(2,1)S(1)}, bf16[24,8,128]{2,1,0:T(8,128)(2,1)S(1)}, u32[]{:S(2)}, u32[]{:S(2)}) collective-permute-start(bf16[24,8,128]{2,1,0:T(8,128)(2,1)S(1)} %get-tuple-element.44), channel_id=1, source_target_pairs={{1,0},{2,1},{3,2},{4,3},{5,4},{6,5},{7,6},{0,7},{9,8},{10,9},{11,1... | collective-permute-start | bytes 147464 | tf_op jit(solution)/shard_map/ppermute | solution.py:150
  25.5 11.2 %collective-permute-start.3 = (bf16[24,8,128]{2,1,0:T(8,128)(2,1)S(1)}, bf16[24,8,128]{2,1,0:T(8,128)(2,1)S(1)}, u32[]{:S(2)}, u32[]{:S(2)}) collective-permute-start(bf16[24,8,128]{2,1,0:T(8,128)(2,1)S(1)} %get-tuple-element.45), channel_id=1, source_target_pairs={{0,1},{1,2},{2,3},{3,4},{4,5},{5,6},{6,7},{7,0},{8,9},{9,10},{10,1... | collective-permute-start | bytes 147464 | tf_op jit(solution)/shard_map/ppermute | solution.py:149
  36.8 15.0 %copy-start.3 = (f32[128]{0:T(128)S(1)}, f32[128]{0:T(128)}, u32[]{:S(2)}) copy-start(f32[128]{0:T(128)} %param.22) | copy-start | bytes 1540
  36.8 15.0 %copy-start.4 = (bf16[1024,128]{1,0:T(8,128)(2,1)S(1)}, bf16[1024,128]{1,0:T(8,128)(2,1)}, u32[]{:S(2)}) copy-start(bf16[1024,128]{1,0:T(8,128)(2,1)} %wout_ref.1) | copy-start | bytes 786436
  36.8 15.0 %copy-start.8 = (s32[24,5]{1,0:T(8,128)S(1)}, s32[24,5]{1,0:T(8,128)}, u32[]{:S(2)}) copy-start(s32[24,5]{1,0:T(8,128)} %constant.123.clone.table_ref) | copy-start | bytes 1444
  51.8 39.6 %copy-start.2 = (f32[69,16,128]{2,1,0:T(8,128)S(1)}, f32[69,16,128]{2,1,0:T(8,128)}, u32[]{:S(2)}) copy-start(f32[69,16,128]{2,1,0:T(8,128)} %state_in.1) | copy-start | bytes 1695748
  51.8 39.6 %copy-start.7 = (f32[69]{0:T(128)S(1)}, f32[69]{0:T(128)}, u32[]{:S(2)}) copy-start(f32[69]{0:T(128)} %param.15) | copy-start | bytes 832
  67.4 38.5 %all-to-all-start.1 = ((bf16[32,64,128]{2,1,0:T(8,128)(2,1)}), bf16[32,64,128]{2,1,0:T(8,128)(2,1)S(1)}, u32[]{:S(2)}, u32[]{:S(2)}) async-start(bf16[32,64,128]{2,1,0:T(8,128)(2,1)} %get-tuple-element.49), calls=%async_computation.1 | async-start | bytes 1048576 | tf_op jit(solution)/shard_map/all_to_all | solution.py:585
  72.9 6.2 %collective-permute-start.4 = (bf16[2,128,128]{2,1,0:T(8,128)(2,1)S(1)}, bf16[2,128,128]{2,1,0:T(8,128)(2,1)S(1)}, u32[]{:S(2)}, u32[]{:S(2)}) collective-permute-start(bf16[2,128,128]{2,1,0:T(8,128)(2,1)S(1)} %get-tuple-element.51), channel_id=1, source_target_pairs={{0,8},{8,16},{16,24},{1,9},{9,17},{17,25},{2,10},{10,18},{18,26},{... | collective-permute-start | bytes 196616 | tf_op jit(solution)/shard_map/ppermute | solution.py:138
  76.6 6.4 %collective-permute-start.5 = (bf16[2,128,128]{2,1,0:T(8,128)(2,1)S(1)}, bf16[2,128,128]{2,1,0:T(8,128)(2,1)S(1)}, u32[]{:S(2)}, u32[]{:S(2)}) collective-permute-start(bf16[2,128,128]{2,1,0:T(8,128)(2,1)S(1)} %get-tuple-element.52), channel_id=1, source_target_pairs={{8,0},{16,8},{24,16},{9,1},{17,9},{25,17},{10,2},{18,10},{26,18},{... | collective-permute-start | bytes 196616 | tf_op jit(solution)/shard_map/ppermute | solution.py:139
  83.0 4.8 %collective-permute-start.6 = (bf16[20,8,128]{2,1,0:T(8,128)(2,1)S(1)}, bf16[20,8,128]{2,1,0:T(8,128)(2,1)S(1)}, u32[]{:S(2)}, u32[]{:S(2)}) collective-permute-start(bf16[20,8,128]{2,1,0:T(8,128)(2,1)S(1)} %get-tuple-element.55), channel_id=1, source_target_pairs={{1,0},{2,1},{3,2},{4,3},{5,4},{6,5},{7,6},{0,7},{9,8},{10,9},{11,1... | collective-permute-start | bytes 122888 | tf_op jit(solution)/shard_map/ppermute | solution.py:150
  86.2 5.2 %collective-permute-start.7 = (bf16[20,8,128]{2,1,0:T(8,128)(2,1)S(1)}, bf16[20,8,128]{2,1,0:T(8,128)(2,1)S(1)}, u32[]{:S(2)}, u32[]{:S(2)}) collective-permute-start(bf16[20,8,128]{2,1,0:T(8,128)(2,1)S(1)} %get-tuple-element.56), channel_id=1, source_target_pairs={{0,1},{1,2},{2,3},{3,4},{4,5},{5,6},{6,7},{7,0},{8,9},{9,10},{10,1... | collective-permute-start | bytes 122888 | tf_op jit(solution)/shard_map/ppermute | solution.py:149
  91.4 14.6 %copy-start = (f32[32,64,128]{2,1,0:T(8,128)S(1)}, f32[32,64,128]{2,1,0:T(8,128)}, u32[]{:S(2)}) copy-start(f32[32,64,128]{2,1,0:T(8,128)} %get-tuple-element.50.obs_ref) | copy-start | bytes 3145732
